TPU v7x, 512 devices: a whole 4x4x16 slice. The times are simulated.
512 devices in a mesh: user: 32 (over x, y, core), item: 16 (over z).
Axes of the slice: x: 4, y: 4, z: 16, core: 2. Of those that a mesh axis runs over, the one named last changes fastest.
Arguments:
- tokens: bfloat16 [262144, 1024], P(('user', 'item')), may hold values from -6 to 6
- lengths: int32 [512, 32], P(('user', 'item')), may hold values from 1 to 16, as said below
- destination: int32 [512, 32], P(('user', 'item')), may hold values from 0 to 31, as said below
- worker_offset: int32 [512, 32], P(('user', 'item')), may hold values from 0 to 255
- positives: int32 [262144], P(('user', 'item')), may hold values from 0 to 4095, as said below
- negatives: int32 [16, 256], replicated, may hold values from 0 to 4095, as said below
- table: bfloat16 [4096, 1024], P('item'), may hold values from -6 to 6
- in_gain: float32 [1024], replicated, may hold values from 0.1 to 1.9
- w_uvqk: bfloat16 [1024, 2048], P('item'), may hold values from -0.1875 to 0.1875
- out_gain: float32 [512], replicated, may hold values from 0.1 to 1.9
- w_out: bfloat16 [512, 1024], P(None, 'item'), may hold values from -0.25 to 0.25
Outputs:
- layer_out: bfloat16 [131072, 1024], P(('user', 'item'))
- token_grad: bfloat16 [262144, 1024], P(('user', 'item'))
- item_grad: float32 [4096, 1024], P('item', 'user')
Inputs may be any that keep to these rules, and one draw needn't show every extreme that they name: `lengths`: A device's histories lie in its rows in order from row 0 and fill at most 512 rows; every destination receives a history of exactly 16 tokens. `destination`: A device sends its 32 histories to 32 different destinations along user; the histories sent to one device by the devices of its item index, placed at their worker_offset, cover its 256 rows exactly once. `positives`: the target ids of a device lie among the 256 table rows of its item index. `negatives`: columns k * 16 to k * 16 + 15 of each group name rows held by item index k.
All inputs are finite; a program needn't handle non-finite values.
Results may differ from a plain program's by a relative error of at most 0.017.
Values may be sent and summed in bfloat16 or wider, within the bound.
No kernel may reach another device: no remote copies, remote signals or barrier semaphores. Data moves between devices by JAX's collectives and lax.ppermute only.
A program may use at most 64 MiB of HBM per device.

v0:
```python
import jax
import jax.numpy as jnp
from jax import lax
from jax.sharding import PartitionSpec as P

HEAD = 128
TOK_DEV = 256


norm_epsilon = 1e-05
scale_epsilon = 1e-06
inverse_temp = 20.0
loss_scale = 32.0


def joined_along(blocks, dim):
    blocks = jnp.moveaxis(blocks, 0, dim)
    shape = blocks.shape
    return blocks.reshape(*shape[:dim], shape[dim] * shape[dim + 1], *shape[dim + 2 :])


def from_everyone(shard, axis):
    count = lax.axis_size(axis)
    return lax.all_to_all(
        jnp.broadcast_to(shard[None], (count, *shard.shape)), axis, 0, 0, tiled=True
    )


def gather_directly(shard, axis, dim):
    return joined_along(from_everyone(shard, axis), dim)


def in_blocks(shard, dim, count):
    shape = shard.shape
    blocks = shard.reshape(*shape[:dim], count, shape[dim] // count, *shape[dim + 1 :])
    return jnp.moveaxis(blocks, dim, 0)


def sent_and_summed(shard, axis, dim):
    count = lax.axis_size(axis)
    blocks = lax.all_to_all(in_blocks(shard, dim, count), axis, 0, 0, tiled=True)
    return jnp.sum(blocks.astype(jnp.float32), axis=0)


def over_copies(shard, axis):
    everything = from_everyone(shard, axis)
    return jnp.sum(everything, axis=0)


def layer_norm(values, gain):
    center = jnp.mean(values, axis=-1, keepdims=True)
    shifted = values - center
    spread = jnp.mean(shifted * shifted, axis=-1, keepdims=True)
    return shifted * lax.rsqrt(spread + norm_epsilon) * gain


def hstu_block(rows, segment, in_gain, w_uvqk, out_gain, w_out):
    count = rows.shape[0]
    rows_f = rows.astype(jnp.float32)
    normed = layer_norm(rows_f, in_gain).astype(jnp.bfloat16)
    projected = jnp.dot(
        normed,
        lax.all_gather(w_uvqk, "item", axis=0, tiled=True),
        preferred_element_type=jnp.float32,
    )
    active = jax.nn.silu(projected).astype(jnp.bfloat16)
    width = active.shape[1] // 4
    heads = width // HEAD
    gate_u = active[:, :width]
    values_v = active[:, width : 2 * width].reshape(count, heads, HEAD)
    queries = active[:, 2 * width : 3 * width].reshape(count, heads, HEAD)
    key_rows = active[:, 3 * width :].reshape(count, heads, HEAD)
    scores = jnp.einsum(
        "qhd,khd->hqk", queries, key_rows, preferred_element_type=jnp.float32
    ) * HEAD ** (-0.5)
    order = jnp.arange(count, dtype=jnp.int32)
    allowed = (segment[:, None] == segment[None, :]) & (order[None, :] <= order[:, None])
    weights = jnp.where(allowed[None], jax.nn.silu(scores), 0.0).astype(jnp.bfloat16)
    mixed = jnp.einsum(
        "hqk,khd->qhd", weights, values_v, preferred_element_type=jnp.float32
    ).reshape(count, width)
    gated = (layer_norm(mixed, out_gain) * gate_u.astype(jnp.float32)).astype(jnp.bfloat16)
    delta = jnp.dot(gated, gather_directly(w_out, "item", 1), preferred_element_type=jnp.float32)
    return (rows_f + delta).astype(jnp.bfloat16)


def dispatch(rows, home_start, history_len, targets, offsets, slot_rows, user_count):
    peers = jnp.arange(user_count, dtype=jnp.int32)
    chosen = (targets[None, :] == peers[:, None]).astype(jnp.int32)
    first_row = jnp.sum(chosen * home_start[None, :], axis=1)
    sent_count = jnp.sum(chosen * history_len[None, :], axis=1)
    landing = jnp.sum(chosen * offsets[None, :], axis=1)
    within = jnp.arange(slot_rows, dtype=jnp.int32)
    picked = jnp.minimum(first_row[:, None] + within[None, :], rows.shape[0] - 1)
    filled = within[None, :] < sent_count[:, None]
    parcels = jnp.where(filled[:, :, None], rows[picked], jnp.zeros((), rows.dtype))
    labels = jnp.stack([landing, sent_count], axis=1)
    arrived, arrived_labels = (
        lax.all_to_all(parcels, "user", split_axis=0, concat_axis=0, tiled=True),
        lax.all_to_all(labels, "user", split_axis=0, concat_axis=0, tiled=True),
    )
    worker_rows = jnp.arange(TOK_DEV, dtype=jnp.int32)
    lower = arrived_labels[:, 0]
    upper = lower + arrived_labels[:, 1]
    inside = (
        (worker_rows[:, None] >= lower[None, :]) & (worker_rows[:, None] < upper[None, :])
    ).astype(jnp.int32)
    source = jnp.sum(inside * peers[None, :], axis=1)
    begin = jnp.sum(inside * lower[None, :], axis=1)
    flattened = arrived.reshape(-1, arrived.shape[-1])
    gathered = flattened[source * slot_rows + worker_rows - begin]
    return (gathered, source, arrived_labels)


def per_device(
    tokens,
    lengths,
    destination,
    worker_offset,
    positives,
    negatives,
    table,
    in_gain,
    w_uvqk,
    out_gain,
    w_out,
):
    user_count = lax.axis_size("user")
    item_count = lax.axis_size("item")
    item_here = lax.axis_index("item")
    user_here = lax.axis_index("user")
    home_rows = tokens.shape[0]
    model_width = tokens.shape[1]
    hist_count = lengths.shape[1]
    slot_rows = home_rows // hist_count
    history_len = lengths[0]
    targets = destination[0]
    offsets = worker_offset[0]
    home_start = jnp.cumsum(history_len) - history_len
    row_ids = jnp.arange(home_rows, dtype=jnp.int32)
    finished = (row_ids[:, None] >= (home_start + history_len)[None, :]).astype(jnp.int32)
    home_segment = jnp.sum(finished, axis=1)
    valid = row_ids < jnp.sum(history_len)
    home_out = hstu_block(tokens, home_segment, in_gain, w_uvqk, out_gain, w_out)
    layer_out = dispatch(
        home_out, home_start, history_len, targets, offsets, slot_rows, user_count
    )[0]
    item_rows = table.shape[0]
    table_f = table.astype(jnp.float32)
    table_scale = lax.rsqrt(jnp.mean(table_f * table_f, axis=1) + scale_epsilon)
    table_hat = table_f * table_scale[:, None]
    table_low = table_hat.astype(jnp.bfloat16)
    share = negatives.shape[1] // item_count
    owned_ids = (
        lax.dynamic_slice_in_dim(negatives, item_here * share, share, 1) - item_here * item_rows
    )
    group_rows = lax.all_to_all(
        table_low[owned_ids], "item", split_axis=0, concat_axis=0, tiled=True
    ).reshape(-1, model_width)
    positive_local = positives - item_here * item_rows
    positive_rows = table_low[positive_local]
    out_f = home_out.astype(jnp.float32)
    out_scale = lax.rsqrt(jnp.mean(out_f * out_f, axis=1) + scale_epsilon)
    out_hat = out_f * out_scale[:, None]
    out_low = out_hat.astype(jnp.bfloat16)
    factor = inverse_temp / model_width
    positive_logit = (
        jnp.einsum("rd,rd->r", out_low, positive_rows, preferred_element_type=jnp.float32) * factor
    )
    negative_logit = (
        jnp.einsum("rd,nd->rn", out_low, group_rows, preferred_element_type=jnp.float32) * factor
    )
    positive_exp = jnp.exp(positive_logit)
    negative_exp = jnp.exp(negative_logit)
    partition = positive_exp + jnp.sum(negative_exp, axis=1)
    weight = jnp.where(valid, loss_scale, 0.0)
    positive_grad = weight * (positive_exp / partition - 1.0)
    negative_grad = (weight[:, None] * negative_exp / partition[:, None]).astype(jnp.bfloat16)
    grad_hat = (
        positive_grad[:, None] * positive_rows.astype(jnp.float32)
        + jnp.dot(negative_grad, group_rows, preferred_element_type=jnp.float32)
    ) * factor
    token_grad = (
        (grad_hat - out_hat * jnp.mean(grad_hat * out_hat, axis=1, keepdims=True))
        * out_scale[:, None]
    ).astype(jnp.bfloat16)
    negative_terms = (
        jnp.einsum("rn,rd->nd", negative_grad, out_low, preferred_element_type=jnp.float32) * factor
    )
    owned_terms = lax.all_to_all(
        negative_terms.reshape(item_count, share, model_width).astype(jnp.bfloat16),
        "item",
        split_axis=0,
        concat_axis=0,
        tiled=True,
    ).astype(jnp.float32)
    positive_terms = (positive_grad * factor)[:, None] * out_low.astype(jnp.float32)
    catalog = jnp.arange(item_rows, dtype=jnp.int32)
    positive_hits = (positive_local[None, :] == catalog[:, None]).astype(jnp.float32)
    negative_hits = (owned_ids.reshape(-1)[None, :] == catalog[:, None]).astype(jnp.float32)
    row_sums = jnp.dot(positive_hits, positive_terms)
    row_sums = row_sums + jnp.dot(negative_hits, owned_terms.reshape(-1, model_width))
    column_width = model_width // user_count
    part = sent_and_summed(row_sums.astype(jnp.bfloat16), "user", 1)
    hat_part = lax.dynamic_slice_in_dim(table_hat, user_here * column_width, column_width, 1)
    inner = over_copies(jnp.sum(part * hat_part, axis=1), "user") / model_width
    item_grad = (part - hat_part * inner[:, None]) * table_scale[:, None]
    return (layer_out, token_grad, item_grad)


def solution(mesh):
    return jax.shard_map(
        per_device,
        mesh=mesh,
        in_specs=(
            P(("user", "item"), None),
            P(("user", "item"), None),
            P(("user", "item"), None),
            P(("user", "item"), None),
            P(("user", "item")),
            P(),
            P("item", None),
            P(),
            P("item", None),
            P(),
            P(None, "item"),
        ),
        out_specs=(P(("user", "item"), None), P(("user", "item"), None), P("item", "user")),
        check_vma=False,
    )
```

profile of v0, /device:TPU:1, one launch (start us, length us, event | category | flops | bytes accessed | tf_op | source)
XLA Modules:
  0.0 277.3 jit_solution(9776412261107728501)
XLA Ops:
  7.3 0.7 all-gather.2.cloned.1.call-update
  7.9 1.9 broadcast_in_dim.43
  9.9 15.8 %all-to-all-start = ((bf16[16,512,64]{1,2,0:T(8,128)(2,1)}), bf16[16,512,64]{1,2,0:T(8,128)(2,1)}, u32[]{:S(2)}, u32[]{:S(2)}) async-start(bf16[16,512,64]{1,2,0:T(8,128)(2,1)} %broadcast_in_dim.43), calls=%async_computation | async-start | bytes 2097152 | tf_op jit(solution)/shard_map/all_to_all | solution.py:24
  26.3 1.2 convert_multiply_fusion.8
  27.5 2.0 gather_fusion.2
  29.6 2.0 gather_fusion.3
  31.6 0.7 fusion.61
  32.4 0.7 copy.55
  33.1 0.7 fusion.51
  33.9 0.2 convert_reduce_fusion
  34.1 0.4 fusion.5
  34.8 87.9 %all-gather.2.cloned.1.call-done = bf16[1024,2048]{1,0:T(8,128)(2,1)} async-done(((bf16[64,2048]{1,0:T(8,128)(2,1)}), bf16[1024,2048]{1,0:T(8,128)(2,1)}) %all-gather.2.cloned.1.call-update) | async-done | bytes 4194320 | tf_op jit(solution)/shard_map/all_gather | solution.py:63
  122.7 5.1 %multiply_convert_fusion = bf16[512,2048]{1,0:T(8,128)(2,1)S(1)} fusion(bf16[1024,2048]{1,0:T(8,128)(2,1)} %all-gather.2.cloned.1.call-done, bf16[512,1024]{1,0:T(8,128)(2,1)S(1)} %copy-done, f32[1024]{0:T(1024)S(1)} %copy-done.8, f32[512]{0:T(512)S(1)} %add_rsqrt_fusion.2, f32[512]{0:T(512)S(1)} %broadcast_multiply_fusion.3), kind=kOutput, calls=%fused_computation.5 | convolution fusion | flops 2155347968 | bytes 7348224 | tf_op jit(solution)/shard_map/dot_general | solution.py:61
  127.7 1.3 copy-done.2
  129.1 1.2 slice_bitcast_fusion.1
  130.3 1.0 copy.66
  131.3 7.0 %all-to-all-start.3 = ((bf16[16,16,1024]{2,1,0:T(8,128)(2,1)}), bf16[16,16,1024]{2,1,0:T(8,128)(2,1)}, u32[]{:S(2)}, u32[]{:S(2)}) async-start(bf16[16,16,1024]{2,1,0:T(8,128)(2,1)} %bitcast.21), calls=%async_computation.3 | async-start | bytes 1048576 | tf_op jit(solution)/shard_map/all_to_all | solution.py:157
  138.3 3.4 %fusion.62 = (f32[512]{0:T(512)S(1)}, f32[4,128,512]{2,1,0:T(8,128)S(1)}) fusion(bf16[512,4,128]{0,2,1:T(8,128)(2,1)} %bitcast.73, pred[512,512]{1,0:T(8,128)(4,1)S(1)} %fusion.34, bf16[64,4,8,128]{3,2,1,0:T(8,128)(2,1)} %get-tuple-element.30, bf16[64,4,8,128]{3,2,1,0:T(8,128)(2,1)} %get-tuple-element.29), kind=kOutput, calls=%fused_computation.120 | convolution fusion | flops 544472576 | bytes 2885632 | tf_op jit(solution)/shard_map/hqk,khd->qhd/dot_general | solution.py:79
  141.7 1.3 copy.67
  143.2 2.6 fusion.12
  145.8 0.5 fusion.15
  146.3 10.5 %all-to-all-done.3 = bf16[16,16,1024]{2,1,0:T(8,128)(2,1)} async-done(((bf16[16,16,1024]{2,1,0:T(8,128)(2,1)}), bf16[16,16,1024]{2,1,0:T(8,128)(2,1)}, u32[]{:S(2)}, u32[]{:S(2)}) %all-to-all-start.3) | async-done | bytes 524320 | tf_op jit(solution)/shard_map/all_to_all | solution.py:157
  156.8 17.8 %all-to-all-start.2 = ((s32[32,1,2]{2,1,0:T(1,128)}), s32[32,1,2]{2,1,0:T(1,128)S(1)}, u32[]{:S(2)}, u32[]{:S(2)}) async-start(s32[32,1,2]{2,1,0:T(1,128)} %copy.55), calls=%async_computation.2 | async-start | bytes 32768 | tf_op jit(solution)/shard_map/all_to_all | solution.py:100
  174.7 1.6 fusion.67
  176.3 0.7 broadcast_multiply_fusion
  177.0 1.4 fusion.20
  178.4 3.2 %all-to-all-done.2 = s32[32,1,2]{2,1,0:T(1,128)S(1)} async-done(((s32[32,1,2]{2,1,0:T(1,128)}), s32[32,1,2]{2,1,0:T(1,128)S(1)}, u32[]{:S(2)}, u32[]{:S(2)}) %all-to-all-start.2) | async-done | bytes 288 | tf_op jit(solution)/shard_map/all_to_all | solution.py:100
  181.6 6.8 %all-to-all-start.4 = ((bf16[16,16,1024]{2,1,0:T(8,128)(2,1)}), bf16[16,16,1024]{2,1,0:T(8,128)(2,1)S(1)}, u32[]{:S(2)}, u32[]{:S(2)}) async-start(bf16[16,16,1024]{2,1,0:T(8,128)(2,1)} %bitcast.23), calls=%async_computation.4 | async-start | bytes 1048576 | tf_op jit(solution)/shard_map/all_to_all | solution.py:190
  188.8 22.6 %all-to-all-done.4 = bf16[16,16,1024]{2,1,0:T(8,128)(2,1)S(1)} async-done(((bf16[16,16,1024]{2,1,0:T(8,128)(2,1)}), bf16[16,16,1024]{2,1,0:T(8,128)(2,1)S(1)}, u32[]{:S(2)}, u32[]{:S(2)}) %all-to-all-start.4) | async-done | bytes 524320 | tf_op jit(solution)/shard_map/all_to_all | solution.py:190
  211.4 0.3 fusion.48
  211.7 0.6 fusion.21
  212.3 1.0 copy.57
  213.3 11.2 %all-to-all-start.5 = ((bf16[32,256,32]{1,2,0:T(8,128)(2,1)}), bf16[32,256,32]{1,2,0:T(8,128)(2,1)}, u32[]{:S(2)}, u32[]{:S(2)}) async-start(bf16[32,256,32]{1,2,0:T(8,128)(2,1)} %bitcast.26), calls=%async_computation.5 | async-start | bytes 1048576 | tf_op jit(solution)/shard_map/all_to_all | solution.py:41
  224.7 2.1 gather_fusion
  226.7 1.1 broadcast_select_fusion
  227.8 8.5 %all-to-all-done.5 = bf16[32,256,32]{1,2,0:T(8,128)(2,1)} async-done(((bf16[32,256,32]{1,2,0:T(8,128)(2,1)}), bf16[32,256,32]{1,2,0:T(8,128)(2,1)}, u32[]{:S(2)}, u32[]{:S(2)}) %all-to-all-start.5) | async-done | bytes 524320 | tf_op jit(solution)/shard_map/all_to_all | solution.py:41
  236.3 3.7 %all-to-all-start.1 = ((bf16[32,16,1024]{2,1,0:T(8,128)(2,1)}), bf16[32,16,1024]{2,1,0:T(8,128)(2,1)S(1)}, u32[]{:S(2)}, u32[]{:S(2)}) async-start(bf16[32,16,1024]{2,1,0:T(8,128)(2,1)} %broadcast_select_fusion), calls=%async_computation.1 | async-start | bytes 2097152 | tf_op jit(solution)/shard_map/all_to_all | solution.py:99
  240.1 3.3 %fusion.8 = (f32[512]{0:T(512)S(1)}, f32[512,1024]{1,0:T(8,128)}) fusion(bf16[512,1024]{1,0:T(8,128)(2,1)S(1)} %get-tuple-element.40, f32[512]{0:T(512)S(1)} %add_rsqrt_fusion, bf16[256,1024]{1,0:T(8,128)(2,1)} %bitcast.22, f32[512,256]{0,1:T(8,128)} %copy-done.10, f32[512]{0:T(512)S(1)} %get-tuple-element.34, f32[512]{0:T(512)S(1)} %fusion.51, ...), kind=kOutput, calls=%fused_computation.22 | convolution fusion | flops 273022464 | bytes 5253120 | tf_op jit(solution)/shard_map/dot_general | solution.py:181
  243.4 1.1 convert_reduce_fusion.1
  244.6 1.1 multiply_reduce_fusion
  245.7 11.1 %all-to-all-done.1 = bf16[32,16,1024]{2,1,0:T(8,128)(2,1)S(1)} async-done(((bf16[32,16,1024]{2,1,0:T(8,128)(2,1)}), bf16[32,16,1024]{2,1,0:T(8,128)(2,1)S(1)}, u32[]{:S(2)}, u32[]{:S(2)}) %all-to-all-start.1) | async-done | bytes 1048608 | tf_op jit(solution)/shard_map/all_to_all | solution.py:99
  256.8 0.6 broadcast_in_dim.50
  257.4 3.9 %all-to-all-start.6 = ((f32[32,1,256]{2,1,0:T(1,128)}), f32[32,1,256]{2,1,0:T(1,128)S(1)}, u32[]{:S(2)}, u32[]{:S(2)}) async-start(f32[32,1,256]{2,1,0:T(1,128)} %broadcast_in_dim.50), calls=%async_computation.6 | async-start | bytes 65536 | tf_op jit(solution)/shard_map/all_to_all | solution.py:24
  261.4 3.0 %fusion.11 = bf16[512,1024]{1,0:T(8,128)(2,1)} fusion(f32[512,1024]{1,0:T(8,128)} %get-tuple-element.44, bf16[512,1024]{1,0:T(8,128)(2,1)S(1)} %get-tuple-element.40, f32[512]{0:T(512)S(1)} %broadcast_multiply_fusion.2, f32[512]{0:T(512)S(1)} %add_rsqrt_fusion), kind=kLoop, calls=%fused_computation.25 | loop fusion | flops 3145728 | bytes 4198400 | tf_op jit(solution)/shard_map/convert_element_type | solution.py:186
  264.4 2.0 gather_fusion.1
  266.3 2.3 all-to-all-done.6
  268.7 1.1 subtract_multiply_fusion
  269.8 0.7 copy.61
  (59 shorter events, 2.1 us)
Async XLA Ops:
  7.2 18.5 %copy-start.3 = (s32[1,32]{1,0:T(1,128)S(1)}, s32[1,32]{1,0:T(1,128)}, u32[]{:S(2)}) copy-start(s32[1,32]{1,0:T(1,128)} %param.12) | copy-start | bytes 388
  7.2 18.7 %copy-start.4 = (s32[16,256]{1,0:T(8,128)S(1)}, s32[16,256]{1,0:T(8,128)}, u32[]{:S(2)}) copy-start(s32[16,256]{1,0:T(8,128)} %param.16) | copy-start | bytes 49156
  7.2 18.9 %copy-start.5 = (s32[512]{0:T(512)S(1)}, s32[512]{0:T(512)}, u32[]{:S(2)}) copy-start(s32[512]{0:T(512)} %param.15) | copy-start | bytes 6148
  7.2 18.9 %copy-start.1 = (bf16[256,1024]{1,0:T(8,128)(2,1)S(1)}, bf16[256,1024]{1,0:T(8,128)(2,1)}, u32[]{:S(2)}) copy-start(bf16[256,1024]{1,0:T(8,128)(2,1)} %param.17) | copy-start | bytes 1572868
  7.2 115.4 %all-gather.2.cloned.1.call-start = ((), (), s32[]{:S(2)}) async-start(), calls=%async_computation.7 | async-start | bytes 4456448 | tf_op jit(solution)/shard_map/all_gather | solution.py:63
  9.9 121.4 %all-to-all-start = ((bf16[16,512,64]{1,2,0:T(8,128)(2,1)}), bf16[16,512,64]{1,2,0:T(8,128)(2,1)}, u32[]{:S(2)}, u32[]{:S(2)}) async-start(bf16[16,512,64]{1,2,0:T(8,128)(2,1)} %broadcast_in_dim.43), calls=%async_computation | async-start | bytes 2097152 | tf_op jit(solution)/shard_map/all_to_all | solution.py:24
  29.5 2.7 copy-start.6
  29.6 2.7 copy-start.7
  29.6 4.4 %copy-start = (bf16[512,1024]{1,0:T(8,128)(2,1)S(1)}, bf16[512,1024]{1,0:T(8,128)(2,1)}, u32[]{:S(2)}) copy-start(bf16[512,1024]{1,0:T(8,128)(2,1)} %param.11) | copy-start | bytes 3145732
  31.6 91.1 %copy-start.8 = (f32[1024]{0:T(1024)S(1)}, f32[1024]{0:T(1024)}, u32[]{:S(2)}) copy-start(f32[1024]{0:T(1024)} %param.18) | copy-start | bytes 12292
  127.7 1.4 copy-start.2
  131.3 25.5 %all-to-all-start.3 = ((bf16[16,16,1024]{2,1,0:T(8,128)(2,1)}), bf16[16,16,1024]{2,1,0:T(8,128)(2,1)}, u32[]{:S(2)}, u32[]{:S(2)}) async-start(bf16[16,16,1024]{2,1,0:T(8,128)(2,1)} %bitcast.21), calls=%async_computation.3 | async-start | bytes 1048576 | tf_op jit(solution)/shard_map/all_to_all | solution.py:157
  141.7 1.5 copy-start.9
  156.8 24.8 %all-to-all-start.2 = ((s32[32,1,2]{2,1,0:T(1,128)}), s32[32,1,2]{2,1,0:T(1,128)S(1)}, u32[]{:S(2)}, u32[]{:S(2)}) async-start(s32[32,1,2]{2,1,0:T(1,128)} %copy.55), calls=%async_computation.2 | async-start | bytes 32768 | tf_op jit(solution)/shard_map/all_to_all | solution.py:100
  176.3 5.3 %copy-start.10 = (f32[512,256]{0,1:T(8,128)}, f32[512,256]{0,1:T(8,128)S(1)}, u32[]{:S(2)}) copy-start(f32[512,256]{0,1:T(8,128)S(1)} %get-tuple-element.42) | copy-start | bytes 1572868
  181.6 29.8 %all-to-all-start.4 = ((bf16[16,16,1024]{2,1,0:T(8,128)(2,1)}), bf16[16,16,1024]{2,1,0:T(8,128)(2,1)S(1)}, u32[]{:S(2)}, u32[]{:S(2)}) async-start(bf16[16,16,1024]{2,1,0:T(8,128)(2,1)} %bitcast.23), calls=%async_computation.4 | async-start | bytes 1048576 | tf_op jit(solution)/shard_map/all_to_all | solution.py:190
  213.3 23.0 %all-to-all-start.5 = ((bf16[32,256,32]{1,2,0:T(8,128)(2,1)}), bf16[32,256,32]{1,2,0:T(8,128)(2,1)}, u32[]{:S(2)}, u32[]{:S(2)}) async-start(bf16[32,256,32]{1,2,0:T(8,128)(2,1)} %bitcast.26), calls=%async_computation.5 | async-start | bytes 1048576 | tf_op jit(solution)/shard_map/all_to_all | solution.py:41
  236.3 20.5 %all-to-all-start.1 = ((bf16[32,16,1024]{2,1,0:T(8,128)(2,1)}), bf16[32,16,1024]{2,1,0:T(8,128)(2,1)S(1)}, u32[]{:S(2)}, u32[]{:S(2)}) async-start(bf16[32,16,1024]{2,1,0:T(8,128)(2,1)} %broadcast_select_fusion), calls=%async_computation.1 | async-start | bytes 2097152 | tf_op jit(solution)/shard_map/all_to_all | solution.py:99
  257.4 11.2 %all-to-all-start.6 = ((f32[32,1,256]{2,1,0:T(1,128)}), f32[32,1,256]{2,1,0:T(1,128)S(1)}, u32[]{:S(2)}, u32[]{:S(2)}) async-start(f32[32,1,256]{2,1,0:T(1,128)} %broadcast_in_dim.50), calls=%async_computation.6 | async-start | bytes 65536 | tf_op jit(solution)/shard_map/all_to_all | solution.py:24
Sparse Core Ops, SparseCore 0:
  10.1 112.5 all-gather.1
where the time goes:
time: 278 us; the launch traced here: 277 us
  waiting for transfers between devices  147 us (53%)
  starting transfers between devices  66.3 us (24%)
  local copies, waits for them, and re-layouts  18.4 us (7%)
  matrix products  18.3 us (7%)
  between operations  14.3 us (5%)
  other arithmetic  13.3 us (5%)
    all_gather x1, waiting for transfers between devices, hstu_block(): lax.all_gather(w_uvqk, 'item', axis=0, tiled=True)  87.9 us
    all_to_all x1, waiting for transfers between devices, per_device(): lax.all_to_all(negative_terms.reshape(item_count, share, model_width).ast...  22.6 us
    all_to_all x2, starting transfers between devices, from_everyone(): lax.all_to_all(jnp.broadcast_to(shard[None], (count, *shard.shape)), axis...  19.7 us
    all_to_all x1, starting transfers between devices, dispatch(): lax.all_to_all(labels, 'user', split_axis=0, concat_axis=0, tiled=True)  17.8 us
    all_to_all x1, starting transfers between devices, sent_and_summed(): lax.all_to_all(in_blocks(shard, dim, count), axis, 0, 0, tiled=True)  11.2 us
    all_to_all x1, waiting for transfers between devices, dispatch(): lax.all_to_all(parcels, 'user', split_axis=0, concat_axis=0, tiled=True)  11.1 us
    all_to_all x1, waiting for transfers between devices, per_device(): lax.all_to_all(table_low[owned_ids], 'item', split_axis=0, concat_axis=0,...  10.5 us
    all_to_all x1, waiting for transfers between devices, sent_and_summed(): lax.all_to_all(in_blocks(shard, dim, count), axis, 0, 0, tiled=True)  8.47 us
  transfers between devices with their start and end apart: 8, of which 7 were waited for; matrix products, arithmetic and copies ran while one was open for 16% of the time, Pallas kernels for 0%

commit v1 on v0

v1 whole, which is shorter than its diff:
```python
import jax
import jax.numpy as jnp
from jax import lax
from jax.experimental import pallas as pl
from jax.experimental.pallas import tpu as pltpu
from jax.sharding import PartitionSpec as P

norm_epsilon = 1e-05
scale_epsilon = 1e-06
inverse_temp = 20.0
loss_scale = 32.0

F32 = jnp.float32
BF16 = jnp.bfloat16

USERS = 32
ITEMS = 16
PLANE = 16
LANES = 128
ROWS = 512
MOST = 16
WIDTH = 1024
HEAD = 128

FIRST = [[x * 8 + y * 2 for x in range(4)] for y in range(4)] + [
    [x * 8 + y * 2 + 1 for y in range(4)] for x in range(4)
]
SECOND = [[x * 8 + y * 2 for y in range(4)] for x in range(4)] + [
    [x * 8 + y * 2 + 1 for x in range(4)] for y in range(4)
]
SAME_CORE = [[k * 2 + c for k in range(PLANE)] for c in range(2)]
PARTNER = [(k, k ^ 1) for k in range(USERS)]

VMEM = pl.BlockSpec(memory_space=pltpu.VMEM)
SMEM = pl.BlockSpec(memory_space=pltpu.SMEM)
W_ROWS = 512
REST = 208


def shape(dims, kind=BF16):
    return jax.ShapeDtypeStruct(dims, kind)


def dot(a, b, contract=((1,), (0,))):
    return lax.dot_general(a, b, (contract, ((), ())), preferred_element_type=F32)


def call(body, outs, specs, scratch=(), name=None):
    return pl.pallas_call(
        body,
        out_shape=outs,
        in_specs=specs,
        out_specs=jax.tree.map(lambda _: VMEM, outs),
        scratch_shapes=list(scratch),
        name=name,
        compiler_params=pltpu.CompilerParams(vmem_limit_bytes=56 * 2**20),
    )


def forward_body(got, label, out):
    for i in range(ITEMS):
        out[0, i * 32 : (i + 1) * 32, :] = got[i, 0:32, :]
    for b in range(8):
        out[0, W_ROWS + b * 16 : W_ROWS + (b + 1) * 16, :] = (
            got[2 * b, 32:48, :].astype(F32) + got[2 * b + 1, 32:48, :].astype(F32)
        ).astype(BF16)
    quads = got[:, 48:56, :].astype(F32)
    for b in range(4):
        out[0, W_ROWS + 128 + b * 16 : W_ROWS + 144 + b * 16, :] = quads[:, b, :].astype(BF16)
    out[0, W_ROWS + 192 : W_ROWS + 208, :] = label[...]
    for g in range(1, 4):
        out[g] = out[0]


def half_body(x_ref, w_ref, first_ref, u_ref, mixed_ref):
    x = x_ref[...]

    def part(q):
        w = jnp.concatenate([w_ref[2 * q], w_ref[2 * q + 1]], axis=1)
        return jax.nn.silu(dot(x, w)).astype(BF16)

    u_ref[...] = part(0)
    v = part(1)
    q = part(2)
    k = part(3)
    for b in range(4):
        lo, hi = b * 128, (b + 1) * 128
        at = max(lo - 128, 0)
        rows = lo + lax.broadcasted_iota(jnp.int32, (128, hi - at), 0)
        cols = at + lax.broadcasted_iota(jnp.int32, (128, hi - at), 1)
        first = first_ref[lo:hi, :]
        allowed = (cols >= first) & (cols <= rows)
        for h in range(2):
            d0, d1 = h * HEAD, (h + 1) * HEAD
            scores = dot(q[lo:hi, d0:d1], k[at:hi, d0:d1], ((1,), (1,))) * HEAD ** (-0.5)
            weights = jnp.where(allowed, jax.nn.silu(scores), 0.0).astype(BF16)
            mixed_ref[lo:hi, d0:d1] = dot(weights, v[at:hi, d0:d1])


def out_body(tok_ref, u0, m0, rest0, u1, m1, rest1, gain_ref, send_ref, out_ref, parcel_ref):
    a, b = m0[...], m1[...]
    width = 512.0
    center = (jnp.sum(a, axis=1, keepdims=True) + jnp.sum(b, axis=1, keepdims=True)) / width
    a, b = a - center, b - center
    spread = (
        jnp.sum(a * a, axis=1, keepdims=True) + jnp.sum(b * b, axis=1, keepdims=True)
    ) / width
    inv = lax.rsqrt(spread + norm_epsilon)
    ga = (a * inv * gain_ref[:, 0:256] * u0[...].astype(F32)).astype(BF16)
    gb = (b * inv * gain_ref[:, 256:512] * u1[...].astype(F32)).astype(BF16)

    def columns(rest):
        return jnp.concatenate(
            [rest[:, n * 16 : (n + 1) * 16, :].reshape(256, LANES) for n in range(8)], axis=1
        )

    delta = dot(ga, columns(rest0)) + dot(gb, columns(rest1))
    out = (tok_ref[...].astype(F32) + delta).astype(BF16)
    out_ref[...] = out
    parcel_ref[...] = dot(send_ref[...], out).astype(BF16)


def loss_body(core, out_ref, low_ref, rest0, rest1, pos_ref, weight_ref, grad_ref, own_ref, send_ref, own_inner, terms):
    c = core[0]

    def columns(rest):
        return jnp.concatenate(
            [rest[:, 128 + n * 16 : 144 + n * 16, :].reshape(256, LANES) for n in range(4)], axis=1
        ).astype(F32)

    g0, g1 = columns(rest0), columns(rest1)
    size = (jnp.sum(g0 * g0, axis=1, keepdims=True) + jnp.sum(g1 * g1, axis=1, keepdims=True)) / WIDTH
    scale = lax.rsqrt(size + scale_epsilon)
    g0, g1 = (g0 * scale).astype(BF16), (g1 * scale).astype(BF16)
    here = c == 0
    both = jnp.concatenate([jnp.where(here, g0, g1), jnp.where(here, g1, g0)], axis=1)
    row = lax.broadcasted_iota(jnp.int32, (256, 256), 0)
    col = lax.broadcasted_iota(jnp.int32, (256, 256), 1)
    swap = jnp.where(col == (row % 16) * 16 + row // 16, 1.0, 0.0).astype(BF16)
    group = dot(swap, both).astype(BF16)
    rows = jnp.concatenate([low_ref[...], group], axis=0)

    out = out_ref[...].astype(F32)
    out_scale = lax.rsqrt(jnp.mean(out * out, axis=1, keepdims=True) + scale_epsilon)
    hat = out * out_scale
    low = hat.astype(BF16)
    factor = inverse_temp / WIDTH
    raw = dot(low, rows, ((1,), (1,)))
    hit = lax.broadcasted_iota(jnp.int32, (ROWS, 256), 1) == pos_ref[...]
    pos = jnp.exp(jnp.sum(jnp.where(hit, raw[:, :256], 0.0), axis=1, keepdims=True) * factor)
    neg = jnp.exp(raw[:, 256:] * factor)
    total = pos + jnp.sum(neg, axis=1, keepdims=True)
    weight = weight_ref[...]
    pos_grad = weight * (pos / total - 1.0)
    grads = jnp.concatenate(
        [jnp.where(hit, pos_grad, 0.0).astype(BF16), (weight * neg / total).astype(BF16)], axis=1
    )
    grad_hat = dot(grads, rows) * factor
    inner = jnp.mean(grad_hat * hat, axis=1, keepdims=True)
    grad_ref[...] = ((grad_hat - hat * inner) * out_scale).astype(BF16)
    sums = dot(low, grads, ((0,), (0,))) * factor
    terms[...] = sums.astype(BF16).reshape(PLANE, 2, 32, ROWS)
    for k in range(PLANE):
        own_ref[k] = terms[k, c]
        send_ref[k * 32 : (k + 1) * 32, :] = terms[k, 1 - c]
    products = jnp.sum(grads.astype(F32) * raw, axis=0, keepdims=True) * factor
    own_inner[...] = products
    top = products.astype(BF16).astype(F32)
    send_ref[512:528, :] = split_rows(top, products - top).astype(BF16)


def split_rows(top, rest):
    at = lax.broadcasted_iota(jnp.int32, (16, ROWS), 0)
    return jnp.where(at == 0, top, jnp.where(at == 1, rest, 0.0))


def pair_body(own_ref, inner_ref, got_ref, out_ref):
    other = got_ref[512:528, :].astype(F32)
    inner = inner_ref[...] + other[0:1, :] + other[1:2, :]
    top = inner.astype(BF16).astype(F32)
    tail = split_rows(top, inner - top).astype(BF16)
    for k in range(PLANE):
        mine = own_ref[k].astype(F32) + got_ref[k * 32 : (k + 1) * 32, :].astype(F32)
        out_ref[k, 0:32, :] = mine.astype(BF16)
        out_ref[k, 32:48, :] = tail


def plane_body(got_ref, pos_ref, neg_ref):
    acc = got_ref[0].astype(F32)
    for k in range(1, PLANE):
        acc = acc + got_ref[k].astype(F32)
    inner = acc[32:33, :] + acc[33:34, :]
    top = inner.astype(BF16).astype(F32)
    full = jnp.concatenate(
        [acc[0:32, :], split_rows(top, inner - top), jnp.zeros((80, ROWS), F32)], axis=0
    )
    turned = jnp.transpose(full)
    pos_ref[...] = turned[0:256, :]
    neg_ref[...] = turned[256:512, :].astype(BF16)


def item_body(pos_ref, hits_ref, got_ref, hat_ref, scale_ref, out_ref):
    total = pos_ref[...] + dot(hits_ref[...], got_ref[...])
    inner = (total[:, 32:33] + total[:, 33:34]) / WIDTH
    out_ref[...] = (total[:, 0:32] - hat_ref[...] * inner) * scale_ref[...]


def layer_norm(values, gain):
    center = jnp.mean(values, axis=-1, keepdims=True)
    shifted = values - center
    spread = jnp.mean(shifted * shifted, axis=-1, keepdims=True)
    return shifted * lax.rsqrt(spread + norm_epsilon) * gain


def copies(block, count):
    return jnp.broadcast_to(block[None], (count, *block.shape))


def exchange(blocks, axis, groups=None):
    return lax.all_to_all(blocks, axis, 0, 0, tiled=True, axis_index_groups=groups)


def per_device(
    tokens,
    lengths,
    destination,
    worker_offset,
    positives,
    negatives,
    table,
    in_gain,
    w_uvqk,
    out_gain,
    w_out,
):
    item = lax.axis_index("item")
    user = lax.axis_index("user")
    x, y, core = user // 8, (user // 2) % 4, user % 2
    place = jnp.where(core == 0, y * 4 + x, x * 4 + y)
    item_rows = table.shape[0]

    chunk, half = place // 2, place % 2
    block = (chunk // 2) * 4 + core * 2 + chunk % 2
    w_part = lax.dynamic_slice(w_uvqk, (half * 32, block * LANES), (32, LANES))
    o_part = lax.dynamic_slice(w_out, (core * 256 + place * 16, 0), (16, 64))
    blank = jnp.zeros_like(o_part)
    odd = item % 2 == 1
    o_part = jnp.concatenate(
        [jnp.where(odd, blank, o_part), jnp.where(odd, o_part, blank)], axis=1
    )
    ids = lax.dynamic_slice(negatives, (0, item * 16 + place), (ITEMS, 1)) - item * item_rows
    pick = (ids == jnp.arange(item_rows, dtype=jnp.int32)[None, :]).astype(BF16)
    g_part = jnp.dot(pick, lax.dynamic_slice(table, (0, core * 512), (item_rows, 512)))
    first_message = jnp.concatenate(
        [
            copies(jnp.concatenate([w_part, o_part], axis=0), ITEMS),
            jnp.pad(g_part.reshape(ITEMS, 4, LANES), ((0, 0), (0, 4), (0, 0))),
        ],
        axis=1,
    )
    got = exchange(first_message, "item")

    history_len = lengths[0]
    home_start = jnp.cumsum(history_len) - history_len
    row_ids = jnp.arange(ROWS, dtype=jnp.int32)
    inside = (row_ids[:, None] >= home_start[None, :]) & (
        row_ids[:, None] < (home_start + history_len)[None, :]
    )
    valid = jnp.any(inside, axis=1, keepdims=True)
    first = jnp.where(
        valid,
        jnp.sum(jnp.where(inside, home_start[None, :], 0), axis=1, keepdims=True),
        row_ids[:, None],
    )
    weight = jnp.where(valid, loss_scale, 0.0).astype(F32)
    peers = jnp.arange(USERS, dtype=jnp.int32)
    chosen = (destination[0][None, :] == peers[:, None]).astype(jnp.int32)
    first_row = jnp.sum(chosen * home_start[None, :], axis=1)
    count = jnp.sum(chosen * history_len[None, :], axis=1)
    landing = jnp.sum(chosen * worker_offset[0][None, :], axis=1)
    label = jnp.concatenate([landing, count, jnp.zeros((64,), jnp.int32)]).astype(BF16)
    labels = jnp.broadcast_to(label[None], (16, LANES))
    within = jnp.arange(MOST, dtype=jnp.int32)
    source = jnp.where(within[None, :] < count[:, None], first_row[:, None] + within[None, :], -1)
    send = (source.reshape(-1)[:, None] == row_ids[None, :]).astype(BF16)

    message = call(
        forward_body, shape((4, W_ROWS + REST, LANES)), [VMEM, VMEM], name="forward"
    )(got, labels)
    mid = exchange(message, "user", FIRST)
    w_own = exchange(copies(mid[:, :W_ROWS], 4), "user", SECOND).reshape(8, 2 * W_ROWS, LANES)
    w_other = lax.ppermute(w_own, "user", PARTNER)
    rest_own = exchange(copies(mid[:, W_ROWS:], 4), "user", SECOND).reshape(16, REST, LANES)
    rest_other = lax.ppermute(rest_own, "user", PARTNER)

    normed = layer_norm(tokens.astype(F32), in_gain).astype(BF16)
    at = jnp.arange(WIDTH, dtype=jnp.int32)
    wanted = (at % 512) // 32 * 64 + at // 512 * 32 + at % 32
    order = (at[:, None] == wanted[None, :]).astype(BF16)
    normed = jnp.dot(normed, order, preferred_element_type=F32).astype(BF16)
    layer_half = call(
        half_body, (shape((ROWS, 256)), shape((ROWS, 256), F32)), [VMEM] * 3, name="half"
    )
    u_own, mixed_own = layer_half(normed, w_own, first)
    u_other, mixed_other = layer_half(normed, w_other, first)
    gain = jnp.where(core == 0, out_gain, jnp.roll(out_gain, 256))[None]
    home_out, parcels = call(
        out_body, (shape((ROWS, WIDTH)), shape((ROWS, WIDTH))), [VMEM] * 9, name="layer_out"
    )(tokens, u_own, mixed_own, rest_own, u_other, mixed_other, rest_other, gain, send)
    arrived = exchange(parcels.reshape(USERS, MOST, WIDTH), "user").reshape(ROWS, WIDTH)

    near, far = rest_own[:, 192, :], rest_other[:, 192, :]
    mine = (jnp.arange(LANES, dtype=jnp.int32)[None, :] == user).astype(F32)
    mine_count = (jnp.arange(LANES, dtype=jnp.int32)[None, :] == user + USERS).astype(F32)

    def by_user(select):
        a = jnp.sum(near.astype(F32) * select, axis=1)
        b = jnp.sum(far.astype(F32) * select, axis=1)
        even = jnp.where(core == 0, a, b).reshape(4, 4).T
        uneven = jnp.where(core == 0, b, a).reshape(4, 4)
        return jnp.stack([even, uneven], axis=2).reshape(USERS).astype(jnp.int32)

    lower, arrived_count = by_user(mine), by_user(mine_count)
    lands = jnp.where(within[None, :] < arrived_count[:, None], lower[:, None] + within[None, :], -1)
    receive = (jnp.arange(256, dtype=jnp.int32)[:, None] == lands.reshape(-1)[None, :]).astype(BF16)
    layer_out = jnp.dot(receive, arrived, preferred_element_type=F32).astype(BF16)

    table_f = table.astype(F32)
    table_scale = lax.rsqrt(jnp.mean(table_f * table_f, axis=1, keepdims=True) + scale_epsilon)
    table_hat = table_f * table_scale
    table_low = table_hat.astype(BF16)
    positive_local = (positives - item * item_rows)[:, None]
    token_grad, own, sent, own_inner = call(
        loss_body,
        (
            shape((ROWS, WIDTH)),
            shape((PLANE, 32, ROWS)),
            shape((528, ROWS)),
            shape((1, ROWS), F32),
        ),
        [SMEM] + [VMEM] * 6,
        scratch=[pltpu.VMEM((PLANE, 2, 32, ROWS), BF16)],
        name="loss",
    )(core.reshape(1), home_out, table_low, rest_own, rest_other, positive_local, weight)
    partner_terms = lax.ppermute(sent, "user", PARTNER)
    pair = call(pair_body, shape((PLANE, 48, ROWS)), [VMEM] * 3, name="pair")(
        own, own_inner, partner_terms
    )
    plane = exchange(pair, "user", SAME_CORE)
    positive_part, negative_part = call(
        plane_body, (shape((256, LANES), F32), shape((256, LANES))), [VMEM], name="plane"
    )(plane)
    owned = exchange(negative_part.reshape(ITEMS, 16, LANES), "item").reshape(256, LANES)
    owned_ids = lax.dynamic_slice_in_dim(negatives, item * 16, 16, 1) - item * item_rows
    hits = (
        jnp.arange(item_rows, dtype=jnp.int32)[:, None] == owned_ids.reshape(-1)[None, :]
    ).astype(BF16)
    hat_part = lax.dynamic_slice_in_dim(table_hat, user * 32, 32, 1)
    item_grad = call(item_body, shape((256, 32), F32), [VMEM] * 5, name="item_grad")(
        positive_part, hits, owned, hat_part, table_scale
    )
    return (layer_out, token_grad, item_grad)


def solution(mesh):
    return jax.shard_map(
        per_device,
        mesh=mesh,
        in_specs=(
            P(("user", "item"), None),
            P(("user", "item"), None),
            P(("user", "item"), None),
            P(("user", "item"), None),
            P(("user", "item")),
            P(),
            P("item", None),
            P(),
            P("item", None),
            P(),
            P(None, "item"),
        ),
        out_specs=(P(("user", "item"), None), P(("user", "item"), None), P("item", "user")),
        check_vma=False,
    )
```

time: 278 us -> 196 us (0.71)
  waiting for transfers between devices: 147 us -> 63.4 us
  Pallas kernels: 0 us -> 28.3 us
  matrix products: 18.3 us -> 4.79 us
  between operations: 14.3 us -> 1.07 us
  starting transfers between devices: 66.3 us -> 53.5 us
  blocking collectives: 0 us -> 12.3 us
    all_gather x1 -> x0, waiting for transfers between devices: 87.9 us -> none  [hstu_block(): lax.all_gather(w_uvqk, 'item', axis=0, tiled=True)]
    pallas_call x0 -> x8, Pallas kernels: none -> 28.3 us  [the longest x1 5.9 us: per_device(): call(loss_body, (shape((ROWS, WIDTH)), shape((PLANE, 32, ROWS)), shape((5...]
    all_to_all x7 -> x6, starting transfers between devices: 66.3 us -> 38.4 us  [exchange(): lax.all_to_all(blocks, axis, 0, 0, tiled=True, axis_index_groups=groups)]
    ppermute x0 -> x3, starting transfers between devices: none -> 15.1 us  [the longest x1 10.1 us: per_device(): w_other = lax.ppermute(w_own, 'user', PARTNER)]
    dot_general x8 -> x3, matrix products: 18.3 us -> 4.79 us  [the longest x1 2.42 us: per_device(): normed = jnp.dot(normed, order, preferred_element_type=F32).astype(BF16)]
    all_to_all x0 -> x1, blocking collectives: none -> 12.3 us  [exchange(): lax.all_to_all(blocks, axis, 0, 0, tiled=True, axis_index_groups=groups)]
    gather x4 -> x0, local copies, waits for them, and re-layouts: 8.04 us -> none  [the longest x1 2.06 us: dispatch(): rows[picked]]
    all_to_all x7 -> x6, waiting for transfers between devices: 58.2 us -> 61.2 us  [exchange(): lax.all_to_all(blocks, axis, 0, 0, tiled=True, axis_index_groups=groups)]
  transfers between devices with their start and end apart: 8 -> 9, of which waited for: 7 -> 7; matrix products, arithmetic and copies ran while one was open for 16% -> 12% of each run, Pallas kernels for 0% -> 6%
where the time goes in v1:
time: 196 us; the launch traced here: 194 us
  waiting for transfers between devices  63.4 us (32%)
  starting transfers between devices  53.5 us (27%)
  Pallas kernels  28.3 us (14%)
  local copies, waits for them, and re-layouts  18.2 us (9%)
  other arithmetic  12.7 us (6%)
  blocking collectives  12.3 us (6%)
  matrix products  4.79 us (2%)
    all_to_all x6, waiting for transfers between devices, exchange(): lax.all_to_all(blocks, axis, 0, 0, tiled=True, axis_index_groups=groups)  61.2 us
    all_to_all x6, starting transfers between devices, exchange(): lax.all_to_all(blocks, axis, 0, 0, tiled=True, axis_index_groups=groups)  38.4 us
    all_to_all x1, blocking collectives, exchange(): lax.all_to_all(blocks, axis, 0, 0, tiled=True, axis_index_groups=groups)  12.3 us
    ppermute x1, starting transfers between devices, per_device(): w_other = lax.ppermute(w_own, 'user', PARTNER)  10.1 us
    unnamed x36, local copies, waits for them, and re-layouts  5.92 us
    pallas_call x1, Pallas kernels, per_device(): call(loss_body, (shape((ROWS, WIDTH)), shape((PLANE, 32, ROWS)), shape((5...  5.9 us
    pallas_call x1, Pallas kernels, per_device(): call(out_body, (shape((ROWS, WIDTH)), shape((ROWS, WIDTH))), [VMEM] * 9,...  4.87 us
    pallas_call x1, Pallas kernels, per_device(): u_other, mixed_other = layer_half(normed, w_other, first)  4.64 us
  transfers between devices with their start and end apart: 9, of which 7 were waited for; matrix products, arithmetic and copies ran while one was open for 12% of the time, Pallas kernels for 6%

profile of v1, /device:TPU:1, one launch (start us, length us, event | category | flops | bytes accessed | tf_op | source)
XLA Modules:
  0.0 194.2 jit_solution(11792578792139401056)
XLA Ops:
  0.8 0.9 subtract_reduce_fusion
  1.6 1.1 fusion.16
  4.5 15.7 %all-to-all-start = ((bf16[16,56,128]{2,1,0:T(8,128)(2,1)}), bf16[16,56,128]{2,1,0:T(8,128)(2,1)S(1)}, u32[]{:S(2)}, u32[]{:S(2)}) async-start(bf16[16,56,128]{2,1,0:T(8,128)(2,1)} %fusion.19), calls=%async_computation | async-start | bytes 458752 | tf_op jit(solution)/shard_map/all_to_all | solution.py:220
  21.8 0.8 select_reduce_fusion.1
  22.8 10.1 %all-to-all-done.got = bf16[16,56,128]{2,1,0:T(8,128)(2,1)S(1)} async-done(((bf16[16,56,128]{2,1,0:T(8,128)(2,1)}), bf16[16,56,128]{2,1,0:T(8,128)(2,1)S(1)}, u32[]{:S(2)}, u32[]{:S(2)}) %all-to-all-start) | async-done | bytes 229408 | tf_op jit(solution)/shard_map/all_to_all | solution.py:220
  33.6 1.9 forward.1
  35.5 12.3 %all_to_all.35 = bf16[4,720,128]{2,1,0:T(8,128)(2,1)S(1)} all-to-all(bf16[4,720,128]{2,1,0:T(8,128)(2,1)} %forward.1), channel_id=1, replica_groups={{0,128,256,384},{32,160,288,416},{64,192,320,448},{96,224,352,480},{16,..., dimensions={0} | all-to-all | bytes 1474560 | tf_op jit(solution)/shard_map/all_to_all | solution.py:220
  47.8 0.9 copy-done.8
  48.7 1.8 broadcast_in_dim.45
  50.4 4.2 %all-to-all-start.3 = ((bf16[4,4,512,128]{3,2,1,0:T(8,128)(2,1)}), bf16[4,4,512,128]{3,2,1,0:T(8,128)(2,1)S(1)}, u32[]{:S(2)}, u32[]{:S(2)}) async-start(bf16[4,4,512,128]{3,2,1,0:T(8,128)(2,1)} %broadcast_in_dim.45), calls=%async_computation.3 | async-start | bytes 4194304 | tf_op jit(solution)/shard_map/all_to_all | solution.py:220
  54.8 0.9 copy.68
  55.8 0.9 copy.72.pos_ref
  56.8 0.9 reshape_select_fusion.weight_ref
  57.7 1.2 fusion.8
  59.5 10.5 %all-to-all-done.3 = bf16[4,4,512,128]{3,2,1,0:T(8,128)(2,1)S(1)} async-done(((bf16[4,4,512,128]{3,2,1,0:T(8,128)(2,1)}), bf16[4,4,512,128]{3,2,1,0:T(8,128)(2,1)S(1)}, u32[]{:S(2)}, u32[]{:S(2)}) %all-to-all-start.3) | async-done | bytes 2097184 | tf_op jit(solution)/shard_map/all_to_all | solution.py:220
  70.0 10.1 %collective-permute-start.1 = (bf16[8,1024,128]{2,1,0:T(8,128)(2,1)S(1)}, bf16[8,1024,128]{2,1,0:T(8,128)(2,1)}, u32[]{:S(2)}, u32[]{:S(2)}) collective-permute-start(bf16[8,1024,128]{2,1,0:T(8,128)(2,1)S(1)} %bitcast.34), channel_id=1, source_target_pairs={{0,16},{16,0},{32,48},{48,32},{64,80},{80,64},{96,112},{112,96},{1... | collective-permute-start | bytes 6291464 | tf_op jit(solution)/shard_map/ppermute | solution.py:292
  80.3 1.1 broadcast_in_dim.43
  81.5 4.2 %all-to-all-start.2 = ((bf16[4,4,208,128]{3,1,2,0:T(4,128)(2,1)}), bf16[4,4,208,128]{3,1,2,0:T(4,128)(2,1)}, u32[]{:S(2)}, u32[]{:S(2)}) async-start(bf16[4,4,208,128]{3,1,2,0:T(4,128)(2,1)} %broadcast_in_dim.43), calls=%async_computation.2 | async-start | bytes 1703936 | tf_op jit(solution)/shard_map/all_to_all | solution.py:220
  86.3 0.9 fusion.13.send_ref
  87.2 7.5 %all-to-all-done.2 = bf16[4,4,208,128]{3,1,2,0:T(4,128)(2,1)} async-done(((bf16[4,4,208,128]{3,1,2,0:T(4,128)(2,1)}), bf16[4,4,208,128]{3,1,2,0:T(4,128)(2,1)}, u32[]{:S(2)}, u32[]{:S(2)}) %all-to-all-start.2) | async-done | bytes 852000 | tf_op jit(solution)/shard_map/all_to_all | solution.py:220
  94.7 1.5 copy.60
  96.2 0.9 copy-done.5
  97.4 3.0 %collective-permute-start = (bf16[16,208,128]{2,1,0:T(8,128)(2,1)S(1)}, bf16[16,208,128]{2,1,0:T(8,128)(2,1)S(1)}, u32[]{:S(2)}, u32[]{:S(2)}) collective-permute-start(bf16[16,208,128]{2,1,0:T(8,128)(2,1)S(1)} %copy.61.rest0), channel_id=1, source_target_pairs={{0,16},{16,0},{32,48},{48,32},{64,80},{80,64},{96,112},{112,96},{1... | collective-permute-start | bytes 2555912 | tf_op jit(solution)/shard_map/ppermute | solution.py:294
  100.4 0.8 reshape_select_fusion.1.first_ref
  101.2 1.4 convert_multiply_fusion
  102.6 2.4 %fusion.7.x_ref = bf16[512,1024]{1,0:T(8,128)(2,1)} fusion(s32[1024]{0:T(1024)S(1)} %fusion.38, bf16[512,1024]{1,0:T(8,128)(2,1)S(1)} %copy-done.1, f32[1024]{0:T(1024)S(1)} %copy-done.16, f32[512]{0:T(512)S(1)} %add_rsqrt_fusion, f32[512]{0:T(512)S(1)} %broadcast_multiply_fusion), kind=kOutput, calls=%fused_computation.10 | convolution fusion | flops 1077936128 | bytes 2109440 | tf_op jit(solution)/shard_map/dot_general | solution.py:300
  105.0 4.6 %half.2 = (bf16[512,256]{1,0:T(8,128)(2,1)}, f32[512,256]{1,0:T(8,128)}) custom-call(bf16[512,1024]{1,0:T(8,128)(2,1)} %fusion.7.x_ref, bf16[8,1024,128]{2,1,0:T(8,128)(2,1)} %bitcast.35, s32[512,1]{1,0:T(8,128)} %reshape_select_fusion.1.first_ref), custom_call_target="tpu_custom_call" | custom-call | tf_op jit(solution)/shard_map/half/pallas_call | solution.py:304
  109.6 4.6 %half.3 = (bf16[512,256]{1,0:T(8,128)(2,1)}, f32[512,256]{1,0:T(8,128)}) custom-call(bf16[512,1024]{1,0:T(8,128)(2,1)} %fusion.7.x_ref, bf16[8,1024,128]{2,1,0:T(8,128)(2,1)} %collective-permute-done.1.w_ref, s32[512,1]{1,0:T(8,128)} %reshape_select_fusion.1.first_ref), custom_call_target="tpu_custom_call" | custom-call | tf_op jit(solution)/shard_map/half/pallas_call | solution.py:305
  114.3 0.9 copy-done.4
  115.2 4.9 %layer_out.1 = (bf16[512,1024]{1,0:T(8,128)(2,1)}, bf16[512,1024]{1,0:T(8,128)(2,1)}) custom-call(bf16[512,1024]{1,0:T(8,128)(2,1)} %tok_ref.1, bf16[512,256]{1,0:T(8,128)(2,1)} %get-tuple-element.15.u0, f32[512,256]{1,0:T(8,128)} %get-tuple-element.16.m0, bf16[16,208,128]{2,1,0:T(8,128)(2,1)} %copy-done.3, bf16[512,256]{1,0:T(8,128)(2,1)} %get-tuple-element.17.u1, ...), custom_call_target="tpu_custom_call" | custom-call | tf_op jit(solution)/shard_map/layer_out/pallas_call | solution.py:307
  120.1 5.9 %loss.1 = (bf16[512,1024]{1,0:T(8,128)(2,1)}, bf16[16,32,512]{2,1,0:T(8,128)(2,1)}, bf16[528,512]{1,0:T(8,128)(2,1)}, f32[1,512]{1,0:T(1,128)}) custom-call(s32[1]{0:T(128)} %bitcast.18.core, bf16[512,1024]{1,0:T(8,128)(2,1)} %get-tuple-element.20.out_ref, bf16[256,1024]{1,0:T(8,128)(2,1)} %get-tuple-element.49.low_ref, bf16[16,208,128]{2,1,0:T(8,128)(2,1)} %copy-done.3, ...), custom_call_target="tpu_custom_call" | custom-call | tf_op jit(solution)/shard_map/loss/pallas_call | solution.py:333
  126.0 2.0 %collective-permute-start.2 = (bf16[528,512]{1,0:T(8,128)(2,1)}, bf16[528,512]{1,0:T(8,128)(2,1)S(1)}, u32[]{:S(2)}, u32[]{:S(2)}) collective-permute-start(bf16[528,512]{1,0:T(8,128)(2,1)} %get-tuple-element.24), channel_id=1, source_target_pairs={{0,16},{16,0},{32,48},{48,32},{64,80},{80,64},{96,112},{112,96},{1... | collective-permute-start | bytes 1622024 | tf_op jit(solution)/shard_map/ppermute | solution.py:345
  128.0 2.1 %collective-permute-done.2.got_ref = bf16[528,512]{1,0:T(8,128)(2,1)S(1)} collective-permute-done((bf16[528,512]{1,0:T(8,128)(2,1)}, bf16[528,512]{1,0:T(8,128)(2,1)S(1)}, u32[]{:S(2)}, u32[]{:S(2)}) %collective-permute-start.2) | collective-permute-done | bytes 540704 | tf_op jit(solution)/shard_map/ppermute | solution.py:345
  130.1 0.8 copy-done.11
  130.9 2.3 %pair.1 = bf16[16,48,512]{2,1,0:T(8,128)(2,1)} custom-call(bf16[16,32,512]{2,1,0:T(8,128)(2,1)} %get-tuple-element.22.own_ref, f32[1,512]{1,0:T(1,128)} %get-tuple-element.23.inner_ref, bf16[528,512]{1,0:T(8,128)(2,1)} %copy-done.11), custom_call_target="tpu_custom_call" | custom-call | tf_op jit(solution)/shard_map/pair/pallas_call | solution.py:346
  133.2 3.6 %all-to-all-start.5 = ((bf16[16,48,512]{2,1,0:T(8,128)(2,1)}), bf16[16,48,512]{2,1,0:T(8,128)(2,1)S(1)}, u32[]{:S(2)}, u32[]{:S(2)}) async-start(bf16[16,48,512]{2,1,0:T(8,128)(2,1)} %pair.1), calls=%async_computation.5 | async-start | bytes 1572864 | tf_op jit(solution)/shard_map/all_to_all | solution.py:220
  137.0 1.7 constant_dynamic-slice_fusion.hat_ref
  139.4 11.3 %all-to-all-done.5.got_ref = bf16[16,48,512]{2,1,0:T(8,128)(2,1)S(1)} async-done(((bf16[16,48,512]{2,1,0:T(8,128)(2,1)}), bf16[16,48,512]{2,1,0:T(8,128)(2,1)S(1)}, u32[]{:S(2)}, u32[]{:S(2)}) %all-to-all-start.5) | async-done | bytes 786464 | tf_op jit(solution)/shard_map/all_to_all | solution.py:220
  150.7 5.3 %all-to-all-start.4 = ((bf16[32,16,1024]{2,1,0:T(8,128)(2,1)}), bf16[32,16,1024]{2,1,0:T(8,128)(2,1)S(1)}, u32[]{:S(2)}, u32[]{:S(2)}) async-start(bf16[32,16,1024]{2,1,0:T(8,128)(2,1)} %bitcast.16), calls=%async_computation.4 | async-start | bytes 2097152 | tf_op jit(solution)/shard_map/all_to_all | solution.py:220
  156.0 0.8 copy.73.scale_ref
  157.5 0.8 multiply_reduce_fusion.1
  159.5 2.0 %plane.1 = (f32[256,128]{1,0:T(8,128)}, bf16[256,128]{1,0:T(8,128)(2,1)}) custom-call(bf16[16,48,512]{2,1,0:T(8,128)(2,1)} %copy-done.7), custom_call_target="tpu_custom_call" | custom-call | tf_op jit(solution)/shard_map/plane/pallas_call | solution.py:350
  161.5 11.4 %all-to-all-done.4 = bf16[32,16,1024]{2,1,0:T(8,128)(2,1)S(1)} async-done(((bf16[32,16,1024]{2,1,0:T(8,128)(2,1)}), bf16[32,16,1024]{2,1,0:T(8,128)(2,1)S(1)}, u32[]{:S(2)}, u32[]{:S(2)}) %all-to-all-start.4) | async-done | bytes 1048608 | tf_op jit(solution)/shard_map/all_to_all | solution.py:220
  173.0 5.3 %all-to-all-start.6 = ((bf16[16,16,128]{2,1,0:T(8,128)(2,1)}), bf16[16,16,128]{2,1,0:T(8,128)(2,1)S(1)}, u32[]{:S(2)}, u32[]{:S(2)}) async-start(bf16[16,16,128]{2,1,0:T(8,128)(2,1)} %bitcast.40), calls=%async_computation.6 | async-start | bytes 131072 | tf_op jit(solution)/shard_map/all_to_all | solution.py:220
  178.3 1.2 convolution_convert_fusion
  179.5 10.4 %all-to-all-done.6 = bf16[16,16,128]{2,1,0:T(8,128)(2,1)S(1)} async-done(((bf16[16,16,128]{2,1,0:T(8,128)(2,1)}), bf16[16,16,128]{2,1,0:T(8,128)(2,1)S(1)}, u32[]{:S(2)}, u32[]{:S(2)}) %all-to-all-start.6) | async-done | bytes 65568 | tf_op jit(solution)/shard_map/all_to_all | solution.py:220
  190.5 2.1 %item_grad.1 = f32[256,32]{1,0:T(8,128)} custom-call(f32[256,128]{1,0:T(8,128)} %get-tuple-element.25.pos_ref, bf16[256,256]{1,0:T(8,128)(2,1)} %fusion.18.hits_ref, bf16[256,128]{1,0:T(8,128)(2,1)} %bitcast.39, f32[256,32]{1,0:T(8,128)} %constant_dynamic-slice_fusion.hat_ref, f32[256,1]{1,0:T(8,128)} %copy.73.scale_ref), custom_call_target="tpu_custom_call" | custom-call | tf_op jit(solution)/shard_map/item_grad/pallas_call | solution.py:359
  192.6 1.6 copy.74
  (88 shorter events, 9.4 us)
Async XLA Ops:
  0.6 2.2 %copy-start = (bf16[512,64]{0,1:T(8,128)(2,1)S(1)}, bf16[512,64]{0,1:T(8,128)(2,1)}, u32[]{:S(2)}) copy-start(bf16[512,64]{0,1:T(8,128)(2,1)} %param.21) | copy-start | bytes 196612
  4.5 28.4 %all-to-all-start = ((bf16[16,56,128]{2,1,0:T(8,128)(2,1)}), bf16[16,56,128]{2,1,0:T(8,128)(2,1)S(1)}, u32[]{:S(2)}, u32[]{:S(2)}) async-start(bf16[16,56,128]{2,1,0:T(8,128)(2,1)} %fusion.19), calls=%async_computation | async-start | bytes 458752 | tf_op jit(solution)/shard_map/all_to_all | solution.py:220
  32.9 0.7 copy-start.10
  47.8 0.9 copy-start.8
  50.4 5.4 %copy-start.15 = (s32[512]{0:T(512)S(1)}, s32[512]{0:T(512)}, u32[]{:S(2)}) copy-start(s32[512]{0:T(512)} %param.15) | copy-start | bytes 6148
  50.4 8.5 %copy-start.1 = (bf16[512,1024]{1,0:T(8,128)(2,1)S(1)}, bf16[512,1024]{1,0:T(8,128)(2,1)}, u32[]{:S(2)}) copy-start(bf16[512,1024]{1,0:T(8,128)(2,1)} %tok_ref.1) | copy-start | bytes 3145732
  50.4 19.6 %all-to-all-start.3 = ((bf16[4,4,512,128]{3,2,1,0:T(8,128)(2,1)}), bf16[4,4,512,128]{3,2,1,0:T(8,128)(2,1)S(1)}, u32[]{:S(2)}, u32[]{:S(2)}) async-start(bf16[4,4,512,128]{3,2,1,0:T(8,128)(2,1)} %broadcast_in_dim.45), calls=%async_computation.3 | async-start | bytes 4194304 | tf_op jit(solution)/shard_map/all_to_all | solution.py:220
  54.7 25.5 %copy-start.14 = (f32[512]{0:T(512)S(1)}, f32[512]{0:T(512)}, u32[]{:S(2)}) copy-start(f32[512]{0:T(512)} %param.20) | copy-start | bytes 6148
  54.7 25.6 %slice-start = ((bf16[4,720,128]{2,1,0:T(8,128)(2,1)}), bf16[4,208,128]{2,1,0:T(8,128)(2,1)S(1)}, s32[]{:S(2)}) async-start(bf16[4,720,128]{2,1,0:T(8,128)(2,1)} %copy-done.8), calls=%async_computation.7 | async-start | bytes 425984 | tf_op jit(solution)/shard_map/slice | solution.py:293
  70.0 26.2 %copy-start.2 = (bf16[4,4,512,128]{3,2,1,0:T(8,128)(2,1)}, bf16[4,4,512,128]{3,2,1,0:T(8,128)(2,1)S(1)}, u32[]{:S(2)}) copy-start(bf16[4,4,512,128]{3,2,1,0:T(8,128)(2,1)S(1)} %all-to-all-done.3) | copy-start | bytes 6291460
  70.0 39.6 %collective-permute-start.1 = (bf16[8,1024,128]{2,1,0:T(8,128)(2,1)S(1)}, bf16[8,1024,128]{2,1,0:T(8,128)(2,1)}, u32[]{:S(2)}, u32[]{:S(2)}) collective-permute-start(bf16[8,1024,128]{2,1,0:T(8,128)(2,1)S(1)} %bitcast.34), channel_id=1, source_target_pairs={{0,16},{16,0},{32,48},{48,32},{64,80},{80,64},{96,112},{112,96},{1... | collective-permute-start | bytes 6291464 | tf_op jit(solution)/shard_map/ppermute | solution.py:292
  81.5 13.2 %all-to-all-start.2 = ((bf16[4,4,208,128]{3,1,2,0:T(4,128)(2,1)}), bf16[4,4,208,128]{3,1,2,0:T(4,128)(2,1)}, u32[]{:S(2)}, u32[]{:S(2)}) async-start(bf16[4,4,208,128]{3,1,2,0:T(4,128)(2,1)} %broadcast_in_dim.43), calls=%async_computation.2 | async-start | bytes 1703936 | tf_op jit(solution)/shard_map/all_to_all | solution.py:220
  85.7 14.7 %copy-start.9 = (s32[512,1]{1,0:T(8,128)S(1)}, s32[512,1]{1,0:T(8,128)}, u32[]{:S(2)}) copy-start(s32[512,1]{1,0:T(8,128)} %copy.68) | copy-start | bytes 6148
  94.7 6.5 %copy-start.6 = (bf16[256,1024]{1,0:T(8,128)(2,1)S(1)}, bf16[256,1024]{1,0:T(8,128)(2,1)}, u32[]{:S(2)}) copy-start(bf16[256,1024]{1,0:T(8,128)(2,1)} %param.17) | copy-start | bytes 1572868
  96.2 0.9 copy-start.5
  97.2 5.4 %copy-start.16 = (f32[1024]{0:T(1024)S(1)}, f32[1024]{0:T(1024)}, u32[]{:S(2)}) copy-start(f32[1024]{0:T(1024)} %param.18) | copy-start | bytes 12292
  97.4 7.6 %copy-start.3 = (bf16[16,208,128]{2,1,0:T(8,128)(2,1)}, bf16[16,208,128]{2,1,0:T(8,128)(2,1)S(1)}, u32[]{:S(2)}) copy-start(bf16[16,208,128]{2,1,0:T(8,128)(2,1)S(1)} %copy.61.rest0) | copy-start | bytes 2555908
  97.4 16.9 %collective-permute-start = (bf16[16,208,128]{2,1,0:T(8,128)(2,1)S(1)}, bf16[16,208,128]{2,1,0:T(8,128)(2,1)S(1)}, u32[]{:S(2)}, u32[]{:S(2)}) collective-permute-start(bf16[16,208,128]{2,1,0:T(8,128)(2,1)S(1)} %copy.61.rest0), channel_id=1, source_target_pairs={{0,16},{16,0},{32,48},{48,32},{64,80},{80,64},{96,112},{112,96},{1... | collective-permute-start | bytes 2555912 | tf_op jit(solution)/shard_map/ppermute | solution.py:294
  114.3 0.9 copy-start.4
  126.0 10.9 %copy-start.13 = (s32[16,256]{1,0:T(8,128)S(1)}, s32[16,256]{1,0:T(8,128)}, u32[]{:S(2)}) copy-start(s32[16,256]{1,0:T(8,128)} %param.16) | copy-start | bytes 49156
  126.0 4.2 %collective-permute-start.2 = (bf16[528,512]{1,0:T(8,128)(2,1)}, bf16[528,512]{1,0:T(8,128)(2,1)S(1)}, u32[]{:S(2)}, u32[]{:S(2)}) collective-permute-start(bf16[528,512]{1,0:T(8,128)(2,1)} %get-tuple-element.24), channel_id=1, source_target_pairs={{0,16},{16,0},{32,48},{48,32},{64,80},{80,64},{96,112},{112,96},{1... | collective-permute-start | bytes 1622024 | tf_op jit(solution)/shard_map/ppermute | solution.py:345
  130.1 0.8 copy-start.11
  133.2 17.4 %all-to-all-start.5 = ((bf16[16,48,512]{2,1,0:T(8,128)(2,1)}), bf16[16,48,512]{2,1,0:T(8,128)(2,1)S(1)}, u32[]{:S(2)}, u32[]{:S(2)}) async-start(bf16[16,48,512]{2,1,0:T(8,128)(2,1)} %pair.1), calls=%async_computation.5 | async-start | bytes 1572864 | tf_op jit(solution)/shard_map/all_to_all | solution.py:220
  150.7 8.9 %copy-start.7 = (bf16[16,48,512]{2,1,0:T(8,128)(2,1)}, bf16[16,48,512]{2,1,0:T(8,128)(2,1)S(1)}, u32[]{:S(2)}) copy-start(bf16[16,48,512]{2,1,0:T(8,128)(2,1)S(1)} %all-to-all-done.5.got_ref) | copy-start | bytes 2359300
  150.7 22.3 %all-to-all-start.4 = ((bf16[32,16,1024]{2,1,0:T(8,128)(2,1)}), bf16[32,16,1024]{2,1,0:T(8,128)(2,1)S(1)}, u32[]{:S(2)}, u32[]{:S(2)}) async-start(bf16[32,16,1024]{2,1,0:T(8,128)(2,1)} %bitcast.16), calls=%async_computation.4 | async-start | bytes 2097152 | tf_op jit(solution)/shard_map/all_to_all | solution.py:220
  173.0 17.0 %all-to-all-start.6 = ((bf16[16,16,128]{2,1,0:T(8,128)(2,1)}), bf16[16,16,128]{2,1,0:T(8,128)(2,1)S(1)}, u32[]{:S(2)}, u32[]{:S(2)}) async-start(bf16[16,16,128]{2,1,0:T(8,128)(2,1)} %bitcast.40), calls=%async_computation.6 | async-start | bytes 131072 | tf_op jit(solution)/shard_map/all_to_all | solution.py:220
  189.9 0.6 copy-start.12

commit v2 on v1

--- a/solution.py
+++ b/solution.py
@@ -4,6 +4,7 @@
 from jax.experimental import pallas as pl
 from jax.experimental.pallas import tpu as pltpu
 from jax.sharding import PartitionSpec as P
+
 
 norm_epsilon = 1e-05
 scale_epsilon = 1e-06
@@ -45,15 +46,14 @@
     return lax.dot_general(a, b, (contract, ((), ())), preferred_element_type=F32)
 
 
-def call(body, outs, specs, scratch=(), name=None):
+def call(body, outs, specs, scratch=(), mib=8):
     return pl.pallas_call(
         body,
         out_shape=outs,
         in_specs=specs,
         out_specs=jax.tree.map(lambda _: VMEM, outs),
         scratch_shapes=list(scratch),
-        name=name,
-        compiler_params=pltpu.CompilerParams(vmem_limit_bytes=56 * 2**20),
+        compiler_params=pltpu.CompilerParams(vmem_limit_bytes=mib * 2**20),
     )
 
 
@@ -72,11 +72,27 @@
         out[g] = out[0]
 
 
-def half_body(x_ref, w_ref, first_ref, u_ref, mixed_ref):
+def half_body(x_ref, w_ref, first_ref, u_ref, mixed_ref, o_ref, g_ref, label_ref):
     x = x_ref[...]
+    for n in range(8):
+        o_ref[:, n * LANES : (n + 1) * LANES] = w_ref[
+            :, W_ROWS + n * 16 : W_ROWS + (n + 1) * 16, :
+        ].reshape(256, LANES)
+    for n in range(4):
+        g_ref[:, n * LANES : (n + 1) * LANES] = w_ref[
+            :, W_ROWS + 128 + n * 16 : W_ROWS + 144 + n * 16, :
+        ].reshape(256, LANES)
+    for n in range(PLANE):
+        label_ref[n : n + 1, :] = w_ref[n, W_ROWS + 192 : W_ROWS + 208, :].astype(F32)[0:1, :]
 
     def part(q):
-        w = jnp.concatenate([w_ref[2 * q], w_ref[2 * q + 1]], axis=1)
+        w = jnp.concatenate(
+            [
+                jnp.concatenate([w_ref[n, :W_ROWS, :], w_ref[n + 1, :W_ROWS, :]], axis=0)
+                for n in (4 * q, 4 * q + 2)
+            ],
+            axis=1,
+        )
         return jax.nn.silu(dot(x, w)).astype(BF16)
 
     u_ref[...] = part(0)
@@ -97,7 +113,7 @@
             mixed_ref[lo:hi, d0:d1] = dot(weights, v[at:hi, d0:d1])
 
 
-def out_body(tok_ref, u0, m0, rest0, u1, m1, rest1, gain_ref, send_ref, out_ref, parcel_ref):
+def out_body(tok_ref, u0, m0, o0, u1, m1, o1, gain_ref, send_ref, out_ref, parcel_ref):
     a, b = m0[...], m1[...]
     width = 512.0
     center = (jnp.sum(a, axis=1, keepdims=True) + jnp.sum(b, axis=1, keepdims=True)) / width
@@ -109,26 +125,16 @@
     ga = (a * inv * gain_ref[:, 0:256] * u0[...].astype(F32)).astype(BF16)
     gb = (b * inv * gain_ref[:, 256:512] * u1[...].astype(F32)).astype(BF16)
 
-    def columns(rest):
-        return jnp.concatenate(
-            [rest[:, n * 16 : (n + 1) * 16, :].reshape(256, LANES) for n in range(8)], axis=1
-        )
-
-    delta = dot(ga, columns(rest0)) + dot(gb, columns(rest1))
+    delta = dot(ga, o0[...]) + dot(gb, o1[...])
     out = (tok_ref[...].astype(F32) + delta).astype(BF16)
     out_ref[...] = out
     parcel_ref[...] = dot(send_ref[...], out).astype(BF16)
 
 
-def loss_body(core, out_ref, low_ref, rest0, rest1, pos_ref, weight_ref, grad_ref, own_ref, send_ref, own_inner, terms):
+def loss_body(core, out_ref, low_ref, g0_ref, g1_ref, pos_ref, weight_ref, grad_ref, own_ref, send_ref, own_inner, terms):
     c = core[0]
 
-    def columns(rest):
-        return jnp.concatenate(
-            [rest[:, 128 + n * 16 : 144 + n * 16, :].reshape(256, LANES) for n in range(4)], axis=1
-        ).astype(F32)
-
-    g0, g1 = columns(rest0), columns(rest1)
+    g0, g1 = g0_ref[...].astype(F32), g1_ref[...].astype(F32)
     size = (jnp.sum(g0 * g0, axis=1, keepdims=True) + jnp.sum(g1 * g1, axis=1, keepdims=True)) / WIDTH
     scale = lax.rsqrt(size + scale_epsilon)
     g0, g1 = (g0 * scale).astype(BF16), (g1 * scale).astype(BF16)
@@ -191,18 +197,16 @@
         acc = acc + got_ref[k].astype(F32)
     inner = acc[32:33, :] + acc[33:34, :]
     top = inner.astype(BF16).astype(F32)
-    full = jnp.concatenate(
-        [acc[0:32, :], split_rows(top, inner - top), jnp.zeros((80, ROWS), F32)], axis=0
-    )
-    turned = jnp.transpose(full)
-    pos_ref[...] = turned[0:256, :]
-    neg_ref[...] = turned[256:512, :].astype(BF16)
+    full = jnp.concatenate([acc[0:32, :], split_rows(top, inner - top)], axis=0)
+    pos_ref[...] = full[:, 0:256]
+    tail = jnp.concatenate([full[:, 256:512], jnp.zeros((80, 256), F32)], axis=0)
+    neg_ref[...] = jnp.transpose(tail).astype(BF16)
 
 
 def item_body(pos_ref, hits_ref, got_ref, hat_ref, scale_ref, out_ref):
-    total = pos_ref[...] + dot(hits_ref[...], got_ref[...])
-    inner = (total[:, 32:33] + total[:, 33:34]) / WIDTH
-    out_ref[...] = (total[:, 0:32] - hat_ref[...] * inner) * scale_ref[...]
+    total = pos_ref[...] + dot(got_ref[...], hits_ref[...], ((0,), (0,)))[0:48, :]
+    inner = (total[32:33, :] + total[33:34, :]) / WIDTH
+    out_ref[...] = (total[0:32, :] - hat_ref[...] * inner) * scale_ref[...]
 
 
 def layer_norm(values, gain):
@@ -284,52 +288,56 @@
     source = jnp.where(within[None, :] < count[:, None], first_row[:, None] + within[None, :], -1)
     send = (source.reshape(-1)[:, None] == row_ids[None, :]).astype(BF16)
 
-    message = call(
-        forward_body, shape((4, W_ROWS + REST, LANES)), [VMEM, VMEM], name="forward"
-    )(got, labels)
-    mid = exchange(message, "user", FIRST)
-    w_own = exchange(copies(mid[:, :W_ROWS], 4), "user", SECOND).reshape(8, 2 * W_ROWS, LANES)
-    w_other = lax.ppermute(w_own, "user", PARTNER)
-    rest_own = exchange(copies(mid[:, W_ROWS:], 4), "user", SECOND).reshape(16, REST, LANES)
-    rest_other = lax.ppermute(rest_own, "user", PARTNER)
-
     normed = layer_norm(tokens.astype(F32), in_gain).astype(BF16)
     at = jnp.arange(WIDTH, dtype=jnp.int32)
     wanted = (at % 512) // 32 * 64 + at // 512 * 32 + at % 32
     order = (at[:, None] == wanted[None, :]).astype(BF16)
     normed = jnp.dot(normed, order, preferred_element_type=F32).astype(BF16)
-    layer_half = call(
-        half_body, (shape((ROWS, 256)), shape((ROWS, 256), F32)), [VMEM] * 3, name="half"
-    )
-    u_own, mixed_own = layer_half(normed, w_own, first)
-    u_other, mixed_other = layer_half(normed, w_other, first)
-    gain = jnp.where(core == 0, out_gain, jnp.roll(out_gain, 256))[None]
-    home_out, parcels = call(
-        out_body, (shape((ROWS, WIDTH)), shape((ROWS, WIDTH))), [VMEM] * 9, name="layer_out"
-    )(tokens, u_own, mixed_own, rest_own, u_other, mixed_other, rest_other, gain, send)
-    arrived = exchange(parcels.reshape(USERS, MOST, WIDTH), "user").reshape(ROWS, WIDTH)
-
-    near, far = rest_own[:, 192, :], rest_other[:, 192, :]
-    mine = (jnp.arange(LANES, dtype=jnp.int32)[None, :] == user).astype(F32)
-    mine_count = (jnp.arange(LANES, dtype=jnp.int32)[None, :] == user + USERS).astype(F32)
-
-    def by_user(select):
-        a = jnp.sum(near.astype(F32) * select, axis=1)
-        b = jnp.sum(far.astype(F32) * select, axis=1)
-        even = jnp.where(core == 0, a, b).reshape(4, 4).T
-        uneven = jnp.where(core == 0, b, a).reshape(4, 4)
-        return jnp.stack([even, uneven], axis=2).reshape(USERS).astype(jnp.int32)
-
-    lower, arrived_count = by_user(mine), by_user(mine_count)
-    lands = jnp.where(within[None, :] < arrived_count[:, None], lower[:, None] + within[None, :], -1)
-    receive = (jnp.arange(256, dtype=jnp.int32)[:, None] == lands.reshape(-1)[None, :]).astype(BF16)
-    layer_out = jnp.dot(receive, arrived, preferred_element_type=F32).astype(BF16)
+    got, normed, first, labels = lax.optimization_barrier((got, normed, first, labels))
+
+    message = call(forward_body, shape((4, W_ROWS + REST, LANES)), [VMEM, VMEM])(got, labels)
+    mid = exchange(message, "user", FIRST)
+    mid = mid.reshape(4 * (W_ROWS + REST), LANES)
+    held = exchange(copies(mid, 4), "user", SECOND).reshape(PLANE, W_ROWS + REST, LANES)
 
     table_f = table.astype(F32)
     table_scale = lax.rsqrt(jnp.mean(table_f * table_f, axis=1, keepdims=True) + scale_epsilon)
     table_hat = table_f * table_scale
     table_low = table_hat.astype(BF16)
     positive_local = (positives - item * item_rows)[:, None]
+    owned_ids = lax.dynamic_slice_in_dim(negatives, item * 16, 16, 1) - item * item_rows
+    hits = (
+        owned_ids.reshape(-1)[:, None] == jnp.arange(item_rows, dtype=jnp.int32)[None, :]
+    ).astype(BF16)
+    hat_part = lax.dynamic_slice_in_dim(table_hat, user * 32, 32, 1).T
+    table_scale = table_scale.reshape(1, item_rows)
+    gain = jnp.where(core == 0, out_gain, jnp.roll(out_gain, 256))[None]
+    held, send, positive_local, weight, table_low, table_scale, hits, hat_part, gain = (
+        lax.optimization_barrier(
+            (held, send, positive_local, weight, table_low, table_scale, hits, hat_part, gain)
+        )
+    )
+    held_other = lax.ppermute(held, "user", PARTNER)
+
+    layer_half = call(
+        half_body,
+        (
+            shape((ROWS, 256)),
+            shape((ROWS, 256), F32),
+            shape((256, WIDTH)),
+            shape((256, 512)),
+            shape((PLANE, LANES), F32),
+        ),
+        [VMEM] * 3,
+        mib=12,
+    )
+    u_own, mixed_own, o_own, g_own, near = layer_half(normed, held, first)
+    u_other, mixed_other, o_other, g_other, far = layer_half(normed, held_other, first)
+    home_out, parcels = call(
+        out_body, (shape((ROWS, WIDTH)), shape((ROWS, WIDTH))), [VMEM] * 9, mib=12
+    )(tokens, u_own, mixed_own, o_own, u_other, mixed_other, o_other, gain, send)
+    arrived = exchange(parcels.reshape(USERS, MOST, WIDTH), "user").reshape(ROWS, WIDTH)
+
     token_grad, own, sent, own_inner = call(
         loss_body,
         (
@@ -340,25 +348,35 @@
         ),
         [SMEM] + [VMEM] * 6,
         scratch=[pltpu.VMEM((PLANE, 2, 32, ROWS), BF16)],
-        name="loss",
-    )(core.reshape(1), home_out, table_low, rest_own, rest_other, positive_local, weight)
+        mib=16,
+    )(core.reshape(1), home_out, table_low, g_own, g_other, positive_local, weight)
     partner_terms = lax.ppermute(sent, "user", PARTNER)
-    pair = call(pair_body, shape((PLANE, 48, ROWS)), [VMEM] * 3, name="pair")(
-        own, own_inner, partner_terms
-    )
+    pair = call(pair_body, shape((PLANE, 48, ROWS)), [VMEM] * 3)(own, own_inner, partner_terms)
+    pair, arrived = lax.optimization_barrier((pair, arrived))
     plane = exchange(pair, "user", SAME_CORE)
+
+    mine = (jnp.arange(LANES, dtype=jnp.int32)[None, :] == user).astype(F32)
+    mine_count = (jnp.arange(LANES, dtype=jnp.int32)[None, :] == user + USERS).astype(F32)
+
+    def by_user(select):
+        a = jnp.sum(near * select, axis=1)
+        b = jnp.sum(far * select, axis=1)
+        even = jnp.where(core == 0, a, b).reshape(4, 4).T
+        uneven = jnp.where(core == 0, b, a).reshape(4, 4)
+        return jnp.stack([even, uneven], axis=2).reshape(USERS).astype(jnp.int32)
+
+    lower, arrived_count = by_user(mine), by_user(mine_count)
+    lands = jnp.where(within[None, :] < arrived_count[:, None], lower[:, None] + within[None, :], -1)
+    receive = (jnp.arange(256, dtype=jnp.int32)[:, None] == lands.reshape(-1)[None, :]).astype(BF16)
+    layer_out = jnp.dot(receive, arrived, preferred_element_type=F32).astype(BF16)
+
     positive_part, negative_part = call(
-        plane_body, (shape((256, LANES), F32), shape((256, LANES))), [VMEM], name="plane"
+        plane_body, (shape((48, 256), F32), shape((256, LANES))), [VMEM]
     )(plane)
     owned = exchange(negative_part.reshape(ITEMS, 16, LANES), "item").reshape(256, LANES)
-    owned_ids = lax.dynamic_slice_in_dim(negatives, item * 16, 16, 1) - item * item_rows
-    hits = (
-        jnp.arange(item_rows, dtype=jnp.int32)[:, None] == owned_ids.reshape(-1)[None, :]
-    ).astype(BF16)
-    hat_part = lax.dynamic_slice_in_dim(table_hat, user * 32, 32, 1)
-    item_grad = call(item_body, shape((256, 32), F32), [VMEM] * 5, name="item_grad")(
+    item_grad = call(item_body, shape((32, 256), F32), [VMEM] * 5)(
         positive_part, hits, owned, hat_part, table_scale
-    )
+    ).T
     return (layer_out, token_grad, item_grad)
 
 

time: 196 us -> 152 us (0.78)
  Pallas kernels: 28.3 us -> 14.1 us
  blocking collectives: 12.3 us -> 0 us
  local copies, waits for them, and re-layouts: 18.2 us -> 10.2 us
  waiting for transfers between devices: 63.4 us -> 57 us
  starting transfers between devices: 53.5 us -> 50.1 us
    all_to_all x1 -> x0, blocking collectives: 12.3 us -> none  [exchange(): lax.all_to_all(blocks, axis, 0, 0, tiled=True, axis_index_groups=groups)]
    pallas_call x6, Pallas kernels: 17.6 us -> 7.85 us  [the longest x1 2.14 us: per_device(): layer_half(normed, held_other, first)]
    all_to_all x6, waiting for transfers between devices: 61.2 us -> 54.4 us  [exchange(): lax.all_to_all(blocks, axis, 0, 0, tiled=True, axis_index_groups=groups)]
    ppermute x2 -> x1, starting transfers between devices: 13.1 us -> 9.91 us  [per_device(): held_other = lax.ppermute(held, 'user', PARTNER)]
    pallas_call x1, Pallas kernels: 4.87 us -> 2.59 us  [per_device(): call(out_body, (shape((ROWS, WIDTH)), shape((ROWS, WIDTH))), [VMEM] * 9,...]
    pallas_call x1, Pallas kernels: 5.9 us -> 3.64 us  [per_device(): call(loss_body, (shape((ROWS, WIDTH)), shape((PLANE, 32, ROWS)), shape((5...]
    unnamed x36 -> x40, local copies, waits for them, and re-layouts: 5.92 us -> 3.72 us
  transfers between devices with their start and end apart: 9 -> 8, of which waited for: 7 -> 8; matrix products, arithmetic and copies ran while one was open for 12% -> 13% of each run, Pallas kernels for 6% -> 5%
where the time goes in v2:
time: 152 us; the launch traced here: 150 us
  waiting for transfers between devices  57 us (38%)
  starting transfers between devices  50.1 us (33%)
  Pallas kernels  14.1 us (9%)
  other arithmetic  11.7 us (8%)
  local copies, waits for them, and re-layouts  10.2 us (7%)
  matrix products  6.02 us (4%)
    all_to_all x6, waiting for transfers between devices, exchange(): lax.all_to_all(blocks, axis, 0, 0, tiled=True, axis_index_groups=groups)  54.4 us
    all_to_all x6, starting transfers between devices, exchange(): lax.all_to_all(blocks, axis, 0, 0, tiled=True, axis_index_groups=groups)  37.7 us
    ppermute x1, starting transfers between devices, per_device(): held_other = lax.ppermute(held, 'user', PARTNER)  9.91 us
    unnamed x40, local copies, waits for them, and re-layouts  3.72 us
    pallas_call x1, Pallas kernels, per_device(): call(loss_body, (shape((ROWS, WIDTH)), shape((PLANE, 32, ROWS)), shape((5...  3.64 us
  transfers between devices with their start and end apart: 8, of which 8 were waited for; matrix products, arithmetic and copies ran while one was open for 13% of the time, Pallas kernels for 5%

profile of v2, /device:TPU:1, one launch (start us, length us, event | category | flops | bytes accessed | tf_op | source)
XLA Modules:
  0.0 150.2 jit_solution(16972128458352358105)
XLA Ops:
  0.8 0.7 copy-done
  1.6 0.9 subtract_reduce_fusion
  2.5 1.1 fusion.16
  3.7 0.7 dynamic_slice.18
  4.6 0.7 fusion.19
  5.3 15.7 %all-to-all-start = ((bf16[16,56,128]{2,1,0:T(8,128)(2,1)}), bf16[16,56,128]{2,1,0:T(8,128)(2,1)S(1)}, u32[]{:S(2)}, u32[]{:S(2)}) async-start(bf16[16,56,128]{2,1,0:T(8,128)(2,1)} %fusion.19), calls=%async_computation | async-start | bytes 458752 | tf_op jit(solution)/shard_map/all_to_all | solution.py:224
  21.0 0.7 copy.47
  21.9 0.7 fusion.46
  23.2 0.2 convert_reduce_fusion
  23.4 0.4 fusion.3
  24.1 2.4 %fusion.7.x_ref = bf16[512,1024]{1,0:T(8,128)(2,1)} fusion(s32[1024]{0:T(1024)S(1)} %fusion.37, bf16[512,1024]{1,0:T(8,128)(2,1)S(1)} %copy-done.1, f32[1024]{0:T(1024)S(1)} %copy-done.18, f32[512]{0:T(512)S(1)} %add_rsqrt_fusion, f32[512]{0:T(512)S(1)} %broadcast_multiply_fusion), kind=kOutput, calls=%fused_computation.10 | convolution fusion | flops 1077936128 | bytes 2109440 | tf_op jit(solution)/shard_map/dot_general | solution.py:295
  26.5 7.2 %all-to-all-done.got = bf16[16,56,128]{2,1,0:T(8,128)(2,1)S(1)} async-done(((bf16[16,56,128]{2,1,0:T(8,128)(2,1)}), bf16[16,56,128]{2,1,0:T(8,128)(2,1)S(1)}, u32[]{:S(2)}, u32[]{:S(2)}) %all-to-all-start) | async-done | bytes 229408 | tf_op jit(solution)/shard_map/all_to_all | solution.py:224
  33.7 1.0 shard_map.130
  34.7 4.2 %all-to-all-start.1 = ((bf16[4,720,128]{2,1,0:T(8,128)(2,1)}), bf16[4,720,128]{2,1,0:T(8,128)(2,1)S(1)}, u32[]{:S(2)}, u32[]{:S(2)}) async-start(bf16[4,720,128]{2,1,0:T(8,128)(2,1)} %shard_map.130), calls=%async_computation.1 | async-start | bytes 1474560 | tf_op jit(solution)/shard_map/all_to_all | solution.py:224
  38.9 1.0 copy.51
  40.0 0.7 eq.143
  40.6 6.3 %all-to-all-done.1 = bf16[4,720,128]{2,1,0:T(8,128)(2,1)S(1)} async-done(((bf16[4,720,128]{2,1,0:T(8,128)(2,1)}), bf16[4,720,128]{2,1,0:T(8,128)(2,1)S(1)}, u32[]{:S(2)}, u32[]{:S(2)}) %all-to-all-start.1) | async-done | bytes 737312 | tf_op jit(solution)/shard_map/all_to_all | solution.py:224
  47.0 2.0 %broadcast_in_dim.45 = bf16[4,2880,128]{2,1,0:T(8,128)(2,1)} broadcast(bf16[2880,128]{1,0:T(8,128)(2,1)S(1)} %bitcast.34), dimensions={1,2} | broadcast | bytes 3686400 | tf_op jit(solution)/shard_map/broadcast_in_dim | solution.py:220
  48.9 3.9 %all-to-all-start.2 = ((bf16[4,2880,128]{2,1,0:T(8,128)(2,1)}), bf16[4,2880,128]{2,1,0:T(8,128)(2,1)S(1)}, u32[]{:S(2)}, u32[]{:S(2)}) async-start(bf16[4,2880,128]{2,1,0:T(8,128)(2,1)} %broadcast_in_dim.45), calls=%async_computation.2 | async-start | bytes 5898240 | tf_op jit(solution)/shard_map/all_to_all | solution.py:224
  53.0 1.2 fusion.8
  54.2 1.9 %convert_multiply_fusion = (f32[256,1024]{0,1:T(8,128)S(1)}, bf16[256,1024]{0,1:T(8,128)(2,1)}) fusion(bf16[256,1024]{0,1:T(8,128)(2,1)} %copy.51, f32[256]{0:T(256)S(1)} %add_rsqrt_fusion.1), kind=kLoop, calls=%fused_computation.11 | loop fusion | flops 786432 | bytes 2098176 | tf_op jit(solution)/shard_map/mul | solution.py:305
  56.2 0.6 dynamic-slice_bitcast_fusion.hat_ref
  56.8 0.7 reshape_select_fusion.weight_ref
  57.6 1.3 broadcast_subtract_fusion
  58.8 1.4 fusion.18.hits_ref
  60.3 0.9 fusion.13.send_ref
  61.2 11.9 %all-to-all-done.2 = bf16[4,2880,128]{2,1,0:T(8,128)(2,1)S(1)} async-done(((bf16[4,2880,128]{2,1,0:T(8,128)(2,1)}), bf16[4,2880,128]{2,1,0:T(8,128)(2,1)S(1)}, u32[]{:S(2)}, u32[]{:S(2)}) %all-to-all-start.2) | async-done | bytes 2949152 | tf_op jit(solution)/shard_map/all_to_all | solution.py:224
  73.1 9.9 %collective-permute-start = (bf16[16,720,128]{2,1,0:T(8,128)(2,1)S(1)}, bf16[16,720,128]{2,1,0:T(8,128)(2,1)S(1)}, u32[]{:S(2)}, u32[]{:S(2)}) collective-permute-start(bf16[16,720,128]{2,1,0:T(8,128)(2,1)S(1)} %bitcast.29), channel_id=1, source_target_pairs={{0,16},{16,0},{32,48},{48,32},{64,80},{80,64},{96,112},{112,96},{1... | collective-permute-start | bytes 8847368 | tf_op jit(solution)/shard_map/ppermute | solution.py:320
  83.0 1.2 copy-done.3
  84.2 2.1 %shard_map.131 = (bf16[512,256]{1,0:T(8,128)(2,1)S(1)}, f32[512,256]{1,0:T(8,128)S(1)}, bf16[256,1024]{1,0:T(8,128)(2,1)S(1)}, bf16[256,512]{1,0:T(8,128)(2,1)S(1)}, f32[16,128]{1,0:T(8,128)S(1)}) custom-call(bf16[512,1024]{1,0:T(8,128)(2,1)S(1)} %copy-done.3, bf16[16,720,128]{2,1,0:T(8,128)(2,1)S(1)} %bitcast.30, s32[512,1]{1,0:T(8,128)S(1)} %reshape_select_fusion.1.first_ref), custom_call_target="tpu_custom_call" | custom-call | tf_op jit(solution)/shard_map/pallas_call | solution.py:334
  86.4 0.7 copy-done.6
  87.1 0.9 collective-permute-done.w_ref
  88.0 2.1 %shard_map.132 = (bf16[512,256]{1,0:T(8,128)(2,1)S(1)}, f32[512,256]{1,0:T(8,128)S(1)}, bf16[256,1024]{1,0:T(8,128)(2,1)S(1)}, bf16[256,512]{1,0:T(8,128)(2,1)S(1)}, f32[16,128]{1,0:T(8,128)S(1)}) custom-call(bf16[512,1024]{1,0:T(8,128)(2,1)S(1)} %copy-done.3, bf16[16,720,128]{2,1,0:T(8,128)(2,1)S(1)} %collective-permute-done.w_ref, ...), custom_call_target="tpu_custom_call" | custom-call | tf_op jit(solution)/shard_map/pallas_call | solution.py:335
  90.1 2.6 %shard_map.133 = (bf16[512,1024]{1,0:T(8,128)(2,1)S(1)}, bf16[512,1024]{1,0:T(8,128)(2,1)}) custom-call(bf16[512,1024]{1,0:T(8,128)(2,1)S(1)} %copy-done.2, bf16[512,256]{1,0:T(8,128)(2,1)S(1)} %get-tuple-element.43.u0, f32[512,256]{1,0:T(8,128)S(1)} %get-tuple-element.44.m0, bf16[256,1024]{1,0:T(8,128)(2,1)S(1)} %get-tuple-element.45.o0, ...), custom_call_target="tpu_custom_call" | custom-call | tf_op jit(solution)/shard_map/pallas_call | solution.py:336
  92.7 4.8 %all-to-all-start.3 = ((bf16[32,16,1024]{2,1,0:T(8,128)(2,1)}), bf16[32,16,1024]{2,1,0:T(8,128)(2,1)}, u32[]{:S(2)}, u32[]{:S(2)}) async-start(bf16[32,16,1024]{2,1,0:T(8,128)(2,1)} %bitcast.17), calls=%async_computation.3 | async-start | bytes 2097152 | tf_op jit(solution)/shard_map/all_to_all | solution.py:224
  97.5 0.2 copy.56.low_ref
  97.9 3.6 %shard_map.134 = (bf16[512,1024]{1,0:T(8,128)(2,1)}, bf16[16,32,512]{2,1,0:T(8,128)(2,1)S(1)}, bf16[528,512]{1,0:T(8,128)(2,1)}, f32[1,512]{1,0:T(1,128)S(1)}) custom-call(s32[1]{0:T(128)} %bitcast.16.core, bf16[512,1024]{1,0:T(8,128)(2,1)S(1)} %get-tuple-element.51.out_ref, bf16[256,1024]{1,0:T(8,128)(2,1)S(1)} %copy.56.low_ref, ...), custom_call_target="tpu_custom_call" | custom-call | tf_op jit(solution)/shard_map/pallas_call | solution.py:341
  101.6 2.5 %collective-permute-start.1 = (bf16[528,512]{1,0:T(8,128)(2,1)}, bf16[528,512]{1,0:T(8,128)(2,1)S(1)}, u32[]{:S(2)}, u32[]{:S(2)}) collective-permute-start(bf16[528,512]{1,0:T(8,128)(2,1)} %get-tuple-element.59), channel_id=1, source_target_pairs={{0,16},{16,0},{32,48},{48,32},{64,80},{80,64},{96,112},{112,96},{1... | collective-permute-start | bytes 1622024 | tf_op jit(solution)/shard_map/ppermute | solution.py:353
  104.1 1.7 %collective-permute-done.1.got_ref = bf16[528,512]{1,0:T(8,128)(2,1)S(1)} collective-permute-done((bf16[528,512]{1,0:T(8,128)(2,1)}, bf16[528,512]{1,0:T(8,128)(2,1)S(1)}, u32[]{:S(2)}, u32[]{:S(2)}) %collective-permute-start.1) | collective-permute-done | bytes 540704 | tf_op jit(solution)/shard_map/ppermute | solution.py:353
  105.8 1.0 shard_map.135
  106.8 7.7 %all-to-all-done.3 = bf16[32,16,1024]{2,1,0:T(8,128)(2,1)} async-done(((bf16[32,16,1024]{2,1,0:T(8,128)(2,1)}), bf16[32,16,1024]{2,1,0:T(8,128)(2,1)}, u32[]{:S(2)}, u32[]{:S(2)}) %all-to-all-start.3) | async-done | bytes 1048608 | tf_op jit(solution)/shard_map/all_to_all | solution.py:224
  114.5 3.7 %all-to-all-start.4 = ((bf16[16,48,512]{2,1,0:T(8,128)(2,1)}), bf16[16,48,512]{2,1,0:T(8,128)(2,1)S(1)}, u32[]{:S(2)}, u32[]{:S(2)}) async-start(bf16[16,48,512]{2,1,0:T(8,128)(2,1)} %shard_map.135), calls=%async_computation.4 | async-start | bytes 1572864 | tf_op jit(solution)/shard_map/all_to_all | solution.py:224
  119.6 12.1 %all-to-all-done.4.got_ref = bf16[16,48,512]{2,1,0:T(8,128)(2,1)S(1)} async-done(((bf16[16,48,512]{2,1,0:T(8,128)(2,1)}), bf16[16,48,512]{2,1,0:T(8,128)(2,1)S(1)}, u32[]{:S(2)}, u32[]{:S(2)}) %all-to-all-start.4) | async-done | bytes 786464 | tf_op jit(solution)/shard_map/all_to_all | solution.py:224
  131.7 0.8 shard_map.136
  132.4 5.3 %all-to-all-start.5 = ((bf16[16,16,128]{2,1,0:T(8,128)(2,1)}), bf16[16,16,128]{2,1,0:T(8,128)(2,1)S(1)}, u32[]{:S(2)}, u32[]{:S(2)}) async-start(bf16[16,16,128]{2,1,0:T(8,128)(2,1)} %bitcast.19), calls=%async_computation.5 | async-start | bytes 131072 | tf_op jit(solution)/shard_map/all_to_all | solution.py:224
  137.7 2.5 %convolution_convert_fusion = bf16[256,1024]{1,0:T(8,128)(2,1)} fusion(bf16[512,1024]{1,0:T(8,128)(2,1)} %bitcast.18, s32[512]{0:T(512)S(1)} %select_n.252), kind=kOutput, calls=%fused_computation.13 | convolution fusion | flops 268828672 | bytes 1574912 | tf_op jit(solution)/shard_map/dot_general | solution.py:371
  140.2 9.2 %all-to-all-done.5 = bf16[16,16,128]{2,1,0:T(8,128)(2,1)S(1)} async-done(((bf16[16,16,128]{2,1,0:T(8,128)(2,1)}), bf16[16,16,128]{2,1,0:T(8,128)(2,1)S(1)}, u32[]{:S(2)}, u32[]{:S(2)}) %all-to-all-start.5) | async-done | bytes 65568 | tf_op jit(solution)/shard_map/all_to_all | solution.py:224
  149.4 0.8 shard_map.137
  (81 shorter events, 3.0 us)
Async XLA Ops:
  0.6 0.8 copy-start
  0.6 22.3 %copy-start.15 = (s32[1,32]{1,0:T(1,128)S(1)}, s32[1,32]{1,0:T(1,128)}, u32[]{:S(2)}) copy-start(s32[1,32]{1,0:T(1,128)} %param.12) | copy-start | bytes 388
  0.7 22.3 %copy-start.16 = (s32[1,32]{1,0:T(1,128)S(1)}, s32[1,32]{1,0:T(1,128)}, u32[]{:S(2)}) copy-start(s32[1,32]{1,0:T(1,128)} %param.13) | copy-start | bytes 388
  0.7 22.3 %copy-start.17 = (s32[1,32]{1,0:T(1,128)S(1)}, s32[1,32]{1,0:T(1,128)}, u32[]{:S(2)}) copy-start(s32[1,32]{1,0:T(1,128)} %param.14) | copy-start | bytes 388
  0.7 22.5 %copy-start.1 = (bf16[512,1024]{1,0:T(8,128)(2,1)S(1)}, bf16[512,1024]{1,0:T(8,128)(2,1)}, u32[]{:S(2)}) copy-start(bf16[512,1024]{1,0:T(8,128)(2,1)} %tok_ref.1) | copy-start | bytes 3145732
  3.7 20.4 %copy-start.18 = (f32[1024]{0:T(1024)S(1)}, f32[1024]{0:T(1024)}, u32[]{:S(2)}) copy-start(f32[1024]{0:T(1024)} %param.18) | copy-start | bytes 12292
  5.3 28.4 %all-to-all-start = ((bf16[16,56,128]{2,1,0:T(8,128)(2,1)}), bf16[16,56,128]{2,1,0:T(8,128)(2,1)S(1)}, u32[]{:S(2)}, u32[]{:S(2)}) async-start(bf16[16,56,128]{2,1,0:T(8,128)(2,1)} %fusion.19), calls=%async_computation | async-start | bytes 458752 | tf_op jit(solution)/shard_map/all_to_all | solution.py:224
  22.7 1.4 copy-start.14
  26.5 12.4 %copy-start.10 = (bf16[256,1024]{1,0:T(8,128)(2,1)S(1)}, bf16[256,1024]{1,0:T(8,128)(2,1)}, u32[]{:S(2)}) copy-start(bf16[256,1024]{1,0:T(8,128)(2,1)} %param.17) | copy-start | bytes 1572868
  26.5 13.4 %copy-start.11 = (s32[16,256]{1,0:T(8,128)S(1)}, s32[16,256]{1,0:T(8,128)}, u32[]{:S(2)}) copy-start(s32[16,256]{1,0:T(8,128)} %param.16) | copy-start | bytes 49156
  34.7 12.3 %all-to-all-start.1 = ((bf16[4,720,128]{2,1,0:T(8,128)(2,1)}), bf16[4,720,128]{2,1,0:T(8,128)(2,1)S(1)}, u32[]{:S(2)}, u32[]{:S(2)}) async-start(bf16[4,720,128]{2,1,0:T(8,128)(2,1)} %shard_map.130), calls=%async_computation.1 | async-start | bytes 1474560 | tf_op jit(solution)/shard_map/all_to_all | solution.py:224
  48.9 24.1 %all-to-all-start.2 = ((bf16[4,2880,128]{2,1,0:T(8,128)(2,1)}), bf16[4,2880,128]{2,1,0:T(8,128)(2,1)S(1)}, u32[]{:S(2)}, u32[]{:S(2)}) async-start(bf16[4,2880,128]{2,1,0:T(8,128)(2,1)} %broadcast_in_dim.45), calls=%async_computation.2 | async-start | bytes 5898240 | tf_op jit(solution)/shard_map/all_to_all | solution.py:224
  52.9 4.7 %copy-start.13 = (f32[512]{0:T(512)S(1)}, f32[512]{0:T(512)}, u32[]{:S(2)}) copy-start(f32[512]{0:T(512)} %param.20) | copy-start | bytes 6148
  73.1 14.9 %collective-permute-start = (bf16[16,720,128]{2,1,0:T(8,128)(2,1)S(1)}, bf16[16,720,128]{2,1,0:T(8,128)(2,1)S(1)}, u32[]{:S(2)}, u32[]{:S(2)}) collective-permute-start(bf16[16,720,128]{2,1,0:T(8,128)(2,1)S(1)} %bitcast.29), channel_id=1, source_target_pairs={{0,16},{16,0},{32,48},{48,32},{64,80},{80,64},{96,112},{112,96},{1... | collective-permute-start | bytes 8847368 | tf_op jit(solution)/shard_map/ppermute | solution.py:320
  83.0 1.2 copy-start.3
  86.4 0.7 copy-start.6
  87.1 3.1 %copy-start.2 = (bf16[512,1024]{1,0:T(8,128)(2,1)S(1)}, bf16[512,1024]{1,0:T(8,128)(2,1)}, u32[]{:S(2)}) copy-start(bf16[512,1024]{1,0:T(8,128)(2,1)} %tok_ref.1) | copy-start | bytes 3145732
  87.1 3.1 %copy-start.4 = (bf16[512,512]{1,0:T(8,128)(2,1)S(1)}, bf16[512,512]{1,0:T(8,128)(2,1)}, u32[]{:S(2)}) copy-start(bf16[512,512]{1,0:T(8,128)(2,1)} %fusion.13.send_ref) | copy-start | bytes 1572868
  92.7 4.8 %copy-start.9 = (bf16[256,1024]{0,1:T(8,128)(2,1)S(1)}, bf16[256,1024]{0,1:T(8,128)(2,1)}, u32[]{:S(2)}) copy-start(bf16[256,1024]{0,1:T(8,128)(2,1)} %get-tuple-element.52) | copy-start | bytes 1572868
  92.7 5.0 %copy-start.12 = (s32[512]{0:T(512)S(1)}, s32[512]{0:T(512)}, u32[]{:S(2)}) copy-start(s32[512]{0:T(512)} %broadcast_subtract_fusion) | copy-start | bytes 6148
  92.7 5.2 %copy-start.7 = (bf16[256,512]{1,0:T(8,128)(2,1)S(1)}, bf16[256,512]{1,0:T(8,128)(2,1)}, u32[]{:S(2)}) copy-start(bf16[256,512]{1,0:T(8,128)(2,1)} %copy-done.6) | copy-start | bytes 786436
  92.7 21.8 %all-to-all-start.3 = ((bf16[32,16,1024]{2,1,0:T(8,128)(2,1)}), bf16[32,16,1024]{2,1,0:T(8,128)(2,1)}, u32[]{:S(2)}, u32[]{:S(2)}) async-start(bf16[32,16,1024]{2,1,0:T(8,128)(2,1)} %bitcast.17), calls=%async_computation.3 | async-start | bytes 2097152 | tf_op jit(solution)/shard_map/all_to_all | solution.py:224
  101.6 4.2 %collective-permute-start.1 = (bf16[528,512]{1,0:T(8,128)(2,1)}, bf16[528,512]{1,0:T(8,128)(2,1)S(1)}, u32[]{:S(2)}, u32[]{:S(2)}) collective-permute-start(bf16[528,512]{1,0:T(8,128)(2,1)} %get-tuple-element.59), channel_id=1, source_target_pairs={{0,16},{16,0},{32,48},{48,32},{64,80},{80,64},{96,112},{112,96},{1... | collective-permute-start | bytes 1622024 | tf_op jit(solution)/shard_map/ppermute | solution.py:353
  114.5 34.9 %copy-start.5 = (bf16[256,256]{1,0:T(8,128)(2,1)S(1)}, bf16[256,256]{1,0:T(8,128)(2,1)}, u32[]{:S(2)}) copy-start(bf16[256,256]{1,0:T(8,128)(2,1)} %fusion.18.hits_ref) | copy-start | bytes 393220
  114.5 34.9 %copy-start.8 = (f32[32,256]{1,0:T(8,128)S(1)}, f32[32,256]{1,0:T(8,128)}, u32[]{:S(2)}) copy-start(f32[32,256]{1,0:T(8,128)} %dynamic-slice_bitcast_fusion.hat_ref) | copy-start | bytes 98308
  114.5 17.1 %all-to-all-start.4 = ((bf16[16,48,512]{2,1,0:T(8,128)(2,1)}), bf16[16,48,512]{2,1,0:T(8,128)(2,1)S(1)}, u32[]{:S(2)}, u32[]{:S(2)}) async-start(bf16[16,48,512]{2,1,0:T(8,128)(2,1)} %shard_map.135), calls=%async_computation.4 | async-start | bytes 1572864 | tf_op jit(solution)/shard_map/all_to_all | solution.py:224
  132.4 17.0 %all-to-all-start.5 = ((bf16[16,16,128]{2,1,0:T(8,128)(2,1)}), bf16[16,16,128]{2,1,0:T(8,128)(2,1)S(1)}, u32[]{:S(2)}, u32[]{:S(2)}) async-start(bf16[16,16,128]{2,1,0:T(8,128)(2,1)} %bitcast.19), calls=%async_computation.5 | async-start | bytes 131072 | tf_op jit(solution)/shard_map/all_to_all | solution.py:224

commit v3 on v2

--- a/solution.py
+++ b/solution.py
@@ -60,11 +60,15 @@
 def forward_body(got, label, out):
     for i in range(ITEMS):
         out[0, i * 32 : (i + 1) * 32, :] = got[i, 0:32, :]
+    left = lax.broadcasted_iota(jnp.int32, (8, LANES), 1) < 64
     for b in range(8):
-        out[0, W_ROWS + b * 16 : W_ROWS + (b + 1) * 16, :] = (
-            got[2 * b, 32:48, :].astype(F32) + got[2 * b + 1, 32:48, :].astype(F32)
+        even, odd = got[2 * b, 32:40, :].astype(F32), got[2 * b + 1, 32:40, :].astype(F32)
+        top = jnp.where(left, even, pltpu.roll(odd, 64, 1))
+        bottom = jnp.where(left, pltpu.roll(even, 64, 1), odd)
+        out[0, W_ROWS + b * 16 : W_ROWS + (b + 1) * 16, :] = jnp.concatenate(
+            [top, bottom], axis=0
         ).astype(BF16)
-    quads = got[:, 48:56, :].astype(F32)
+    quads = got[:, 40:48, :].astype(F32)
     for b in range(4):
         out[0, W_ROWS + 128 + b * 16 : W_ROWS + 144 + b * 16, :] = quads[:, b, :].astype(BF16)
     out[0, W_ROWS + 192 : W_ROWS + 208, :] = label[...]
@@ -72,8 +76,36 @@
         out[g] = out[0]
 
 
+def project(x, w_ref, q):
+    w = jnp.concatenate(
+        [
+            jnp.concatenate([w_ref[n, :W_ROWS, :], w_ref[n + 1, :W_ROWS, :]], axis=0)
+            for n in (4 * q, 4 * q + 2)
+        ],
+        axis=1,
+    )
+    return jax.nn.silu(dot(x, w)).astype(BF16)
+
+
+def attend(x, w_ref, first, u_ref, mixed_ref):
+    u_ref[...] = project(x, w_ref, 0)
+    v = project(x, w_ref, 1)
+    q = project(x, w_ref, 2)
+    k = project(x, w_ref, 3)
+    for b in range(x.shape[0] // 128):
+        lo, hi = b * 128, (b + 1) * 128
+        at = max(lo - 128, 0)
+        rows = lo + lax.broadcasted_iota(jnp.int32, (128, hi - at), 0)
+        cols = at + lax.broadcasted_iota(jnp.int32, (128, hi - at), 1)
+        allowed = (cols >= first[lo:hi, :]) & (cols <= rows)
+        for h in range(2):
+            d0, d1 = h * HEAD, (h + 1) * HEAD
+            scores = dot(q[lo:hi, d0:d1], k[at:hi, d0:d1], ((1,), (1,))) * HEAD ** (-0.5)
+            weights = jnp.where(allowed, jax.nn.silu(scores), 0.0).astype(BF16)
+            mixed_ref[lo:hi, d0:d1] = dot(weights, v[at:hi, d0:d1])
+
+
 def half_body(x_ref, w_ref, first_ref, u_ref, mixed_ref, o_ref, g_ref, label_ref):
-    x = x_ref[...]
     for n in range(8):
         o_ref[:, n * LANES : (n + 1) * LANES] = w_ref[
             :, W_ROWS + n * 16 : W_ROWS + (n + 1) * 16, :
@@ -84,36 +116,10 @@
         ].reshape(256, LANES)
     for n in range(PLANE):
         label_ref[n : n + 1, :] = w_ref[n, W_ROWS + 192 : W_ROWS + 208, :].astype(F32)[0:1, :]
-
-    def part(q):
-        w = jnp.concatenate(
-            [
-                jnp.concatenate([w_ref[n, :W_ROWS, :], w_ref[n + 1, :W_ROWS, :]], axis=0)
-                for n in (4 * q, 4 * q + 2)
-            ],
-            axis=1,
-        )
-        return jax.nn.silu(dot(x, w)).astype(BF16)
-
-    u_ref[...] = part(0)
-    v = part(1)
-    q = part(2)
-    k = part(3)
-    for b in range(4):
-        lo, hi = b * 128, (b + 1) * 128
-        at = max(lo - 128, 0)
-        rows = lo + lax.broadcasted_iota(jnp.int32, (128, hi - at), 0)
-        cols = at + lax.broadcasted_iota(jnp.int32, (128, hi - at), 1)
-        first = first_ref[lo:hi, :]
-        allowed = (cols >= first) & (cols <= rows)
-        for h in range(2):
-            d0, d1 = h * HEAD, (h + 1) * HEAD
-            scores = dot(q[lo:hi, d0:d1], k[at:hi, d0:d1], ((1,), (1,))) * HEAD ** (-0.5)
-            weights = jnp.where(allowed, jax.nn.silu(scores), 0.0).astype(BF16)
-            mixed_ref[lo:hi, d0:d1] = dot(weights, v[at:hi, d0:d1])
-
-
-def out_body(tok_ref, u0, m0, o0, u1, m1, o1, gain_ref, send_ref, out_ref, parcel_ref):
+    attend(x_ref[...], w_ref, first_ref[...], u_ref, mixed_ref)
+
+
+def gated_out(rows, u0, m0, o0, u1, m1, o1, gain_ref):
     a, b = m0[...], m1[...]
     width = 512.0
     center = (jnp.sum(a, axis=1, keepdims=True) + jnp.sum(b, axis=1, keepdims=True)) / width
@@ -124,11 +130,26 @@
     inv = lax.rsqrt(spread + norm_epsilon)
     ga = (a * inv * gain_ref[:, 0:256] * u0[...].astype(F32)).astype(BF16)
     gb = (b * inv * gain_ref[:, 256:512] * u1[...].astype(F32)).astype(BF16)
-
     delta = dot(ga, o0[...]) + dot(gb, o1[...])
-    out = (tok_ref[...].astype(F32) + delta).astype(BF16)
-    out_ref[...] = out
-    parcel_ref[...] = dot(send_ref[...], out).astype(BF16)
+    return (rows.astype(F32) + delta).astype(BF16)
+
+
+def out_body(tok_ref, u0, m0, o0, u1, m1, o1, gain_ref, out_ref):
+    out_ref[...] = gated_out(tok_ref[...], u0, m0, o0, u1, m1, o1, gain_ref)
+
+
+def worker_body(
+    lands, lowers, got_ref, order_ref, in_gain, w0, w1, o0, o1, gain_ref, out_ref, u0, u1, m0, m1
+):
+    at = lax.broadcasted_iota(jnp.int32, (256, ROWS), 0)
+    here = at == lands[...]
+    first = jnp.sum(jnp.where(here, lowers[...], 0.0), axis=1, keepdims=True).astype(jnp.int32)
+    rows = dot(jnp.where(here, 1.0, 0.0).astype(BF16), got_ref[...]).astype(BF16)
+    normed = layer_norm(rows.astype(F32), in_gain[...]).astype(BF16)
+    x = dot(normed, order_ref[...]).astype(BF16)
+    attend(x, w0, first, u0, m0)
+    attend(x, w1, first, u1, m1)
+    out_ref[...] = gated_out(rows, u0, m0, o0, u1, m1, o1, gain_ref)
 
 
 def loss_body(core, out_ref, low_ref, g0_ref, g1_ref, pos_ref, weight_ref, grad_ref, own_ref, send_ref, own_inner, terms):
@@ -188,7 +209,7 @@
     for k in range(PLANE):
         mine = own_ref[k].astype(F32) + got_ref[k * 32 : (k + 1) * 32, :].astype(F32)
         out_ref[k, 0:32, :] = mine.astype(BF16)
-        out_ref[k, 32:48, :] = tail
+        out_ref[k, 32:40, :] = tail[0:8, :]
 
 
 def plane_body(got_ref, pos_ref, neg_ref):
@@ -247,11 +268,7 @@
     block = (chunk // 2) * 4 + core * 2 + chunk % 2
     w_part = lax.dynamic_slice(w_uvqk, (half * 32, block * LANES), (32, LANES))
     o_part = lax.dynamic_slice(w_out, (core * 256 + place * 16, 0), (16, 64))
-    blank = jnp.zeros_like(o_part)
-    odd = item % 2 == 1
-    o_part = jnp.concatenate(
-        [jnp.where(odd, blank, o_part), jnp.where(odd, o_part, blank)], axis=1
-    )
+    o_part = jnp.concatenate([o_part[:8], o_part[8:]], axis=1)
     ids = lax.dynamic_slice(negatives, (0, item * 16 + place), (ITEMS, 1)) - item * item_rows
     pick = (ids == jnp.arange(item_rows, dtype=jnp.int32)[None, :]).astype(BF16)
     g_part = jnp.dot(pick, lax.dynamic_slice(table, (0, core * 512), (item_rows, 512)))
@@ -293,6 +310,7 @@
     wanted = (at % 512) // 32 * 64 + at // 512 * 32 + at % 32
     order = (at[:, None] == wanted[None, :]).astype(BF16)
     normed = jnp.dot(normed, order, preferred_element_type=F32).astype(BF16)
+    parcels = jnp.dot(send, tokens, preferred_element_type=F32).astype(BF16)
     got, normed, first, labels = lax.optimization_barrier((got, normed, first, labels))
 
     message = call(forward_body, shape((4, W_ROWS + REST, LANES)), [VMEM, VMEM])(got, labels)
@@ -312,12 +330,24 @@
     hat_part = lax.dynamic_slice_in_dim(table_hat, user * 32, 32, 1).T
     table_scale = table_scale.reshape(1, item_rows)
     gain = jnp.where(core == 0, out_gain, jnp.roll(out_gain, 256))[None]
-    held, send, positive_local, weight, table_low, table_scale, hits, hat_part, gain = (
+    held, parcels, order, positive_local, weight, table_low, table_scale, hits, hat_part, gain = (
         lax.optimization_barrier(
-            (held, send, positive_local, weight, table_low, table_scale, hits, hat_part, gain)
+            (
+                held,
+                parcels,
+                order,
+                positive_local,
+                weight,
+                table_low,
+                table_scale,
+                hits,
+                hat_part,
+                gain,
+            )
         )
     )
     held_other = lax.ppermute(held, "user", PARTNER)
+    arrived = exchange(parcels.reshape(USERS, MOST, WIDTH), "user").reshape(ROWS, WIDTH)
 
     layer_half = call(
         half_body,
@@ -333,10 +363,9 @@
     )
     u_own, mixed_own, o_own, g_own, near = layer_half(normed, held, first)
     u_other, mixed_other, o_other, g_other, far = layer_half(normed, held_other, first)
-    home_out, parcels = call(
-        out_body, (shape((ROWS, WIDTH)), shape((ROWS, WIDTH))), [VMEM] * 9, mib=12
-    )(tokens, u_own, mixed_own, o_own, u_other, mixed_other, o_other, gain, send)
-    arrived = exchange(parcels.reshape(USERS, MOST, WIDTH), "user").reshape(ROWS, WIDTH)
+    home_out = call(out_body, shape((ROWS, WIDTH)), [VMEM] * 8, mib=8)(
+        tokens, u_own, mixed_own, o_own, u_other, mixed_other, o_other, gain
+    )
 
     token_grad, own, sent, own_inner = call(
         loss_body,
@@ -351,7 +380,7 @@
         mib=16,
     )(core.reshape(1), home_out, table_low, g_own, g_other, positive_local, weight)
     partner_terms = lax.ppermute(sent, "user", PARTNER)
-    pair = call(pair_body, shape((PLANE, 48, ROWS)), [VMEM] * 3)(own, own_inner, partner_terms)
+    pair = call(pair_body, shape((PLANE, 40, ROWS)), [VMEM] * 3)(own, own_inner, partner_terms)
     pair, arrived = lax.optimization_barrier((pair, arrived))
     plane = exchange(pair, "user", SAME_CORE)
 
@@ -367,8 +396,30 @@
 
     lower, arrived_count = by_user(mine), by_user(mine_count)
     lands = jnp.where(within[None, :] < arrived_count[:, None], lower[:, None] + within[None, :], -1)
-    receive = (jnp.arange(256, dtype=jnp.int32)[:, None] == lands.reshape(-1)[None, :]).astype(BF16)
-    layer_out = jnp.dot(receive, arrived, preferred_element_type=F32).astype(BF16)
+    lowers = jnp.broadcast_to(lower[:, None], (USERS, MOST)).astype(F32)
+    layer_out = call(
+        worker_body,
+        shape((256, WIDTH)),
+        [VMEM] * 10,
+        scratch=[
+            pltpu.VMEM((256, 256), BF16),
+            pltpu.VMEM((256, 256), BF16),
+            pltpu.VMEM((256, 256), F32),
+            pltpu.VMEM((256, 256), F32),
+        ],
+        mib=12,
+    )(
+        lands.reshape(1, ROWS),
+        lowers.reshape(1, ROWS),
+        arrived,
+        order,
+        in_gain[None],
+        held,
+        held_other,
+        o_own,
+        o_other,
+        gain,
+    )
 
     positive_part, negative_part = call(
         plane_body, (shape((48, 256), F32), shape((256, LANES))), [VMEM]

time: 152 us -> 157 us (1.033)
  waiting for transfers between devices: 57 us -> 40.2 us
  local copies, waits for them, and re-layouts: 10.2 us -> 23 us
  Pallas kernels: 14.1 us -> 21 us
    all_to_all x6, waiting for transfers between devices: 54.4 us -> 38.5 us  [exchange(): lax.all_to_all(blocks, axis, 0, 0, tiled=True, axis_index_groups=groups)]
    unnamed x40 -> x57, local copies, waits for them, and re-layouts: 3.72 us -> 9.82 us
    pallas_call x2 -> x3, Pallas kernels: 3.63 us -> 8.26 us  [the longest x1 7.15 us: per_device(): call(worker_body, shape((256, WIDTH)), [VMEM] * 10, scratch=[pltpu.VMEM((...]
    optimization_barrier x2, local copies, waits for them, and re-layouts: 0.35 us -> 2.97 us  [per_device(): lax.optimization_barrier((held, parcels, order, positive_local, weight, t...]
    convert_element_type x4, local copies, waits for them, and re-layouts: 0.42 us -> 2.82 us  [by_user(): return jnp.stack([even, uneven], axis=2).reshape(USERS).astype(jnp.int32)]
    all_to_all x6, starting transfers between devices: 37.7 us -> 39.9 us  [exchange(): lax.all_to_all(blocks, axis, 0, 0, tiled=True, axis_index_groups=groups)]
    pallas_call x1, Pallas kernels: 2.14 us -> 4.17 us  [per_device(): layer_half(normed, held_other, first)]
    convert_element_type x1 -> x2, other arithmetic: 0.95 us -> 2.81 us  [the longest x1 2.24 us: per_device(): order = (at[:, None] == wanted[None, :]).astype(BF16)]
  transfers between devices with their start and end apart: 8 -> 8, of which waited for: 8 -> 5; matrix products, arithmetic and copies ran while one was open for 13% -> 16% of each run, Pallas kernels for 5% -> 12%
where the time goes in v3:
time: 157 us; the launch traced here: 154 us
  starting transfers between devices  51.5 us (33%)
  waiting for transfers between devices  40.2 us (26%)
  local copies, waits for them, and re-layouts  23 us (15%)
  Pallas kernels  21 us (13%)
  other arithmetic  11.9 us (8%)
  matrix products  5.28 us (3%)
    all_to_all x6, starting transfers between devices, exchange(): lax.all_to_all(blocks, axis, 0, 0, tiled=True, axis_index_groups=groups)  39.9 us
    all_to_all x6, waiting for transfers between devices, exchange(): lax.all_to_all(blocks, axis, 0, 0, tiled=True, axis_index_groups=groups)  38.5 us
    unnamed x57, local copies, waits for them, and re-layouts  9.82 us
    ppermute x1, starting transfers between devices, per_device(): held_other = lax.ppermute(held, 'user', PARTNER)  9.31 us
    pallas_call x1, Pallas kernels, per_device(): call(worker_body, shape((256, WIDTH)), [VMEM] * 10, scratch=[pltpu.VMEM((...  7.15 us
    pallas_call x1, Pallas kernels, per_device(): layer_half(normed, held_other, first)  4.17 us
    pallas_call x1, Pallas kernels, per_device(): call(loss_body, (shape((ROWS, WIDTH)), shape((PLANE, 32, ROWS)), shape((5...  3.43 us
  transfers between devices with their start and end apart: 8, of which 5 were waited for; matrix products, arithmetic and copies ran while one was open for 16% of the time, Pallas kernels for 12%

profile of v3, /device:TPU:1, one launch (start us, length us, event | category | flops | bytes accessed | tf_op | source)
XLA Modules:
  0.0 154.1 jit_solution(9301258446232186778)
XLA Ops:
  0.8 1.0 subtract_reduce_fusion
  1.8 1.1 fusion.16
  2.9 0.9 constant_dynamic-slice_fusion
  4.0 0.7 dynamic_slice.18
  4.8 0.7 fusion.20
  5.5 15.7 %all-to-all-start = ((bf16[16,48,128]{2,1,0:T(8,128)(2,1)}), bf16[16,48,128]{2,1,0:T(8,128)(2,1)S(1)}, u32[]{:S(2)}, u32[]{:S(2)}) async-start(bf16[16,48,128]{2,1,0:T(8,128)(2,1)} %fusion.20), calls=%async_computation | async-start | bytes 393216 | tf_op jit(solution)/shard_map/all_to_all | solution.py:245
  23.0 2.4 %fusion.8.x_ref = bf16[512,1024]{1,0:T(8,128)(2,1)} fusion(s32[1024]{0:T(1024)S(1)} %fusion.37, bf16[512,1024]{1,0:T(8,128)(2,1)S(1)} %copy-done, f32[1024]{0:T(1024)S(1)} %copy-done.17, f32[512]{0:T(512)S(1)} %add_rsqrt_fusion, f32[512]{0:T(512)S(1)} %broadcast_multiply_fusion), kind=kOutput, calls=%fused_computation.11 | convolution fusion | flops 1077936128 | bytes 2109440 | tf_op jit(solution)/shard_map/dot_general | solution.py:312
  25.4 8.3 %all-to-all-done.got = bf16[16,48,128]{2,1,0:T(8,128)(2,1)S(1)} async-done(((bf16[16,48,128]{2,1,0:T(8,128)(2,1)}), bf16[16,48,128]{2,1,0:T(8,128)(2,1)S(1)}, u32[]{:S(2)}, u32[]{:S(2)}) %all-to-all-start) | async-done | bytes 196640 | tf_op jit(solution)/shard_map/all_to_all | solution.py:245
  33.7 1.0 shard_map.130
  34.7 4.2 %all-to-all-start.1 = ((bf16[4,720,128]{2,1,0:T(8,128)(2,1)}), bf16[4,720,128]{2,1,0:T(8,128)(2,1)S(1)}, u32[]{:S(2)}, u32[]{:S(2)}) async-start(bf16[4,720,128]{2,1,0:T(8,128)(2,1)} %shard_map.130), calls=%async_computation.1 | async-start | bytes 1474560 | tf_op jit(solution)/shard_map/all_to_all | solution.py:245
  39.3 7.6 %all-to-all-done.1 = bf16[4,720,128]{2,1,0:T(8,128)(2,1)S(1)} async-done(((bf16[4,720,128]{2,1,0:T(8,128)(2,1)}), bf16[4,720,128]{2,1,0:T(8,128)(2,1)S(1)}, u32[]{:S(2)}, u32[]{:S(2)}) %all-to-all-start.1) | async-done | bytes 737312 | tf_op jit(solution)/shard_map/all_to_all | solution.py:245
  47.0 2.0 %broadcast_in_dim.44 = bf16[4,2880,128]{2,1,0:T(8,128)(2,1)} broadcast(bf16[2880,128]{1,0:T(8,128)(2,1)S(1)} %bitcast.39), dimensions={1,2} | broadcast | bytes 3686400 | tf_op jit(solution)/shard_map/broadcast_in_dim | solution.py:241
  48.9 4.2 %all-to-all-start.2 = ((bf16[4,2880,128]{2,1,0:T(8,128)(2,1)}), bf16[4,2880,128]{2,1,0:T(8,128)(2,1)S(1)}, u32[]{:S(2)}, u32[]{:S(2)}) async-start(bf16[4,2880,128]{2,1,0:T(8,128)(2,1)} %broadcast_in_dim.44), calls=%async_computation.2 | async-start | bytes 5898240 | tf_op jit(solution)/shard_map/all_to_all | solution.py:245
  53.4 2.0 %convert_multiply_fusion = (f32[256,1024]{0,1:T(8,128)S(1)}, bf16[256,1024]{0,1:T(8,128)(2,1)}) fusion(bf16[256,1024]{0,1:T(8,128)(2,1)} %copy-done.19, f32[256]{0:T(256)S(1)} %add_rsqrt_fusion.1), kind=kLoop, calls=%fused_computation.13 | loop fusion | flops 786432 | bytes 2098176 | tf_op jit(solution)/shard_map/mul | solution.py:323
  56.2 0.8 fusion.18.hits_ref
  57.0 1.7 %convolution_convert_fusion = bf16[512,1024]{1,0:T(8,128)(2,1)} fusion(bf16[512,1024]{1,0:T(8,128)(2,1)S(1)} %copy-done.1, s32[512]{0:T(512)S(1)} %select_n.228), kind=kOutput, calls=%fused_computation.12 | convolution fusion | flops 537657344 | bytes 2099200 | tf_op jit(solution)/shard_map/dot_general | solution.py:313
  58.7 2.2 %fusion.order_ref = bf16[1024,1024]{1,0:T(8,128)(2,1)} fusion(s32[1024]{0:T(1024)S(1)} %fusion.37), kind=kLoop, calls=%fused_computation.1 | loop fusion | flops 2097152 | bytes 2101248 | tf_op jit(solution)/shard_map/convert_element_type | solution.py:311
  60.9 12.4 %all-to-all-done.2 = bf16[4,2880,128]{2,1,0:T(8,128)(2,1)S(1)} async-done(((bf16[4,2880,128]{2,1,0:T(8,128)(2,1)}), bf16[4,2880,128]{2,1,0:T(8,128)(2,1)S(1)}, u32[]{:S(2)}, u32[]{:S(2)}) %all-to-all-start.2) | async-done | bytes 2949152 | tf_op jit(solution)/shard_map/all_to_all | solution.py:245
  73.3 9.3 %collective-permute-start = (bf16[16,720,128]{2,1,0:T(8,128)(2,1)S(1)}, bf16[16,720,128]{2,1,0:T(8,128)(2,1)}, u32[]{:S(2)}, u32[]{:S(2)}) collective-permute-start(bf16[16,720,128]{2,1,0:T(8,128)(2,1)S(1)} %bitcast.30), channel_id=1, source_target_pairs={{0,16},{16,0},{32,48},{48,32},{64,80},{80,64},{96,112},{112,96},{1... | collective-permute-start | bytes 8847368 | tf_op jit(solution)/shard_map/ppermute | solution.py:349
  82.6 4.6 %all-to-all-start.3 = ((bf16[32,16,1024]{2,1,0:T(8,128)(2,1)}), bf16[32,16,1024]{2,1,0:T(8,128)(2,1)}, u32[]{:S(2)}, u32[]{:S(2)}) async-start(bf16[32,16,1024]{2,1,0:T(8,128)(2,1)} %bitcast.40), calls=%async_computation.3 | async-start | bytes 2097152 | tf_op jit(solution)/shard_map/all_to_all | solution.py:245
  87.3 2.1 %copy.56.low_ref = bf16[256,1024]{1,0:T(8,128)(2,1)} copy(bf16[256,1024]{0,1:T(8,128)(2,1)} %get-tuple-element.49) | data formatting | bytes 1048576 | tf_op jit(solution)/shard_map/optimization_barrier | solution.py:334
  89.4 0.9 copy.57.pos_ref
  90.3 1.2 copy-done.4
  91.5 2.1 %shard_map.131 = (bf16[512,256]{1,0:T(8,128)(2,1)S(1)}, f32[512,256]{1,0:T(8,128)S(1)}, bf16[256,1024]{1,0:T(8,128)(2,1)S(1)}, bf16[256,512]{1,0:T(8,128)(2,1)S(1)}, f32[16,128]{1,0:T(8,128)S(1)}) custom-call(bf16[512,1024]{1,0:T(8,128)(2,1)S(1)} %copy-done.4, bf16[16,720,128]{2,1,0:T(8,128)(2,1)S(1)} %bitcast.31, s32[512,1]{1,0:T(8,128)S(1)} %reshape_select_fusion.1.first_ref), custom_call_target="tpu_custom_call" | custom-call | tf_op jit(solution)/shard_map/pallas_call | solution.py:364
  93.6 4.2 %shard_map.132 = (bf16[512,256]{1,0:T(8,128)(2,1)S(1)}, f32[512,256]{1,0:T(8,128)S(1)}, bf16[256,1024]{1,0:T(8,128)(2,1)S(1)}, bf16[256,512]{1,0:T(8,128)(2,1)S(1)}, f32[16,128]{1,0:T(8,128)S(1)}) custom-call(bf16[512,1024]{1,0:T(8,128)(2,1)S(1)} %copy-done.4, bf16[16,720,128]{2,1,0:T(8,128)(2,1)} %collective-permute-done.w_ref.w1, ...), custom_call_target="tpu_custom_call" | custom-call | tf_op jit(solution)/shard_map/pallas_call | solution.py:365
  97.9 1.0 shard_map.133.out_ref
  99.1 3.4 %shard_map.134 = (bf16[512,1024]{1,0:T(8,128)(2,1)}, bf16[16,32,512]{2,1,0:T(8,128)(2,1)S(1)}, bf16[528,512]{1,0:T(8,128)(2,1)S(1)}, f32[1,512]{1,0:T(1,128)S(1)}) custom-call(s32[1]{0:T(128)} %bitcast.16.core, bf16[512,1024]{1,0:T(8,128)(2,1)S(1)} %shard_map.133.out_ref, bf16[256,1024]{1,0:T(8,128)(2,1)S(1)} %copy-done.10, ...), custom_call_target="tpu_custom_call" | custom-call | tf_op jit(solution)/shard_map/pallas_call | solution.py:370
  102.6 2.3 %collective-permute-start.1 = (bf16[528,512]{1,0:T(8,128)(2,1)S(1)}, bf16[528,512]{1,0:T(8,128)(2,1)S(1)}, u32[]{:S(2)}, u32[]{:S(2)}) collective-permute-start(bf16[528,512]{1,0:T(8,128)(2,1)S(1)} %get-tuple-element.56), channel_id=1, source_target_pairs={{0,16},{16,0},{32,48},{48,32},{64,80},{80,64},{96,112},{112,96},{1... | collective-permute-start | bytes 1622024 | tf_op jit(solution)/shard_map/ppermute | solution.py:382
  104.9 1.7 %collective-permute-done.1.got_ref = bf16[528,512]{1,0:T(8,128)(2,1)S(1)} collective-permute-done((bf16[528,512]{1,0:T(8,128)(2,1)S(1)}, bf16[528,512]{1,0:T(8,128)(2,1)S(1)}, u32[]{:S(2)}, u32[]{:S(2)}) %collective-permute-start.1) | collective-permute-done | bytes 540704 | tf_op jit(solution)/shard_map/ppermute | solution.py:382
  106.7 0.9 copy-done.5
  107.5 6.5 %all-to-all-start.4 = ((bf16[16,40,512]{2,1,0:T(8,128)(2,1)}), bf16[16,40,512]{2,1,0:T(8,128)(2,1)}, u32[]{:S(2)}, u32[]{:S(2)}) async-start(bf16[16,40,512]{2,1,0:T(8,128)(2,1)} %copy-done.5), calls=%async_computation.4 | async-start | bytes 1310720 | tf_op jit(solution)/shard_map/all_to_all | solution.py:245
  115.4 10.2 %all-to-all-done.4.got_ref = bf16[16,40,512]{2,1,0:T(8,128)(2,1)} async-done(((bf16[16,40,512]{2,1,0:T(8,128)(2,1)}), bf16[16,40,512]{2,1,0:T(8,128)(2,1)}, u32[]{:S(2)}, u32[]{:S(2)}) %all-to-all-start.4) | async-done | bytes 655392 | tf_op jit(solution)/shard_map/all_to_all | solution.py:245
  125.5 1.3 shard_map.137
  128.1 4.7 %all-to-all-start.5 = ((bf16[16,16,128]{2,1,0:T(8,128)(2,1)}), bf16[16,16,128]{2,1,0:T(8,128)(2,1)S(1)}, u32[]{:S(2)}, u32[]{:S(2)}) async-start(bf16[16,16,128]{2,1,0:T(8,128)(2,1)} %bitcast.34), calls=%async_computation.5 | async-start | bytes 131072 | tf_op jit(solution)/shard_map/all_to_all | solution.py:245
  133.4 0.8 copy.53
  134.1 0.7 convert_element_type.84
  134.8 0.8 copy.55
  136.7 1.3 add_select_fusion
  138.1 0.8 select_n.243.lands
  139.5 0.8 reshape.332.lowers
  140.4 1.6 %copy-done.3 = bf16[1024,1024]{1,0:T(8,128)(2,1)S(1)} copy-done((bf16[1024,1024]{1,0:T(8,128)(2,1)S(1)}, bf16[1024,1024]{1,0:T(8,128)(2,1)}, u32[]{:S(2)}) %copy-start.3) | copy-done | bytes 2097176
  141.9 1.0 copy-done.9
  143.0 0.7 copy-done.18
  143.7 7.1 %shard_map.136 = bf16[256,1024]{1,0:T(8,128)(2,1)} custom-call(s32[1,512]{1,0:T(1,128)S(1)} %select_n.243.lands, f32[1,512]{1,0:T(1,128)S(1)} %reshape.332.lowers, bf16[512,1024]{1,0:T(8,128)(2,1)} %bitcast.18.got_ref, bf16[1024,1024]{1,0:T(8,128)(2,1)S(1)} %copy-done.3, f32[1,1024]{1,0:T(1,128)S(1)} %bitcast.38, bf16[16,720,128]{2,1,0:T(8,128)(2,1)S(1)} %bitcast.32, ...), custom_call_target="tpu_custom_call" | custom-call | tf_op jit(solution)/shard_map/pallas_call | solution.py:400
  150.8 0.9 copy-done.12
  151.7 0.8 copy-done.13
  152.5 0.8 copy-done.16
  153.3 0.8 shard_map.138
  (101 shorter events, 8.8 us)
Async XLA Ops:
  0.6 20.6 %copy-start = (bf16[512,1024]{1,0:T(8,128)(2,1)S(1)}, bf16[512,1024]{1,0:T(8,128)(2,1)}, u32[]{:S(2)}) copy-start(bf16[512,1024]{1,0:T(8,128)(2,1)} %tok_ref.1) | copy-start | bytes 3145732
  0.6 21.3 %copy-start.23 = (s32[1,32]{1,0:T(1,128)S(1)}, s32[1,32]{1,0:T(1,128)}, u32[]{:S(2)}) copy-start(s32[1,32]{1,0:T(1,128)} %param.12) | copy-start | bytes 388
  0.7 21.6 %copy-start.26 = (s32[1,32]{1,0:T(1,128)S(1)}, s32[1,32]{1,0:T(1,128)}, u32[]{:S(2)}) copy-start(s32[1,32]{1,0:T(1,128)} %param.14) | copy-start | bytes 388
  0.7 21.6 %copy-start.25 = (s32[1,32]{1,0:T(1,128)S(1)}, s32[1,32]{1,0:T(1,128)}, u32[]{:S(2)}) copy-start(s32[1,32]{1,0:T(1,128)} %param.13) | copy-start | bytes 388
  2.9 20.1 %copy-start.17 = (f32[1024]{0:T(1024)S(1)}, f32[1024]{0:T(1024)}, u32[]{:S(2)}) copy-start(f32[1024]{0:T(1024)} %param.18) | copy-start | bytes 12292
  5.5 28.2 %all-to-all-start = ((bf16[16,48,128]{2,1,0:T(8,128)(2,1)}), bf16[16,48,128]{2,1,0:T(8,128)(2,1)S(1)}, u32[]{:S(2)}, u32[]{:S(2)}) async-start(bf16[16,48,128]{2,1,0:T(8,128)(2,1)} %fusion.20), calls=%async_computation | async-start | bytes 393216 | tf_op jit(solution)/shard_map/all_to_all | solution.py:245
  25.4 13.5 %copy-start.20 = (bf16[256,1024]{1,0:T(8,128)(2,1)S(1)}, bf16[256,1024]{1,0:T(8,128)(2,1)}, u32[]{:S(2)}) copy-start(bf16[256,1024]{1,0:T(8,128)(2,1)} %param.17) | copy-start | bytes 1572868
  34.7 12.3 %all-to-all-start.1 = ((bf16[4,720,128]{2,1,0:T(8,128)(2,1)}), bf16[4,720,128]{2,1,0:T(8,128)(2,1)S(1)}, u32[]{:S(2)}, u32[]{:S(2)}) async-start(bf16[4,720,128]{2,1,0:T(8,128)(2,1)} %shard_map.130), calls=%async_computation.1 | async-start | bytes 1474560 | tf_op jit(solution)/shard_map/all_to_all | solution.py:245
  39.1 9.8 %copy-start.19 = (bf16[256,1024]{0,1:T(8,128)(2,1)}, bf16[256,1024]{0,1:T(8,128)(2,1)S(1)}, u32[]{:S(2)}) copy-start(bf16[256,1024]{0,1:T(8,128)(2,1)S(1)} %copy.51) | copy-start | bytes 1572868
  48.9 4.2 %copy-start.21 = (s32[16,256]{1,0:T(8,128)S(1)}, s32[16,256]{1,0:T(8,128)}, u32[]{:S(2)}) copy-start(s32[16,256]{1,0:T(8,128)} %param.16) | copy-start | bytes 49156
  48.9 24.4 %all-to-all-start.2 = ((bf16[4,2880,128]{2,1,0:T(8,128)(2,1)}), bf16[4,2880,128]{2,1,0:T(8,128)(2,1)S(1)}, u32[]{:S(2)}, u32[]{:S(2)}) async-start(bf16[4,2880,128]{2,1,0:T(8,128)(2,1)} %broadcast_in_dim.44), calls=%async_computation.2 | async-start | bytes 5898240 | tf_op jit(solution)/shard_map/all_to_all | solution.py:245
  53.1 3.1 %copy-start.24 = (s32[512]{0:T(512)S(1)}, s32[512]{0:T(512)}, u32[]{:S(2)}) copy-start(s32[512]{0:T(512)} %param.15) | copy-start | bytes 6148
  53.1 3.1 %copy-start.22 = (f32[512]{0:T(512)S(1)}, f32[512]{0:T(512)}, u32[]{:S(2)}) copy-start(f32[512]{0:T(512)} %param.20) | copy-start | bytes 6148
  53.4 3.6 %copy-start.1 = (bf16[512,1024]{1,0:T(8,128)(2,1)S(1)}, bf16[512,1024]{1,0:T(8,128)(2,1)}, u32[]{:S(2)}) copy-start(bf16[512,1024]{1,0:T(8,128)(2,1)} %tok_ref.1) | copy-start | bytes 3145732
  73.3 20.3 %collective-permute-start = (bf16[16,720,128]{2,1,0:T(8,128)(2,1)S(1)}, bf16[16,720,128]{2,1,0:T(8,128)(2,1)}, u32[]{:S(2)}, u32[]{:S(2)}) collective-permute-start(bf16[16,720,128]{2,1,0:T(8,128)(2,1)S(1)} %bitcast.30), channel_id=1, source_target_pairs={{0,16},{16,0},{32,48},{48,32},{64,80},{80,64},{96,112},{112,96},{1... | collective-permute-start | bytes 8847368 | tf_op jit(solution)/shard_map/ppermute | solution.py:349
  82.6 24.9 %all-to-all-start.3 = ((bf16[32,16,1024]{2,1,0:T(8,128)(2,1)}), bf16[32,16,1024]{2,1,0:T(8,128)(2,1)}, u32[]{:S(2)}, u32[]{:S(2)}) async-start(bf16[32,16,1024]{2,1,0:T(8,128)(2,1)} %bitcast.40), calls=%async_computation.3 | async-start | bytes 2097152 | tf_op jit(solution)/shard_map/all_to_all | solution.py:245
  90.2 1.2 copy-start.4
  93.6 4.2 %copy-start.6 = (bf16[256,1024]{1,0:T(8,128)(2,1)}, bf16[256,1024]{1,0:T(8,128)(2,1)S(1)}, u32[]{:S(2)}) copy-start(bf16[256,1024]{1,0:T(8,128)(2,1)S(1)} %get-tuple-element.44.o0) | copy-start | bytes 1572868
  93.6 4.2 %copy-start.2 = (bf16[512,1024]{1,0:T(8,128)(2,1)S(1)}, bf16[512,1024]{1,0:T(8,128)(2,1)}, u32[]{:S(2)}) copy-start(bf16[512,1024]{1,0:T(8,128)(2,1)} %tok_ref.1) | copy-start | bytes 3145732
  97.8 1.0 copy-start.8
  97.9 1.2 copy-start.10
  97.9 1.3 copy-start.11
  102.6 37.8 %copy-start.7 = (bf16[256,1024]{1,0:T(8,128)(2,1)S(1)}, bf16[256,1024]{1,0:T(8,128)(2,1)}, u32[]{:S(2)}) copy-start(bf16[256,1024]{1,0:T(8,128)(2,1)} %copy-done.6) | copy-start | bytes 1572868
  102.6 3.9 %collective-permute-start.1 = (bf16[528,512]{1,0:T(8,128)(2,1)S(1)}, bf16[528,512]{1,0:T(8,128)(2,1)S(1)}, u32[]{:S(2)}, u32[]{:S(2)}) collective-permute-start(bf16[528,512]{1,0:T(8,128)(2,1)S(1)} %get-tuple-element.56), channel_id=1, source_target_pairs={{0,16},{16,0},{32,48},{48,32},{64,80},{80,64},{96,112},{112,96},{1... | collective-permute-start | bytes 1622024 | tf_op jit(solution)/shard_map/ppermute | solution.py:382
  106.7 0.9 copy-start.5
  107.5 18.0 %all-to-all-start.4 = ((bf16[16,40,512]{2,1,0:T(8,128)(2,1)}), bf16[16,40,512]{2,1,0:T(8,128)(2,1)}, u32[]{:S(2)}, u32[]{:S(2)}) async-start(bf16[16,40,512]{2,1,0:T(8,128)(2,1)} %copy-done.5), calls=%async_computation.4 | async-start | bytes 1310720 | tf_op jit(solution)/shard_map/all_to_all | solution.py:245
  126.8 0.6 copy-start.15
  127.4 0.6 copy-start.14
  128.1 22.8 %all-to-all-start.5 = ((bf16[16,16,128]{2,1,0:T(8,128)(2,1)}), bf16[16,16,128]{2,1,0:T(8,128)(2,1)S(1)}, u32[]{:S(2)}, u32[]{:S(2)}) async-start(bf16[16,16,128]{2,1,0:T(8,128)(2,1)} %bitcast.34), calls=%async_computation.5 | async-start | bytes 131072 | tf_op jit(solution)/shard_map/all_to_all | solution.py:245
  140.3 1.6 %copy-start.3 = (bf16[1024,1024]{1,0:T(8,128)(2,1)S(1)}, bf16[1024,1024]{1,0:T(8,128)(2,1)}, u32[]{:S(2)}) copy-start(bf16[1024,1024]{1,0:T(8,128)(2,1)} %fusion.order_ref) | copy-start | bytes 6291460
  141.9 1.0 copy-start.9
  143.0 0.7 copy-start.18
  150.8 0.9 copy-start.12
  151.7 0.8 copy-start.13
  152.5 0.8 copy-start.16

commit v4 on v3

v4 whole, which is shorter than its diff:
```python
import jax
import jax.numpy as jnp
from jax import lax
from jax.experimental import pallas as pl
from jax.experimental.pallas import tpu as pltpu
from jax.sharding import PartitionSpec as P


norm_epsilon = 1e-05
scale_epsilon = 1e-06
inverse_temp = 20.0
loss_scale = 32.0

F32 = jnp.float32
BF16 = jnp.bfloat16

USERS = 32
ITEMS = 16
PLANE = 16
LANES = 128
ROWS = 512
MOST = 16
WIDTH = 1024
HEAD = 128

FIRST = [[x * 8 + y * 2 for x in range(4)] for y in range(4)] + [
    [x * 8 + y * 2 + 1 for y in range(4)] for x in range(4)
]
SECOND = [[x * 8 + y * 2 for y in range(4)] for x in range(4)] + [
    [x * 8 + y * 2 + 1 for x in range(4)] for y in range(4)
]
PIECE = 4 * 720


def shifted(groups, step):
    return [(g[n], g[(n + step) % 4]) for g in groups for n in range(4)]


SAME_CORE = [[k * 2 + c for k in range(PLANE)] for c in range(2)]
PARTNER = [(k, k ^ 1) for k in range(USERS)]

VMEM = pl.BlockSpec(memory_space=pltpu.VMEM)
ANY = pl.BlockSpec(memory_space=pl.ANY)
HBM = pl.BlockSpec(memory_space=pltpu.HBM)
SMEM = pl.BlockSpec(memory_space=pltpu.SMEM)
W_ROWS = 512
REST = 208


def shape(dims, kind=BF16):
    return jax.ShapeDtypeStruct(dims, kind)


def dot(a, b, contract=((1,), (0,))):
    return lax.dot_general(a, b, (contract, ((), ())), preferred_element_type=F32)


def call(body, outs, specs, scratch=(), mib=8, out_specs=None):
    return pl.pallas_call(
        body,
        out_shape=outs,
        in_specs=specs,
        out_specs=out_specs or jax.tree.map(lambda _: VMEM, outs),
        scratch_shapes=list(scratch),
        compiler_params=pltpu.CompilerParams(vmem_limit_bytes=mib * 2**20),
    )


def column_of(row, n):
    eye = lax.broadcasted_iota(jnp.int32, (n, n), 0) == lax.broadcasted_iota(jnp.int32, (n, n), 1)
    return jnp.sum(jnp.where(eye, row, 0.0), axis=1, keepdims=True)


def reordered(rows):
    at = lax.broadcasted_iota(jnp.int32, (1, WIDTH), 1)
    wanted = (at % 512) // 32 * 64 + at // 512 * 32 + at % 32
    order = lax.broadcasted_iota(jnp.int32, (WIDTH, WIDTH), 0) == wanted
    return dot(rows, jnp.where(order, 1.0, 0.0).astype(BF16)).astype(BF16)


def message_body(
    where, neg_ref, w_ref, o_ref, table_ref, out_ref, w_part, o_part, rows, turned, quads, sems
):
    item, core, place = where[0], where[1], where[2]
    chunk = lax.div(place, 2)
    block = lax.div(chunk, 2) * 4 + core * 2 + lax.rem(chunk, 2)
    copies = (
        pltpu.make_async_copy(
            w_ref.at[pl.ds((place % 2) * 32, 32), pl.ds(block * LANES, LANES)], w_part, sems.at[0]
        ),
        pltpu.make_async_copy(
            o_ref.at[:, pl.ds((core * 2 + place // 8) * LANES, LANES)], o_part, sems.at[1]
        ),
        pltpu.make_async_copy(table_ref.at[:, pl.ds(core * 512, 512)], rows, sems.at[2]),
    )
    for copy in copies:
        copy.start()
    lane = lax.broadcasted_iota(jnp.int32, (ITEMS, 256), 1)
    ids = jnp.sum(
        jnp.where(lane == item * 16 + place, neg_ref[...].astype(F32), 0.0), axis=1, keepdims=True
    ).astype(jnp.int32)
    pick = jnp.where(lane == ids - item * 256, 1.0, 0.0).astype(BF16)
    for copy in copies:
        copy.wait()
    turned[...] = jnp.transpose(o_part[...].astype(F32))
    part = turned[pl.ds((place % 8) * 16, 16), :]
    part = jnp.concatenate([part[0:8, :], part[8:16, :]], axis=1).astype(BF16)
    group = dot(pick, rows[...])
    quads[...] = jnp.zeros_like(quads)
    for b in range(4):
        quads[:, b, :] = group[:, b * LANES : (b + 1) * LANES]
    for i in range(ITEMS):
        out_ref[i, 0:32, :] = w_part[...]
        out_ref[i, 32:40, :] = part
    out_ref[:, 40:48, :] = quads[...].astype(BF16)


def prepare_body(
    where,
    tok_ref,
    len_ref,
    dest_ref,
    off_ref,
    pos_ref,
    in_gain,
    table_ref,
    neg_ref,
    x_ref,
    cols_ref,
    label_ref,
    parcel_ref,
    low_ref,
    hat_ref,
    scale_ref,
    hits_ref,
    tok,
    tab,
    hat,
    turned,
    sems,
):
    item, user = where[0], where[3]
    copies = (
        pltpu.make_async_copy(tok_ref, tok, sems.at[0]),
        pltpu.make_async_copy(table_ref, tab, sems.at[1]),
    )
    for copy in copies:
        copy.start()
    for copy in copies:
        copy.wait()
    normed = layer_norm(tok[...].astype(F32), in_gain[...]).astype(BF16)
    x_ref[...] = reordered(normed)

    lens, dest, off = (r[...].astype(F32) for r in (len_ref, dest_ref, off_ref))
    sub = lax.broadcasted_iota(jnp.int32, (32, 32), 0)
    lane = lax.broadcasted_iota(jnp.int32, (32, 32), 1)
    len_col, dest_col, off_col = (column_of(v, 32) for v in (lens, dest, off))
    start_row = jnp.sum(jnp.where(sub < lane, len_col, 0.0), axis=0, keepdims=True)
    start_col = column_of(start_row, 32)
    row = lax.broadcasted_iota(jnp.int32, (ROWS, 32), 0).astype(F32)
    inside = (row >= start_row) & (row < start_row + lens)
    valid = jnp.sum(jnp.where(inside, 1.0, 0.0), axis=1, keepdims=True) > 0.5
    first = jnp.sum(jnp.where(inside, start_row, 0.0), axis=1, keepdims=True)
    first = jnp.where(valid, first, row[:, 0:1])
    weight = jnp.where(valid, loss_scale, 0.0)
    pos = jnp.transpose(jnp.broadcast_to(pos_ref[...].astype(F32), (LANES, ROWS)))
    at = lax.broadcasted_iota(jnp.int32, (ROWS, LANES), 1)
    local = pos - (item * 256).astype(F32)
    cols_ref[...] = jnp.where(at == 0, first, jnp.where(at == 1, weight, local))

    wide = lax.broadcasted_iota(jnp.int32, (32, LANES), 1).astype(F32)
    to_land = jnp.sum(jnp.where(wide == dest_col, off_col, 0.0), axis=0, keepdims=True)
    to_count = jnp.sum(jnp.where(wide - 32.0 == dest_col, len_col, 0.0), axis=0, keepdims=True)
    label_ref[...] = jnp.broadcast_to(to_land + to_count, (16, LANES)).astype(BF16)

    lane_f = lane.astype(F32)
    first_row = jnp.sum(jnp.where(lane_f == dest_col, start_col, 0.0), axis=0, keepdims=True)
    count_row = jnp.sum(jnp.where(lane_f == dest_col, len_col, 0.0), axis=0, keepdims=True)
    slot = lax.broadcasted_iota(jnp.int32, (ROWS, 32), 0)
    peer = lax.broadcasted_iota(jnp.int32, (ROWS, 32), 1) == slot // MOST
    begin = jnp.sum(jnp.where(peer, first_row, 0.0), axis=1, keepdims=True)
    count = jnp.sum(jnp.where(peer, count_row, 0.0), axis=1, keepdims=True)
    within = (slot[:, 0:1] % MOST).astype(F32)
    source = jnp.where(within < count, begin + within, -1.0)
    send = lax.broadcasted_iota(jnp.int32, (ROWS, ROWS), 1).astype(F32) == source
    parcel_ref[...] = dot(jnp.where(send, 1.0, 0.0).astype(BF16), tok[...]).astype(BF16)

    table = tab[...].astype(F32)
    scale = lax.rsqrt(jnp.mean(table * table, axis=1, keepdims=True) + scale_epsilon)
    hat[...] = table * scale
    low_ref[...] = hat[...].astype(BF16)
    turned[...] = jnp.transpose(hat[:, pl.ds((user // 4) * LANES, LANES)])
    hat_ref[...] = turned[pl.ds((user % 4) * 32, 32), :]
    scale_ref[...] = jnp.transpose(jnp.broadcast_to(scale, (256, LANES)))[0:1, :]

    ids = jnp.broadcast_to(neg_ref[...].astype(F32)[:, None, :], (ITEMS, 16, 256)).reshape(256, 256)
    spot = lax.broadcasted_iota(jnp.int32, (256, 256), 0) % 16 + item * 16
    lanes = lax.broadcasted_iota(jnp.int32, (256, 256), 1)
    ids = jnp.sum(jnp.where(lanes == spot, ids, 0.0), axis=1, keepdims=True)
    hits_ref[...] = jnp.where(lanes.astype(F32) == ids - (item * 256).astype(F32), 1.0, 0.0).astype(BF16)


def forward_body(got, label, out):
    for i in range(ITEMS):
        out[i * 32 : (i + 1) * 32, :] = got[i, 0:32, :]
    left = lax.broadcasted_iota(jnp.int32, (8, LANES), 1) < 64
    for b in range(8):
        even, odd = got[2 * b, 32:40, :].astype(F32), got[2 * b + 1, 32:40, :].astype(F32)
        top = jnp.where(left, even, pltpu.roll(odd, 64, 1))
        bottom = jnp.where(left, pltpu.roll(even, 64, 1), odd)
        out[W_ROWS + b * 16 : W_ROWS + (b + 1) * 16, :] = jnp.concatenate(
            [top, bottom], axis=0
        ).astype(BF16)
    quads = got[:, 40:48, :].astype(F32)
    for b in range(4):
        out[W_ROWS + 128 + b * 16 : W_ROWS + 144 + b * 16, :] = quads[:, b, :].astype(BF16)
    out[W_ROWS + 192 : W_ROWS + 208, :] = label[...]


def collect_body(where, p0, p1, p2, p3, out_ref, sems):
    copies = [
        pltpu.make_async_copy(
            p, out_ref.at[lax.rem(where[5] + 4 - n, 4)], sems.at[n]
        )
        for n, p in enumerate((p0, p1, p2, p3))
    ]
    for copy in copies:
        copy.start()
    for copy in copies:
        copy.wait()


def fetches(pieces, w, sems):
    return [pltpu.make_async_copy(p, w.at[n], sems.at[n]) for n, p in enumerate(pieces)]


def kind_of(position, n):
    return lax.rem(position + 4 - n, 4)


def project(x, w, n):
    parts = [w[n, i * 720 : i * 720 + W_ROWS, :] for i in range(4)]
    both = jnp.concatenate(
        [jnp.concatenate(parts[0:2], axis=0), jnp.concatenate(parts[2:4], axis=0)], axis=1
    )
    return jax.nn.silu(dot(x, both)).astype(BF16)


def attend(act, first, mixed_ref):
    v, q, k = act[1], act[2], act[3]
    for b in range(first.shape[0] // 128):
        lo, hi = b * 128, (b + 1) * 128
        at = max(lo - 128, 0)
        rows = lo + lax.broadcasted_iota(jnp.int32, (128, hi - at), 0)
        cols = at + lax.broadcasted_iota(jnp.int32, (128, hi - at), 1)
        allowed = (cols >= first[lo:hi, :]) & (cols <= rows)
        for h in range(2):
            d0, d1 = h * HEAD, (h + 1) * HEAD
            scores = dot(q[lo:hi, d0:d1], k[at:hi, d0:d1], ((1,), (1,))) * HEAD ** (-0.5)
            weights = jnp.where(allowed, jax.nn.silu(scores), 0.0).astype(BF16)
            mixed_ref[lo:hi, d0:d1] = dot(weights, v[at:hi, d0:d1])


def half_body(
    where,
    x_ref,
    p0,
    p1,
    p2,
    p3,
    cols_ref,
    u_ref,
    mixed_ref,
    o_ref,
    g_ref,
    label_ref,
    x,
    w,
    act,
    sems,
):
    copies = fetches((p0, p1, p2, p3), w, sems)
    first_copy = pltpu.make_async_copy(x_ref, x, sems.at[4])
    first_copy.start()
    for copy in copies:
        copy.start()
    first_copy.wait()
    for n, copy in enumerate(copies):
        copy.wait()
        kind = kind_of(where[0], n)
        act[kind] = project(x[...], w, n)
        row = pl.multiple_of(kind * 64, 64)

        def columns(at):
            return jnp.concatenate(
                [w[n, i * 720 + at : i * 720 + at + 16, :] for i in range(4)], axis=0
            )

        for b in range(8):
            o_ref[pl.ds(row, 64), b * LANES : (b + 1) * LANES] = columns(W_ROWS + b * 16)
        for b in range(4):
            g_ref[pl.ds(row, 64), b * LANES : (b + 1) * LANES] = columns(W_ROWS + 128 + b * 16)
        labels = [
            w[n, i * 720 + W_ROWS + 192 : (i + 1) * 720, :].astype(F32)[0:1, :] for i in range(4)
        ]
        label_ref[kind] = jnp.concatenate(labels + [jnp.zeros((4, LANES), F32)], axis=0)
    u_ref[...] = act[0]
    attend(act, cols_ref[:, 0:1].astype(jnp.int32), mixed_ref)


def gated_out(rows, u0, m0, o0, u1, m1, o1, gain_ref):
    a, b = m0[...], m1[...]
    width = 512.0
    center = (jnp.sum(a, axis=1, keepdims=True) + jnp.sum(b, axis=1, keepdims=True)) / width
    a, b = a - center, b - center
    spread = (
        jnp.sum(a * a, axis=1, keepdims=True) + jnp.sum(b * b, axis=1, keepdims=True)
    ) / width
    inv = lax.rsqrt(spread + norm_epsilon)
    ga = (a * inv * gain_ref[:, 0:256] * u0[...].astype(F32)).astype(BF16)
    gb = (b * inv * gain_ref[:, 256:512] * u1[...].astype(F32)).astype(BF16)
    delta = dot(ga, o0[...]) + dot(gb, o1[...])
    return (rows.astype(F32) + delta).astype(BF16)


def out_body(tok_ref, u0, m0, o0, u1, m1, o1, gain_ref, out_ref):
    out_ref[...] = gated_out(tok_ref[...], u0, m0, o0, u1, m1, o1, gain_ref)


def worker_body(where, near_ref, far_ref, got_ref, in_gain, o0, o1, gain_ref, *rest):
    pieces, (out_ref, w0, w1, a0, a1, m0, m1, sems) = rest[:8], rest[8:]
    core, user = where[1], where[3]
    copies = (
        fetches(pieces[:4], w0, sems.at[0]),
        fetches(pieces[4:], w1, sems.at[1]),
    )
    for copy in copies[0] + copies[1]:
        copy.start()
    lane = lax.broadcasted_iota(jnp.int32, (32, LANES), 1)
    sub = lax.broadcasted_iota(jnp.int32, (32, ROWS), 0)
    slot = lax.broadcasted_iota(jnp.int32, (1, ROWS), 1)
    peer = slot // MOST
    x, y, c = peer // 8, peer // 2 % 4, peer % 2
    spot = jnp.where(c == 0, y * 8 + x, x * 8 + y)

    def of_peer(at):
        total = 0.0
        for ref, mine in ((near_ref, c == core), (far_ref, c != core)):
            labels = ref[...].reshape(32, LANES)
            value = jnp.sum(jnp.where(lane == at, labels, 0.0), axis=1, keepdims=True)
            total = total + jnp.sum(
                jnp.where((sub == spot) & mine, value, 0.0), axis=0, keepdims=True
            )
        return total

    lower, count = of_peer(user), of_peer(user + USERS)
    within = (slot % MOST).astype(F32)
    lands = jnp.where(within < count, lower + within, -1.0)
    here = lax.broadcasted_iota(jnp.int32, (256, ROWS), 0).astype(F32) == lands
    first = jnp.sum(jnp.where(here, lower, 0.0), axis=1, keepdims=True).astype(jnp.int32)
    rows = dot(jnp.where(here, 1.0, 0.0).astype(BF16), got_ref[...]).astype(BF16)
    normed = layer_norm(rows.astype(F32), in_gain[...]).astype(BF16)
    moved = reordered(normed)
    for position, group, w, act, mixed in (
        (where[4], copies[0], w0, a0, m0),
        (where[5], copies[1], w1, a1, m1),
    ):
        for n, copy in enumerate(group):
            copy.wait()
            act[kind_of(position, n)] = project(moved, w, n)
        attend(act, first, mixed)
    out_ref[...] = gated_out(rows, a0.at[0], m0, o0, a1.at[0], m1, o1, gain_ref)


def loss_body(core, out_ref, low_ref, g0_ref, g1_ref, cols_ref, grad_ref, own_ref, send_ref, own_inner, terms):
    c = core[0]

    g0, g1 = g0_ref[...].astype(F32), g1_ref[...].astype(F32)
    size = (jnp.sum(g0 * g0, axis=1, keepdims=True) + jnp.sum(g1 * g1, axis=1, keepdims=True)) / WIDTH
    scale = lax.rsqrt(size + scale_epsilon)
    g0, g1 = (g0 * scale).astype(BF16), (g1 * scale).astype(BF16)
    here = c == 0
    both = jnp.concatenate([jnp.where(here, g0, g1), jnp.where(here, g1, g0)], axis=1)
    row = lax.broadcasted_iota(jnp.int32, (256, 256), 0)
    col = lax.broadcasted_iota(jnp.int32, (256, 256), 1)
    swap = jnp.where(col == (row % 16) * 16 + row // 16, 1.0, 0.0).astype(BF16)
    group = dot(swap, both).astype(BF16)
    rows = jnp.concatenate([low_ref[...], group], axis=0)

    out = out_ref[...].astype(F32)
    out_scale = lax.rsqrt(jnp.mean(out * out, axis=1, keepdims=True) + scale_epsilon)
    hat = out * out_scale
    low = hat.astype(BF16)
    factor = inverse_temp / WIDTH
    raw = dot(low, rows, ((1,), (1,)))
    hit = lax.broadcasted_iota(jnp.int32, (ROWS, 256), 1) == cols_ref[:, 2:3].astype(jnp.int32)
    pos = jnp.exp(jnp.sum(jnp.where(hit, raw[:, :256], 0.0), axis=1, keepdims=True) * factor)
    neg = jnp.exp(raw[:, 256:] * factor)
    total = pos + jnp.sum(neg, axis=1, keepdims=True)
    weight = cols_ref[:, 1:2]
    pos_grad = weight * (pos / total - 1.0)
    grads = jnp.concatenate(
        [jnp.where(hit, pos_grad, 0.0).astype(BF16), (weight * neg / total).astype(BF16)], axis=1
    )
    grad_hat = dot(grads, rows) * factor
    inner = jnp.mean(grad_hat * hat, axis=1, keepdims=True)
    grad_ref[...] = ((grad_hat - hat * inner) * out_scale).astype(BF16)
    sums = dot(low, grads, ((0,), (0,))) * factor
    terms[...] = sums.astype(BF16).reshape(PLANE, 2, 32, ROWS)
    for k in range(PLANE):
        own_ref[k] = terms[k, c]
        send_ref[k * 32 : (k + 1) * 32, :] = terms[k, 1 - c]
    products = jnp.sum(grads.astype(F32) * raw, axis=0, keepdims=True) * factor
    own_inner[...] = products
    top = products.astype(BF16).astype(F32)
    send_ref[512:528, :] = split_rows(top, products - top).astype(BF16)


def split_rows(top, rest):
    at = lax.broadcasted_iota(jnp.int32, (16, ROWS), 0)
    return jnp.where(at == 0, top, jnp.where(at == 1, rest, 0.0))


def pair_body(own_ref, inner_ref, got_ref, out_ref):
    other = got_ref[512:528, :].astype(F32)
    inner = inner_ref[...] + other[0:1, :] + other[1:2, :]
    top = inner.astype(BF16).astype(F32)
    tail = split_rows(top, inner - top).astype(BF16)
    for k in range(PLANE):
        mine = own_ref[k].astype(F32) + got_ref[k * 32 : (k + 1) * 32, :].astype(F32)
        out_ref[k, 0:32, :] = mine.astype(BF16)
        out_ref[k, 32:40, :] = tail[0:8, :]


def plane_body(got_ref, pos_ref, neg_ref):
    acc = got_ref[0].astype(F32)
    for k in range(1, PLANE):
        acc = acc + got_ref[k].astype(F32)
    inner = acc[32:33, :] + acc[33:34, :]
    top = inner.astype(BF16).astype(F32)
    full = jnp.concatenate([acc[0:32, :], split_rows(top, inner - top)], axis=0)
    pos_ref[...] = full[:, 0:256]
    tail = jnp.concatenate([full[:, 256:512], jnp.zeros((80, 256), F32)], axis=0)
    neg_ref[...] = jnp.transpose(tail).astype(BF16)


def item_body(pos_ref, hits_ref, got_ref, hat_ref, scale_ref, out_ref):
    total = pos_ref[...] + dot(got_ref[...], hits_ref[...], ((0,), (0,)))[0:48, :]
    inner = (total[32:33, :] + total[33:34, :]) / WIDTH
    out_ref[...] = (total[0:32, :] - hat_ref[...] * inner) * scale_ref[...]


def layer_norm(values, gain):
    center = jnp.mean(values, axis=-1, keepdims=True)
    shifted = values - center
    spread = jnp.mean(shifted * shifted, axis=-1, keepdims=True)
    return shifted * lax.rsqrt(spread + norm_epsilon) * gain


def in_hbm(values):
    return pltpu.with_memory_space_constraint(values, pltpu.HBM)


def exchange(blocks, axis, groups=None):
    return lax.all_to_all(blocks, axis, 0, 0, tiled=True, axis_index_groups=groups)


def per_device(
    tokens,
    lengths,
    destination,
    worker_offset,
    positives,
    negatives,
    table,
    in_gain,
    w_uvqk,
    out_gain,
    w_out,
):
    item = lax.axis_index("item")
    user = lax.axis_index("user")
    core = user & 1
    x, y = user >> 3, (user >> 1) & 3
    place = jnp.where(core == 0, y * 4 + x, x * 4 + y)
    second = jnp.where(core == 0, y, x)
    first = jnp.where(core == 0, x, y)
    where = jnp.stack([item, core, place, user, second, first]).astype(jnp.int32)

    first_message = call(
        message_body,
        shape((ITEMS, 48, LANES)),
        [SMEM, VMEM, HBM, HBM, HBM],
        scratch=[
            pltpu.VMEM((32, LANES), BF16),
            pltpu.VMEM((64, LANES), BF16),
            pltpu.VMEM((256, 512), BF16),
            pltpu.VMEM((LANES, 64), F32),
            pltpu.VMEM((ITEMS, 8, LANES), F32),
            pltpu.SemaphoreType.DMA((3,)),
        ],
    )(where, negatives, in_hbm(w_uvqk), in_hbm(w_out.T), in_hbm(table))
    got = exchange(first_message, "item")

    x_rows, cols, labels, parcels, table_low, hat_part, table_scale, hits = call(
        prepare_body,
        (
            shape((ROWS, WIDTH)),
            shape((ROWS, LANES), F32),
            shape((16, LANES)),
            shape((ROWS, WIDTH)),
            shape((256, WIDTH)),
            shape((32, 256), F32),
            shape((1, 256), F32),
            shape((256, 256)),
        ),
        [SMEM, HBM] + [VMEM] * 5 + [HBM, VMEM],
        scratch=[
            pltpu.VMEM((ROWS, WIDTH), BF16),
            pltpu.VMEM((256, WIDTH), BF16),
            pltpu.VMEM((256, WIDTH), F32),
            pltpu.VMEM((LANES, 256), F32),
            pltpu.SemaphoreType.DMA((2,)),
        ],
        mib=24,
    )(
        where,
        in_hbm(tokens),
        lengths,
        destination,
        worker_offset,
        positives[None],
        in_gain[None],
        in_hbm(table),
        negatives,
    )
    gain = jnp.where(core == 0, out_gain, jnp.roll(out_gain, 256))[None]
    got, x_rows, gain = lax.optimization_barrier((got, x_rows, gain))

    message = call(forward_body, shape((W_ROWS + REST, LANES)), [VMEM, VMEM])(got, labels)
    line = [message]
    for step in (1, 3, 2):
        line.append(lax.ppermute(message, "user", shifted(FIRST, step)))
    line = [line[0], line[1], line[3], line[2]]
    mid = call(
        collect_body,
        shape((4, W_ROWS + REST, LANES)),
        [SMEM] + [ANY] * 4,
        scratch=[pltpu.SemaphoreType.DMA((4,))],
        out_specs=VMEM,
    )(where, *line).reshape(PIECE, LANES)
    mid, parcels = lax.optimization_barrier((mid, parcels))
    own = {0: mid}
    for step in (1, 3, 2):
        own[step] = lax.ppermute(mid, "user", shifted(SECOND, step))
    other = {}
    for step in (0, 1, 3, 2):
        other[step] = lax.ppermute(own[step], "user", PARTNER)
    own, other = ([d[n] for n in range(4)] for d in (own, other))
    _, parcels = lax.optimization_barrier((own[2], parcels))
    arrived = exchange(parcels.reshape(USERS, MOST, WIDTH), "user").reshape(ROWS, WIDTH)

    layer_half = call(
        half_body,
        (
            shape((ROWS, 256)),
            shape((ROWS, 256), F32),
            shape((256, WIDTH)),
            shape((256, 512)),
            shape((4, 8, LANES), F32),
        ),
        [SMEM] + [ANY] * 5 + [VMEM],
        scratch=[
            pltpu.VMEM((ROWS, WIDTH), BF16),
            pltpu.VMEM((4, PIECE, LANES), BF16),
            pltpu.VMEM((4, ROWS, 256), BF16),
            pltpu.SemaphoreType.DMA((5,)),
        ],
        mib=16,
    )
    u_own, mixed_own, o_own, g_own, near = layer_half(where[4:5], x_rows, *own, cols)
    u_other, mixed_other, o_other, g_other, far = layer_half(where[5:6], x_rows, *other, cols)
    home_out = call(out_body, shape((ROWS, WIDTH)), [VMEM] * 8, mib=8)(
        tokens, u_own, mixed_own, o_own, u_other, mixed_other, o_other, gain
    )

    token_grad, own_terms, sent, own_inner = call(
        loss_body,
        (
            shape((ROWS, WIDTH)),
            shape((PLANE, 32, ROWS)),
            shape((528, ROWS)),
            shape((1, ROWS), F32),
        ),
        [SMEM] + [VMEM] * 5,
        scratch=[pltpu.VMEM((PLANE, 2, 32, ROWS), BF16)],
        mib=16,
    )(core.reshape(1), home_out, table_low, g_own, g_other, cols)
    partner_terms = lax.ppermute(sent, "user", PARTNER)
    pair = call(pair_body, shape((PLANE, 40, ROWS)), [VMEM] * 3)(
        own_terms, own_inner, partner_terms
    )
    pair, arrived = lax.optimization_barrier((pair, arrived))
    plane = exchange(pair, "user", SAME_CORE)

    layer_out = call(
        worker_body,
        shape((256, WIDTH)),
        [SMEM] + [VMEM] * 7 + [ANY] * 8,
        scratch=[
            pltpu.VMEM((4, PIECE, LANES), BF16),
            pltpu.VMEM((4, PIECE, LANES), BF16),
            pltpu.VMEM((4, 256, 256), BF16),
            pltpu.VMEM((4, 256, 256), BF16),
            pltpu.VMEM((256, 256), F32),
            pltpu.VMEM((256, 256), F32),
            pltpu.SemaphoreType.DMA((2, 4)),
        ],
        mib=24,
    )(where, near, far, arrived, in_gain[None], o_own, o_other, gain, *own, *other)

    positive_part, negative_part = call(
        plane_body, (shape((48, 256), F32), shape((256, LANES))), [VMEM]
    )(plane)
    owned = exchange(negative_part.reshape(ITEMS, 16, LANES), "item").reshape(256, LANES)
    item_grad = call(item_body, shape((32, 256), F32), [VMEM] * 5)(
        positive_part, hits, owned, hat_part, table_scale
    ).T
    return (layer_out, token_grad, item_grad)


def solution(mesh):
    return jax.shard_map(
        per_device,
        mesh=mesh,
        in_specs=(
            P(("user", "item"), None),
            P(("user", "item"), None),
            P(("user", "item"), None),
            P(("user", "item"), None),
            P(("user", "item")),
            P(),
            P("item", None),
            P(),
            P("item", None),
            P(),
            P(None, "item"),
        ),
        out_specs=(P(("user", "item"), None), P(("user", "item"), None), P("item", "user")),
        check_vma=False,
    )
```

time: 157 us -> 145 us (0.924); the launches traced: 154 us -> 144 us
  waiting for transfers between devices: 40.2 us -> 17 us
  local copies, waits for them, and re-layouts: 23 us -> 3.35 us
  starting transfers between devices: 51.5 us -> 70.8 us
  blocking collectives: 0 us -> 18.6 us
  Pallas kernels: 21 us -> 33 us
  other arithmetic: 11.9 us -> 0.01 us
  matrix products: 5.28 us -> 0 us
    ppermute x1 -> x10, starting transfers between devices: 9.31 us -> 43.4 us  [the longest x4 24.4 us: per_device(): other[step] = lax.ppermute(own[step], 'user', PARTNER)]
    all_to_all x6 -> x3, waiting for transfers between devices: 38.5 us -> 8.36 us  [exchange(): lax.all_to_all(blocks, axis, 0, 0, tiled=True, axis_index_groups=groups)]
    all_to_all x0 -> x1, blocking collectives: none -> 18.6 us  [exchange(): lax.all_to_all(blocks, axis, 0, 0, tiled=True, axis_index_groups=groups)]
    all_to_all x6 -> x3, starting transfers between devices: 39.9 us -> 25.1 us  [exchange(): lax.all_to_all(blocks, axis, 0, 0, tiled=True, axis_index_groups=groups)]
    pallas_call x4 -> x7, Pallas kernels: 14.4 us -> 26.8 us  [the longest x1 8.7 us: per_device(): call(worker_body, shape((256, WIDTH)), [SMEM] + [VMEM] * 7 + [ANY] * 8, s...]
    ppermute x1 -> x10, waiting for transfers between devices: 0.01 us -> 7.13 us  [the longest x3 4.88 us: per_device(): line.append(lax.ppermute(message, 'user', shifted(FIRST, step)))]
    unnamed x57 -> x30, local copies, waits for them, and re-layouts: 9.82 us -> 3.26 us
    dot_general x3 -> x0, matrix products: 5.28 us -> none  [the longest x1 2.43 us: per_device(): normed = jnp.dot(normed, order, preferred_element_type=F32).astype(BF16)]
  transfers between devices with their start and end apart: 8 -> 14, of which waited for: 5 -> 6; matrix products, arithmetic and copies ran while one was open for 16% -> 0% of each run, Pallas kernels for 12% -> 19%
where the time goes in v4:
time: 145 us; the launch traced here: 144 us
  starting transfers between devices  70.8 us (49%)
  Pallas kernels  33 us (23%)
  blocking collectives  18.6 us (13%)
  waiting for transfers between devices  17 us (12%)
  local copies, waits for them, and re-layouts  3.35 us (2%)
    all_to_all x3, starting transfers between devices, exchange(): lax.all_to_all(blocks, axis, 0, 0, tiled=True, axis_index_groups=groups)  25.1 us
    ppermute x4, starting transfers between devices, per_device(): other[step] = lax.ppermute(own[step], 'user', PARTNER)  24.4 us
    all_to_all x1, blocking collectives, exchange(): lax.all_to_all(blocks, axis, 0, 0, tiled=True, axis_index_groups=groups)  18.6 us
    ppermute x3, starting transfers between devices, per_device(): line.append(lax.ppermute(message, 'user', shifted(FIRST, step)))  9.5 us
    ppermute x3, starting transfers between devices, per_device(): own[step] = lax.ppermute(mid, 'user', shifted(SECOND, step))  9.47 us
    pallas_call x1, Pallas kernels, per_device(): call(worker_body, shape((256, WIDTH)), [SMEM] + [VMEM] * 7 + [ANY] * 8, s...  8.7 us
    all_to_all x3, waiting for transfers between devices, exchange(): lax.all_to_all(blocks, axis, 0, 0, tiled=True, axis_index_groups=groups)  8.36 us
    pallas_call x1, Pallas kernels, per_device(): layer_half(where[5:6], x_rows, *other, cols)  5.14 us
  transfers between devices with their start and end apart: 14, of which 6 were waited for; matrix products, arithmetic and copies ran while one was open for 0% of the time, Pallas kernels for 19%

profile of v4, /device:TPU:1, one launch (start us, length us, event | category | flops | bytes accessed | tf_op | source)
XLA Modules:
  0.0 143.7 jit_solution(15168265576678598229)
XLA Ops:
  0.7 0.1 stack.27.where
  0.7 0.6 copy-done.8
  1.4 2.4 %shard_map.130 = bf16[16,48,128]{2,1,0:T(8,128)(2,1)} custom-call(s32[6]{0:T(128)S(1)} %stack.27.where, s32[16,256]{1,0:T(8,128)S(1)} %copy-done.8, bf16[64,2048]{1,0:T(8,128)(2,1)} %w_ref.1, bf16[64,512]{1,0:T(8,128)(2,1)} %bitcast.30, bf16[256,1024]{1,0:T(8,128)(2,1)} %table_ref.3), custom_call_target="tpu_custom_call" | custom-call | tf_op jit(solution)/shard_map/pallas_call | solution.py:490
  3.8 0.0 copy-start.9
  3.8 15.7 %all-to-all-start = ((bf16[16,48,128]{2,1,0:T(8,128)(2,1)}), bf16[16,48,128]{2,1,0:T(8,128)(2,1)S(1)}, u32[]{:S(2)}, u32[]{:S(2)}) async-start(bf16[16,48,128]{2,1,0:T(8,128)(2,1)} %shard_map.130), calls=%async_computation | async-start | bytes 393216 | tf_op jit(solution)/shard_map/all_to_all | solution.py:465
  19.5 0.0 copy-start.10
  19.6 0.0 copy-start.11
  19.6 0.0 copy-start.12
  19.6 0.0 copy-start.13
  19.6 0.6 copy-done.10
  20.2 0.0 copy-done.13
  20.3 4.5 %shard_map.131 = (bf16[512,1024]{1,0:T(8,128)(2,1)S(1)}, f32[512,128]{1,0:T(8,128)S(1)}, bf16[16,128]{1,0:T(8,128)(2,1)S(1)}, bf16[512,1024]{1,0:T(8,128)(2,1)S(...) custom-call(s32[6]{0:T(128)S(1)} %stack.27.where, ...), custom_call_target="tpu_custom_call" | custom-call | tf_op jit(solution)/shard_map/pallas_call | solution.py:505
  24.7 1.0 copy-done.5
  25.7 0.8 copy-done.6
  26.5 5.5 %all-to-all-done.got = bf16[16,48,128]{2,1,0:T(8,128)(2,1)S(1)} async-done(((bf16[16,48,128]{2,1,0:T(8,128)(2,1)}), bf16[16,48,128]{2,1,0:T(8,128)(2,1)S(1)}, u32[]{:S(2)}, u32[]{:S(2)}) %all-to-all-start) | async-done | bytes 196640 | tf_op jit(solution)/shard_map/all_to_all | solution.py:465
  32.0 0.1 shard_map.132.p0
  32.1 4.6 %collective-permute-start.2 = (bf16[720,128]{1,0:T(8,128)(2,1)S(1)}, bf16[720,128]{1,0:T(8,128)(2,1)S(1)}, u32[]{:S(2)}, u32[]{:S(2)}) collective-permute-start(bf16[720,128]{1,0:T(8,128)(2,1)S(1)} %shard_map.132.p0), channel_id=1, source_target_pairs={{0,384},{128,0},{256,128},{384,256},{32,416},{160,32},{288,160},{4... | collective-permute-start | bytes 552968 | tf_op jit(solution)/shard_map/ppermute | solution.py:543
  36.8 2.3 %collective-permute-start.1 = (bf16[720,128]{1,0:T(8,128)(2,1)S(1)}, bf16[720,128]{1,0:T(8,128)(2,1)S(1)}, u32[]{:S(2)}, u32[]{:S(2)}) collective-permute-start(bf16[720,128]{1,0:T(8,128)(2,1)S(1)} %shard_map.132.p0), channel_id=1, source_target_pairs={{0,256},{128,384},{256,0},{384,128},{32,288},{160,416},{288,32},{4... | collective-permute-start | bytes 552968 | tf_op jit(solution)/shard_map/ppermute | solution.py:543
  39.0 2.6 %collective-permute-start = (bf16[720,128]{1,0:T(8,128)(2,1)S(1)}, bf16[720,128]{1,0:T(8,128)(2,1)S(1)}, u32[]{:S(2)}, u32[]{:S(2)}) collective-permute-start(bf16[720,128]{1,0:T(8,128)(2,1)S(1)} %shard_map.132.p0), channel_id=1, source_target_pairs={{0,128},{128,256},{256,384},{384,0},{32,160},{160,288},{288,416},{... | collective-permute-start | bytes 552968 | tf_op jit(solution)/shard_map/ppermute | solution.py:543
  41.7 2.9 %collective-permute-done.1.p2 = bf16[720,128]{1,0:T(8,128)(2,1)S(1)} collective-permute-done((bf16[720,128]{1,0:T(8,128)(2,1)S(1)}, bf16[720,128]{1,0:T(8,128)(2,1)S(1)}, u32[]{:S(2)}, u32[]{:S(2)}) %collective-permute-start.1) | collective-permute-done | bytes 184352 | tf_op jit(solution)/shard_map/ppermute | solution.py:543
  44.6 2.0 %collective-permute-done.p1 = bf16[720,128]{1,0:T(8,128)(2,1)S(1)} collective-permute-done((bf16[720,128]{1,0:T(8,128)(2,1)S(1)}, bf16[720,128]{1,0:T(8,128)(2,1)S(1)}, u32[]{:S(2)}, u32[]{:S(2)}) %collective-permute-start) | collective-permute-done | bytes 184352 | tf_op jit(solution)/shard_map/ppermute | solution.py:543
  46.5 1.5 %shard_map.133 = bf16[4,720,128]{2,1,0:T(8,128)(2,1)S(1)} custom-call(s32[6]{0:T(128)S(1)} %stack.27.where, bf16[720,128]{1,0:T(8,128)(2,1)S(1)} %shard_map.132.p0, bf16[720,128]{1,0:T(8,128)(2,1)S(1)} %collective-permute-done.p1, bf16[720,128]{1,0:T(8,128)(2,1)S(1)} %collective-permute-done.1.p2, bf16[720,128]{1,0:T(8,128)(2,1)S(1)} %collective-permute-done.2.p3), custom_call_target="tpu_custom_call" | custom-call | tf_op jit(solution)/shard_map/pallas_call | solution.py:545
  48.1 4.7 %collective-permute-start.5 = (bf16[2880,128]{1,0:T(8,128)(2,1)S(1)}, bf16[2880,128]{1,0:T(8,128)(2,1)}, u32[]{:S(2)}, u32[]{:S(2)}) collective-permute-start(bf16[2880,128]{1,0:T(8,128)(2,1)S(1)} %bitcast.16), channel_id=1, source_target_pairs={{0,96},{32,0},{64,32},{96,64},{128,224},{160,128},{192,160},{224,1... | collective-permute-start | bytes 2211848 | tf_op jit(solution)/shard_map/ppermute | solution.py:555
  52.8 2.3 %collective-permute-start.4 = (bf16[2880,128]{1,0:T(8,128)(2,1)S(1)}, bf16[2880,128]{1,0:T(8,128)(2,1)}, u32[]{:S(2)}, u32[]{:S(2)}) collective-permute-start(bf16[2880,128]{1,0:T(8,128)(2,1)S(1)} %bitcast.17), channel_id=1, source_target_pairs={{0,64},{32,96},{64,0},{96,32},{128,192},{160,224},{192,128},{224,1... | collective-permute-start | bytes 2211848 | tf_op jit(solution)/shard_map/ppermute | solution.py:555
  55.1 2.5 %collective-permute-start.3 = (bf16[2880,128]{1,0:T(8,128)(2,1)S(1)}, bf16[2880,128]{1,0:T(8,128)(2,1)}, u32[]{:S(2)}, u32[]{:S(2)}) collective-permute-start(bf16[2880,128]{1,0:T(8,128)(2,1)S(1)} %bitcast.18), channel_id=1, source_target_pairs={{0,32},{32,64},{64,96},{96,0},{128,160},{160,192},{192,224},{224,1... | collective-permute-start | bytes 2211848 | tf_op jit(solution)/shard_map/ppermute | solution.py:555
  57.6 9.2 %collective-permute-start.6 = (bf16[2880,128]{1,0:T(8,128)(2,1)S(1)}, bf16[2880,128]{1,0:T(8,128)(2,1)}, u32[]{:S(2)}, u32[]{:S(2)}) collective-permute-start(bf16[2880,128]{1,0:T(8,128)(2,1)S(1)} %bitcast.19), channel_id=1, source_target_pairs={{0,16},{16,0},{32,48},{48,32},{64,80},{80,64},{96,112},{112,96},{1... | collective-permute-start | bytes 2211848 | tf_op jit(solution)/shard_map/ppermute | solution.py:558
  66.8 2.2 %collective-permute-done.5.p3.rest_3_ = bf16[2880,128]{1,0:T(8,128)(2,1)} collective-permute-done((bf16[2880,128]{1,0:T(8,128)(2,1)S(1)}, bf16[2880,128]{1,0:T(8,128)(2,1)}, u32[]{:S(2)}, u32[]{:S(2)}) %collective-permute-start.5) | collective-permute-done | bytes 737312 | tf_op jit(solution)/shard_map/ppermute | solution.py:555
  69.1 9.2 %collective-permute-start.9 = (bf16[2880,128]{1,0:T(8,128)(2,1)}, bf16[2880,128]{1,0:T(8,128)(2,1)}, u32[]{:S(2)}, u32[]{:S(2)}) collective-permute-start(bf16[2880,128]{1,0:T(8,128)(2,1)} %collective-permute-done.5.p3.rest_3_), channel_id=1, source_target_pairs={{0,16},{16,0},{32,48},{48,32},{64,80},{80,64},{96,112},{112,96},{1... | collective-permute-start | bytes 2211848 | tf_op jit(solution)/shard_map/ppermute | solution.py:558
  78.3 1.9 %collective-permute-start.8 = (bf16[2880,128]{1,0:T(8,128)(2,1)}, bf16[2880,128]{1,0:T(8,128)(2,1)}, u32[]{:S(2)}, u32[]{:S(2)}) collective-permute-start(bf16[2880,128]{1,0:T(8,128)(2,1)} %collective-permute-done.4.p2.rest_2_), channel_id=1, source_target_pairs={{0,16},{16,0},{32,48},{48,32},{64,80},{80,64},{96,112},{112,96},{1... | collective-permute-start | bytes 2211848 | tf_op jit(solution)/shard_map/ppermute | solution.py:558
  80.2 4.0 %collective-permute-start.7 = (bf16[2880,128]{1,0:T(8,128)(2,1)}, bf16[2880,128]{1,0:T(8,128)(2,1)}, u32[]{:S(2)}, u32[]{:S(2)}) collective-permute-start(bf16[2880,128]{1,0:T(8,128)(2,1)} %collective-permute-done.3.p1.rest_1_), channel_id=1, source_target_pairs={{0,16},{16,0},{32,48},{48,32},{64,80},{80,64},{96,112},{112,96},{1... | collective-permute-start | bytes 2211848 | tf_op jit(solution)/shard_map/ppermute | solution.py:558
  84.3 4.7 %all-to-all-start.1 = ((bf16[32,16,1024]{2,1,0:T(8,128)(2,1)}), bf16[32,16,1024]{2,1,0:T(8,128)(2,1)S(1)}, u32[]{:S(2)}, u32[]{:S(2)}) async-start(bf16[32,16,1024]{2,1,0:T(8,128)(2,1)} %bitcast.23), calls=%async_computation.1 | async-start | bytes 2097152 | tf_op jit(solution)/shard_map/all_to_all | solution.py:465
  88.9 4.5 %shard_map.134 = (bf16[512,256]{1,0:T(8,128)(2,1)S(1)}, f32[512,256]{1,0:T(8,128)S(1)}, bf16[256,1024]{1,0:T(8,128)(2,1)S(1)}, bf16[256,512]{1,0:T(8,128)(2,1)S(1)}, f32[4,8,128]{2,1,0:T(8,128)S(1)}) custom-call(s32[1]{0:T(128)} %bitcast.4.where, bf16[512,1024]{1,0:T(8,128)(2,1)S(1)} %get-tuple-element.36.x_ref, bf16[2880,128]{1,0:T(8,128)(2,1)S(1)} %bitcast.20, ...), custom_call_target="tpu_custom_call" | custom-call | tf_op jit(solution)/shard_map/pallas_call | solution.py:581
  93.4 0.0 copy-start.1
  93.4 0.0 copy-start
  93.5 5.1 %shard_map.135 = (bf16[512,256]{1,0:T(8,128)(2,1)S(1)}, f32[512,256]{1,0:T(8,128)S(1)}, bf16[256,1024]{1,0:T(8,128)(2,1)S(1)}, bf16[256,512]{1,0:T(8,128)(2,1)S(1)}, f32[4,8,128]{2,1,0:T(8,128)S(1)}) custom-call(s32[1]{0:T(128)} %bitcast.5.where, bf16[512,1024]{1,0:T(8,128)(2,1)S(1)} %get-tuple-element.36.x_ref, ...), custom_call_target="tpu_custom_call" | custom-call | tf_op jit(solution)/shard_map/pallas_call | solution.py:582
  98.7 0.0 copy-start.7
  98.7 1.0 shard_map.136.out_ref
  99.7 0.2 copy-done.7
  99.9 3.4 %shard_map.137 = (bf16[512,1024]{1,0:T(8,128)(2,1)}, bf16[16,32,512]{2,1,0:T(8,128)(2,1)S(1)}, bf16[528,512]{1,0:T(8,128)(2,1)S(1)}, f32[1,512]{1,0:T(1,128)S(1)}) custom-call(s32[1]{0:T(128)} %bitcast.1.core, bf16[512,1024]{1,0:T(8,128)(2,1)S(1)} %shard_map.136.out_ref, bf16[256,1024]{1,0:T(8,128)(2,1)S(1)} %copy-done.7, ...), custom_call_target="tpu_custom_call" | custom-call | tf_op jit(solution)/shard_map/pallas_call | solution.py:587
  103.3 2.3 %collective-permute-start.10 = (bf16[528,512]{1,0:T(8,128)(2,1)S(1)}, bf16[528,512]{1,0:T(8,128)(2,1)S(1)}, u32[]{:S(2)}, u32[]{:S(2)}) collective-permute-start(bf16[528,512]{1,0:T(8,128)(2,1)S(1)} %get-tuple-element.56), channel_id=1, source_target_pairs={{0,16},{16,0},{32,48},{48,32},{64,80},{80,64},{96,112},{112,96},{1... | collective-permute-start | bytes 1622024 | tf_op jit(solution)/shard_map/ppermute | solution.py:599
  105.6 1.5 %collective-permute-done.10.got_ref = bf16[528,512]{1,0:T(8,128)(2,1)S(1)} collective-permute-done((bf16[528,512]{1,0:T(8,128)(2,1)S(1)}, bf16[528,512]{1,0:T(8,128)(2,1)S(1)}, u32[]{:S(2)}, u32[]{:S(2)}) %collective-permute-start.10) | collective-permute-done | bytes 540704 | tf_op jit(solution)/shard_map/ppermute | solution.py:599
  107.2 0.1 shard_map.138
  107.3 18.6 %all_to_all.20.got_ref = bf16[16,40,512]{2,1,0:T(8,128)(2,1)S(1)} all-to-all(bf16[16,40,512]{2,1,0:T(8,128)(2,1)S(1)} %shard_map.138), channel_id=1, replica_groups={{0,32,64,96,128,160,192,224,256,288,320,352,384,416,448,480},{16,48,80,..., dimensions={0} | all-to-all | bytes 1310720 | tf_op jit(solution)/shard_map/all_to_all | solution.py:465
  125.9 0.8 shard_map.140
  126.7 4.7 %all-to-all-start.3 = ((bf16[16,16,128]{2,1,0:T(8,128)(2,1)}), bf16[16,16,128]{2,1,0:T(8,128)(2,1)S(1)}, u32[]{:S(2)}, u32[]{:S(2)}) async-start(bf16[16,16,128]{2,1,0:T(8,128)(2,1)} %bitcast.13), calls=%async_computation.3 | async-start | bytes 131072 | tf_op jit(solution)/shard_map/all_to_all | solution.py:465
  131.4 8.7 %shard_map.139 = bf16[256,1024]{1,0:T(8,128)(2,1)} custom-call(s32[6]{0:T(128)S(1)} %stack.27.where, f32[4,8,128]{2,1,0:T(8,128)S(1)} %get-tuple-element.42.near_ref, f32[4,8,128]{2,1,0:T(8,128)S(1)} %get-tuple-element.43.far_ref, bf16[512,1024]{1,0:T(8,128)(2,1)S(1)} %bitcast.22, f32[1,1024]{1,0:T(1,128)S(1)} %bitcast.28, bf16[256,1024]{1,0:T(8,128)(2,1)S(1)} %copy-done.2, ...), custom_call_target="tpu_custom_call" | custom-call | tf_op jit(solution)/shard_map/pallas_call | solution.py:606
  140.1 2.8 %all-to-all-done.3 = bf16[16,16,128]{2,1,0:T(8,128)(2,1)S(1)} async-done(((bf16[16,16,128]{2,1,0:T(8,128)(2,1)}), bf16[16,16,128]{2,1,0:T(8,128)(2,1)S(1)}, u32[]{:S(2)}, u32[]{:S(2)}) %all-to-all-start.3) | async-done | bytes 65568 | tf_op jit(solution)/shard_map/all_to_all | solution.py:465
  142.9 0.8 shard_map.141
  (26 shorter events, 0.1 us)
Async XLA Ops:
  0.6 0.7 copy-start.8
  3.8 15.8 %copy-start.9 = (f32[1024]{0:T(1024)S(1)}, f32[1024]{0:T(1024)}, u32[]{:S(2)}) copy-start(f32[1024]{0:T(1024)} %param.18) | copy-start | bytes 12292
  3.8 28.2 %all-to-all-start = ((bf16[16,48,128]{2,1,0:T(8,128)(2,1)}), bf16[16,48,128]{2,1,0:T(8,128)(2,1)S(1)}, u32[]{:S(2)}, u32[]{:S(2)}) async-start(bf16[16,48,128]{2,1,0:T(8,128)(2,1)} %shard_map.130), calls=%async_computation | async-start | bytes 393216 | tf_op jit(solution)/shard_map/all_to_all | solution.py:465
  19.5 0.7 copy-start.10
  19.6 0.7 copy-start.11
  19.6 0.7 copy-start.12
  19.6 0.7 copy-start.13
  20.3 6.2 %copy-start.14 = (f32[512]{0:T(512)S(1)}, f32[512]{0:T(512)}, u32[]{:S(2)}) copy-start(f32[512]{0:T(512)} %param.20) | copy-start | bytes 6148
  24.7 1.0 copy-start.5
  25.7 0.8 copy-start.6
  32.1 9.5 %collective-permute-start.2 = (bf16[720,128]{1,0:T(8,128)(2,1)S(1)}, bf16[720,128]{1,0:T(8,128)(2,1)S(1)}, u32[]{:S(2)}, u32[]{:S(2)}) collective-permute-start(bf16[720,128]{1,0:T(8,128)(2,1)S(1)} %shard_map.132.p0), channel_id=1, source_target_pairs={{0,384},{128,0},{256,128},{384,256},{32,416},{160,32},{288,160},{4... | collective-permute-start | bytes 552968 | tf_op jit(solution)/shard_map/ppermute | solution.py:543
  36.8 7.8 %collective-permute-start.1 = (bf16[720,128]{1,0:T(8,128)(2,1)S(1)}, bf16[720,128]{1,0:T(8,128)(2,1)S(1)}, u32[]{:S(2)}, u32[]{:S(2)}) collective-permute-start(bf16[720,128]{1,0:T(8,128)(2,1)S(1)} %shard_map.132.p0), channel_id=1, source_target_pairs={{0,256},{128,384},{256,0},{384,128},{32,288},{160,416},{288,32},{4... | collective-permute-start | bytes 552968 | tf_op jit(solution)/shard_map/ppermute | solution.py:543
  39.0 7.5 %collective-permute-start = (bf16[720,128]{1,0:T(8,128)(2,1)S(1)}, bf16[720,128]{1,0:T(8,128)(2,1)S(1)}, u32[]{:S(2)}, u32[]{:S(2)}) collective-permute-start(bf16[720,128]{1,0:T(8,128)(2,1)S(1)} %shard_map.132.p0), channel_id=1, source_target_pairs={{0,128},{128,256},{256,384},{384,0},{32,160},{160,288},{288,416},{... | collective-permute-start | bytes 552968 | tf_op jit(solution)/shard_map/ppermute | solution.py:543
  48.1 21.0 %collective-permute-start.5 = (bf16[2880,128]{1,0:T(8,128)(2,1)S(1)}, bf16[2880,128]{1,0:T(8,128)(2,1)}, u32[]{:S(2)}, u32[]{:S(2)}) collective-permute-start(bf16[2880,128]{1,0:T(8,128)(2,1)S(1)} %bitcast.16), channel_id=1, source_target_pairs={{0,96},{32,0},{64,32},{96,64},{128,224},{160,128},{192,160},{224,1... | collective-permute-start | bytes 2211848 | tf_op jit(solution)/shard_map/ppermute | solution.py:555
  52.8 25.5 %collective-permute-start.4 = (bf16[2880,128]{1,0:T(8,128)(2,1)S(1)}, bf16[2880,128]{1,0:T(8,128)(2,1)}, u32[]{:S(2)}, u32[]{:S(2)}) collective-permute-start(bf16[2880,128]{1,0:T(8,128)(2,1)S(1)} %bitcast.17), channel_id=1, source_target_pairs={{0,64},{32,96},{64,0},{96,32},{128,192},{160,224},{192,128},{224,1... | collective-permute-start | bytes 2211848 | tf_op jit(solution)/shard_map/ppermute | solution.py:555
  55.1 25.1 %collective-permute-start.3 = (bf16[2880,128]{1,0:T(8,128)(2,1)S(1)}, bf16[2880,128]{1,0:T(8,128)(2,1)}, u32[]{:S(2)}, u32[]{:S(2)}) collective-permute-start(bf16[2880,128]{1,0:T(8,128)(2,1)S(1)} %bitcast.18), channel_id=1, source_target_pairs={{0,32},{32,64},{64,96},{96,0},{128,160},{160,192},{192,224},{224,1... | collective-permute-start | bytes 2211848 | tf_op jit(solution)/shard_map/ppermute | solution.py:555
  57.6 35.8 %collective-permute-start.6 = (bf16[2880,128]{1,0:T(8,128)(2,1)S(1)}, bf16[2880,128]{1,0:T(8,128)(2,1)}, u32[]{:S(2)}, u32[]{:S(2)}) collective-permute-start(bf16[2880,128]{1,0:T(8,128)(2,1)S(1)} %bitcast.19), channel_id=1, source_target_pairs={{0,16},{16,0},{32,48},{48,32},{64,80},{80,64},{96,112},{112,96},{1... | collective-permute-start | bytes 2211848 | tf_op jit(solution)/shard_map/ppermute | solution.py:558
  69.1 24.4 %collective-permute-start.9 = (bf16[2880,128]{1,0:T(8,128)(2,1)}, bf16[2880,128]{1,0:T(8,128)(2,1)}, u32[]{:S(2)}, u32[]{:S(2)}) collective-permute-start(bf16[2880,128]{1,0:T(8,128)(2,1)} %collective-permute-done.5.p3.rest_3_), channel_id=1, source_target_pairs={{0,16},{16,0},{32,48},{48,32},{64,80},{80,64},{96,112},{112,96},{1... | collective-permute-start | bytes 2211848 | tf_op jit(solution)/shard_map/ppermute | solution.py:558
  78.3 15.2 %collective-permute-start.8 = (bf16[2880,128]{1,0:T(8,128)(2,1)}, bf16[2880,128]{1,0:T(8,128)(2,1)}, u32[]{:S(2)}, u32[]{:S(2)}) collective-permute-start(bf16[2880,128]{1,0:T(8,128)(2,1)} %collective-permute-done.4.p2.rest_2_), channel_id=1, source_target_pairs={{0,16},{16,0},{32,48},{48,32},{64,80},{80,64},{96,112},{112,96},{1... | collective-permute-start | bytes 2211848 | tf_op jit(solution)/shard_map/ppermute | solution.py:558
  80.2 13.3 %collective-permute-start.7 = (bf16[2880,128]{1,0:T(8,128)(2,1)}, bf16[2880,128]{1,0:T(8,128)(2,1)}, u32[]{:S(2)}, u32[]{:S(2)}) collective-permute-start(bf16[2880,128]{1,0:T(8,128)(2,1)} %collective-permute-done.3.p1.rest_1_), channel_id=1, source_target_pairs={{0,16},{16,0},{32,48},{48,32},{64,80},{80,64},{96,112},{112,96},{1... | collective-permute-start | bytes 2211848 | tf_op jit(solution)/shard_map/ppermute | solution.py:558
  84.3 23.1 %all-to-all-start.1 = ((bf16[32,16,1024]{2,1,0:T(8,128)(2,1)}), bf16[32,16,1024]{2,1,0:T(8,128)(2,1)S(1)}, u32[]{:S(2)}, u32[]{:S(2)}) async-start(bf16[32,16,1024]{2,1,0:T(8,128)(2,1)} %bitcast.23), calls=%async_computation.1 | async-start | bytes 2097152 | tf_op jit(solution)/shard_map/all_to_all | solution.py:465
  93.4 5.2 %copy-start.1 = (bf16[256,1024]{1,0:T(8,128)(2,1)}, bf16[256,1024]{1,0:T(8,128)(2,1)S(1)}, u32[]{:S(2)}) copy-start(bf16[256,1024]{1,0:T(8,128)(2,1)S(1)} %get-tuple-element.46.o0) | copy-start | bytes 1572868
  93.4 5.2 %copy-start = (bf16[512,1024]{1,0:T(8,128)(2,1)S(1)}, bf16[512,1024]{1,0:T(8,128)(2,1)}, u32[]{:S(2)}) copy-start(bf16[512,1024]{1,0:T(8,128)(2,1)} %tok_ref.3) | copy-start | bytes 3145732
  98.6 1.0 copy-start.3
  98.7 1.2 copy-start.7
  103.3 3.9 %collective-permute-start.10 = (bf16[528,512]{1,0:T(8,128)(2,1)S(1)}, bf16[528,512]{1,0:T(8,128)(2,1)S(1)}, u32[]{:S(2)}, u32[]{:S(2)}) collective-permute-start(bf16[528,512]{1,0:T(8,128)(2,1)S(1)} %get-tuple-element.56), channel_id=1, source_target_pairs={{0,16},{16,0},{32,48},{48,32},{64,80},{80,64},{96,112},{112,96},{1... | collective-permute-start | bytes 1622024 | tf_op jit(solution)/shard_map/ppermute | solution.py:599
  107.3 24.0 %copy-start.4 = (bf16[256,1024]{1,0:T(8,128)(2,1)S(1)}, bf16[256,1024]{1,0:T(8,128)(2,1)}, u32[]{:S(2)}) copy-start(bf16[256,1024]{1,0:T(8,128)(2,1)} %copy-done.3) | copy-start | bytes 1572868
  125.9 5.5 %copy-start.2 = (bf16[256,1024]{1,0:T(8,128)(2,1)S(1)}, bf16[256,1024]{1,0:T(8,128)(2,1)}, u32[]{:S(2)}) copy-start(bf16[256,1024]{1,0:T(8,128)(2,1)} %copy-done.1) | copy-start | bytes 1572868
  126.7 16.3 %all-to-all-start.3 = ((bf16[16,16,128]{2,1,0:T(8,128)(2,1)}), bf16[16,16,128]{2,1,0:T(8,128)(2,1)S(1)}, u32[]{:S(2)}, u32[]{:S(2)}) async-start(bf16[16,16,128]{2,1,0:T(8,128)(2,1)} %bitcast.13), calls=%async_computation.3 | async-start | bytes 131072 | tf_op jit(solution)/shard_map/all_to_all | solution.py:465

commit v5 on v4

--- a/solution.py
+++ b/solution.py
@@ -202,32 +202,21 @@
 
 def forward_body(got, label, out):
     for i in range(ITEMS):
-        out[i * 32 : (i + 1) * 32, :] = got[i, 0:32, :]
+        out[0, i * 32 : (i + 1) * 32, :] = got[i, 0:32, :]
     left = lax.broadcasted_iota(jnp.int32, (8, LANES), 1) < 64
     for b in range(8):
         even, odd = got[2 * b, 32:40, :].astype(F32), got[2 * b + 1, 32:40, :].astype(F32)
         top = jnp.where(left, even, pltpu.roll(odd, 64, 1))
         bottom = jnp.where(left, pltpu.roll(even, 64, 1), odd)
-        out[W_ROWS + b * 16 : W_ROWS + (b + 1) * 16, :] = jnp.concatenate(
+        out[0, W_ROWS + b * 16 : W_ROWS + (b + 1) * 16, :] = jnp.concatenate(
             [top, bottom], axis=0
         ).astype(BF16)
     quads = got[:, 40:48, :].astype(F32)
     for b in range(4):
-        out[W_ROWS + 128 + b * 16 : W_ROWS + 144 + b * 16, :] = quads[:, b, :].astype(BF16)
-    out[W_ROWS + 192 : W_ROWS + 208, :] = label[...]
-
-
-def collect_body(where, p0, p1, p2, p3, out_ref, sems):
-    copies = [
-        pltpu.make_async_copy(
-            p, out_ref.at[lax.rem(where[5] + 4 - n, 4)], sems.at[n]
-        )
-        for n, p in enumerate((p0, p1, p2, p3))
-    ]
-    for copy in copies:
-        copy.start()
-    for copy in copies:
-        copy.wait()
+        out[0, W_ROWS + 128 + b * 16 : W_ROWS + 144 + b * 16, :] = quads[:, b, :].astype(BF16)
+    out[0, W_ROWS + 192 : W_ROWS + 208, :] = label[...]
+    for g in range(1, 4):
+        out[g] = out[0]
 
 
 def fetches(pieces, w, sems):
@@ -238,8 +227,8 @@
     return lax.rem(position + 4 - n, 4)
 
 
-def project(x, w, n):
-    parts = [w[n, i * 720 : i * 720 + W_ROWS, :] for i in range(4)]
+def project(x, w):
+    parts = [w[i * 720 : i * 720 + W_ROWS, :] for i in range(4)]
     both = jnp.concatenate(
         [jnp.concatenate(parts[0:2], axis=0), jnp.concatenate(parts[2:4], axis=0)], axis=1
     )
@@ -261,51 +250,35 @@
             mixed_ref[lo:hi, d0:d1] = dot(weights, v[at:hi, d0:d1])
 
 
-def half_body(
-    where,
-    x_ref,
-    p0,
-    p1,
-    p2,
-    p3,
-    cols_ref,
-    u_ref,
-    mixed_ref,
-    o_ref,
-    g_ref,
-    label_ref,
-    x,
-    w,
-    act,
-    sems,
-):
-    copies = fetches((p0, p1, p2, p3), w, sems)
-    first_copy = pltpu.make_async_copy(x_ref, x, sems.at[4])
-    first_copy.start()
-    for copy in copies:
-        copy.start()
-    first_copy.wait()
-    for n, copy in enumerate(copies):
-        copy.wait()
-        kind = kind_of(where[0], n)
-        act[kind] = project(x[...], w, n)
-        row = pl.multiple_of(kind * 64, 64)
-
-        def columns(at):
-            return jnp.concatenate(
-                [w[n, i * 720 + at : i * 720 + at + 16, :] for i in range(4)], axis=0
-            )
-
-        for b in range(8):
-            o_ref[pl.ds(row, 64), b * LANES : (b + 1) * LANES] = columns(W_ROWS + b * 16)
-        for b in range(4):
-            g_ref[pl.ds(row, 64), b * LANES : (b + 1) * LANES] = columns(W_ROWS + 128 + b * 16)
-        labels = [
-            w[n, i * 720 + W_ROWS + 192 : (i + 1) * 720, :].astype(F32)[0:1, :] for i in range(4)
-        ]
-        label_ref[kind] = jnp.concatenate(labels + [jnp.zeros((4, LANES), F32)], axis=0)
-    u_ref[...] = act[0]
-    attend(act, cols_ref[:, 0:1].astype(jnp.int32), mixed_ref)
+def project_body(x_ref, w, act_ref, o_ref, g_ref, label_ref):
+    act_ref[...] = project(x_ref[...], w)
+
+    def columns(at):
+        return jnp.concatenate(
+            [w[i * 720 + at : i * 720 + at + 16, :] for i in range(4)], axis=0
+        )
+
+    for b in range(8):
+        o_ref[:, b * LANES : (b + 1) * LANES] = columns(W_ROWS + b * 16)
+    for b in range(4):
+        g_ref[:, b * LANES : (b + 1) * LANES] = columns(W_ROWS + 128 + b * 16)
+    labels = [
+        w[i * 720 + W_ROWS + 192 : (i + 1) * 720, :].astype(F32)[0:1, :] for i in range(4)
+    ]
+    label_ref[...] = jnp.concatenate(labels + [jnp.zeros((4, LANES), F32)], axis=0)
+
+
+def finish_body(where, tok_ref, cols_ref, gain_ref, *rest):
+    acts, parts = rest[:8], rest[8:16]
+    out_ref, o0, o1, act, m0, m1 = rest[16:]
+    first = cols_ref[:, 0:1].astype(jnp.int32)
+    for half, (o, m) in enumerate(((o0, m0), (o1, m1))):
+        for n in range(4):
+            kind = kind_of(where[4 + half], n)
+            act[half, kind] = acts[4 * half + n][...]
+            o[pl.ds(pl.multiple_of(kind * 64, 64), 64), :] = parts[4 * half + n][...]
+        attend(act.at[half], first, m)
+    out_ref[...] = gated_out(tok_ref[...], act.at[0, 0], m0, o0, act.at[1, 0], m1, o1, gain_ref)
 
 
 def gated_out(rows, u0, m0, o0, u1, m1, o1, gain_ref):
@@ -323,12 +296,9 @@
     return (rows.astype(F32) + delta).astype(BF16)
 
 
-def out_body(tok_ref, u0, m0, o0, u1, m1, o1, gain_ref, out_ref):
-    out_ref[...] = gated_out(tok_ref[...], u0, m0, o0, u1, m1, o1, gain_ref)
-
-
-def worker_body(where, near_ref, far_ref, got_ref, in_gain, o0, o1, gain_ref, *rest):
-    pieces, (out_ref, w0, w1, a0, a1, m0, m1, sems) = rest[:8], rest[8:]
+def worker_body(where, got_ref, in_gain, o0, o1, gain_ref, *rest):
+    labels, pieces = rest[:8], rest[8:16]
+    out_ref, w0, w1, a0, a1, m0, m1, sems = rest[16:]
     core, user = where[1], where[3]
     copies = (
         fetches(pieces[:4], w0, sems.at[0]),
@@ -341,13 +311,14 @@
     slot = lax.broadcasted_iota(jnp.int32, (1, ROWS), 1)
     peer = slot // MOST
     x, y, c = peer // 8, peer // 2 % 4, peer % 2
-    spot = jnp.where(c == 0, y * 8 + x, x * 8 + y)
+    outer, inner = jnp.where(c == 0, y, x), jnp.where(c == 0, x, y)
 
     def of_peer(at):
         total = 0.0
-        for ref, mine in ((near_ref, c == core), (far_ref, c != core)):
-            labels = ref[...].reshape(32, LANES)
-            value = jnp.sum(jnp.where(lane == at, labels, 0.0), axis=1, keepdims=True)
+        for half, mine in ((0, c == core), (1, c != core)):
+            table = jnp.concatenate([r[...] for r in labels[4 * half : 4 * half + 4]], axis=0)
+            value = jnp.sum(jnp.where(lane == at, table, 0.0), axis=1, keepdims=True)
+            spot = lax.rem(where[4 + half] + 4 - outer, 4) * 8 + inner
             total = total + jnp.sum(
                 jnp.where((sub == spot) & mine, value, 0.0), axis=0, keepdims=True
             )
@@ -367,24 +338,30 @@
     ):
         for n, copy in enumerate(group):
             copy.wait()
-            act[kind_of(position, n)] = project(moved, w, n)
+            act[kind_of(position, n)] = project(moved, w.at[n])
         attend(act, first, mixed)
     out_ref[...] = gated_out(rows, a0.at[0], m0, o0, a1.at[0], m1, o1, gain_ref)
 
 
-def loss_body(core, out_ref, low_ref, g0_ref, g1_ref, cols_ref, grad_ref, own_ref, send_ref, own_inner, terms):
-    c = core[0]
-
-    g0, g1 = g0_ref[...].astype(F32), g1_ref[...].astype(F32)
+def loss_body(where, out_ref, low_ref, cols_ref, *rest):
+    groups = rest[:8]
+    grad_ref, own_ref, send_ref, own_inner, terms = rest[8:]
+    c = where[1]
+
+    row = lax.broadcasted_iota(jnp.int32, (256, 256), 0)
+    col = lax.broadcasted_iota(jnp.int32, (256, 256), 1)
+    halves = []
+    for half in range(2):
+        taken = lax.rem(where[4 + half] + 4 - row % 16 // 4, 4) * 64 + row % 4 * 16 + row // 16
+        swap = jnp.where(col == taken, 1.0, 0.0).astype(BF16)
+        raw = jnp.concatenate([r[...] for r in groups[4 * half : 4 * half + 4]], axis=0)
+        halves.append(dot(swap, raw))
+    g0, g1 = halves
     size = (jnp.sum(g0 * g0, axis=1, keepdims=True) + jnp.sum(g1 * g1, axis=1, keepdims=True)) / WIDTH
     scale = lax.rsqrt(size + scale_epsilon)
     g0, g1 = (g0 * scale).astype(BF16), (g1 * scale).astype(BF16)
     here = c == 0
-    both = jnp.concatenate([jnp.where(here, g0, g1), jnp.where(here, g1, g0)], axis=1)
-    row = lax.broadcasted_iota(jnp.int32, (256, 256), 0)
-    col = lax.broadcasted_iota(jnp.int32, (256, 256), 1)
-    swap = jnp.where(col == (row % 16) * 16 + row // 16, 1.0, 0.0).astype(BF16)
-    group = dot(swap, both).astype(BF16)
+    group = jnp.concatenate([jnp.where(here, g0, g1), jnp.where(here, g1, g0)], axis=1)
     rows = jnp.concatenate([low_ref[...], group], axis=0)
 
     out = out_ref[...].astype(F32)
@@ -537,52 +514,39 @@
     gain = jnp.where(core == 0, out_gain, jnp.roll(out_gain, 256))[None]
     got, x_rows, gain = lax.optimization_barrier((got, x_rows, gain))
 
-    message = call(forward_body, shape((W_ROWS + REST, LANES)), [VMEM, VMEM])(got, labels)
-    line = [message]
-    for step in (1, 3, 2):
-        line.append(lax.ppermute(message, "user", shifted(FIRST, step)))
-    line = [line[0], line[1], line[3], line[2]]
-    mid = call(
-        collect_body,
-        shape((4, W_ROWS + REST, LANES)),
-        [SMEM] + [ANY] * 4,
-        scratch=[pltpu.SemaphoreType.DMA((4,))],
-        out_specs=VMEM,
-    )(where, *line).reshape(PIECE, LANES)
+    message = call(forward_body, shape((4, W_ROWS + REST, LANES)), [VMEM, VMEM])(got, labels)
+    mid = exchange(message, "user", FIRST).reshape(PIECE, LANES)
     mid, parcels = lax.optimization_barrier((mid, parcels))
-    own = {0: mid}
+    own, other = {0: mid}, {}
     for step in (1, 3, 2):
         own[step] = lax.ppermute(mid, "user", shifted(SECOND, step))
-    other = {}
     for step in (0, 1, 3, 2):
         other[step] = lax.ppermute(own[step], "user", PARTNER)
-    own, other = ([d[n] for n in range(4)] for d in (own, other))
-    _, parcels = lax.optimization_barrier((own[2], parcels))
     arrived = exchange(parcels.reshape(USERS, MOST, WIDTH), "user").reshape(ROWS, WIDTH)
 
-    layer_half = call(
-        half_body,
-        (
-            shape((ROWS, 256)),
-            shape((ROWS, 256), F32),
-            shape((256, WIDTH)),
-            shape((256, 512)),
-            shape((4, 8, LANES), F32),
-        ),
-        [SMEM] + [ANY] * 5 + [VMEM],
+    layer_part = call(
+        project_body,
+        (shape((ROWS, 256)), shape((64, WIDTH)), shape((64, 512)), shape((8, LANES), F32)),
+        [VMEM] * 2,
+        mib=8,
+    )
+    parts = []
+    for pieces in (own, other):
+        for n in range(4):
+            parts.append(layer_part(x_rows, pieces[n]))
+    acts, o_parts, groups, tables = zip(*parts)
+    pieces = [own[n] for n in range(4)] + [other[n] for n in range(4)]
+    home_out, o_own, o_other = call(
+        finish_body,
+        (shape((ROWS, WIDTH)), shape((256, WIDTH)), shape((256, WIDTH))),
+        [SMEM] + [VMEM] * 19,
         scratch=[
-            pltpu.VMEM((ROWS, WIDTH), BF16),
-            pltpu.VMEM((4, PIECE, LANES), BF16),
-            pltpu.VMEM((4, ROWS, 256), BF16),
-            pltpu.SemaphoreType.DMA((5,)),
+            pltpu.VMEM((2, 4, ROWS, 256), BF16),
+            pltpu.VMEM((ROWS, 256), F32),
+            pltpu.VMEM((ROWS, 256), F32),
         ],
         mib=16,
-    )
-    u_own, mixed_own, o_own, g_own, near = layer_half(where[4:5], x_rows, *own, cols)
-    u_other, mixed_other, o_other, g_other, far = layer_half(where[5:6], x_rows, *other, cols)
-    home_out = call(out_body, shape((ROWS, WIDTH)), [VMEM] * 8, mib=8)(
-        tokens, u_own, mixed_own, o_own, u_other, mixed_other, o_other, gain
-    )
+    )(where, tokens, cols, gain, *acts, *o_parts)
 
     token_grad, own_terms, sent, own_inner = call(
         loss_body,
@@ -592,10 +556,10 @@
             shape((528, ROWS)),
             shape((1, ROWS), F32),
         ),
-        [SMEM] + [VMEM] * 5,
+        [SMEM] + [VMEM] * 11,
         scratch=[pltpu.VMEM((PLANE, 2, 32, ROWS), BF16)],
         mib=16,
-    )(core.reshape(1), home_out, table_low, g_own, g_other, cols)
+    )(where, home_out, table_low, cols, *groups)
     partner_terms = lax.ppermute(sent, "user", PARTNER)
     pair = call(pair_body, shape((PLANE, 40, ROWS)), [VMEM] * 3)(
         own_terms, own_inner, partner_terms
@@ -606,7 +570,7 @@
     layer_out = call(
         worker_body,
         shape((256, WIDTH)),
-        [SMEM] + [VMEM] * 7 + [ANY] * 8,
+        [SMEM] + [VMEM] * 13 + [ANY] * 8,
         scratch=[
             pltpu.VMEM((4, PIECE, LANES), BF16),
             pltpu.VMEM((4, PIECE, LANES), BF16),
@@ -617,7 +581,7 @@
             pltpu.SemaphoreType.DMA((2, 4)),
         ],
         mib=24,
-    )(where, near, far, arrived, in_gain[None], o_own, o_other, gain, *own, *other)
+    )(where, arrived, in_gain[None], o_own, o_other, gain, *tables, *pieces)
 
     positive_part, negative_part = call(
         plane_body, (shape((48, 256), F32), shape((256, LANES))), [VMEM]

time: 145 us -> 149 us (1.028)
  blocking collectives: 18.6 us -> 30.5 us
  starting transfers between devices: 70.8 us -> 61.3 us
  waiting for transfers between devices: 17 us -> 10.2 us
  local copies, waits for them, and re-layouts: 3.35 us -> 7.54 us
  Pallas kernels: 33 us -> 36.3 us
    all_to_all x1 -> x2, blocking collectives: 18.6 us -> 30.5 us  [exchange(): lax.all_to_all(blocks, axis, 0, 0, tiled=True, axis_index_groups=groups)]
    ppermute x3 -> x0, starting transfers between devices: 9.5 us -> none  [per_device(): line.append(lax.ppermute(message, 'user', shifted(FIRST, step)))]
    ppermute x3 -> x0, waiting for transfers between devices: 4.88 us -> none  [per_device(): line.append(lax.ppermute(message, 'user', shifted(FIRST, step)))]
    unnamed x30 -> x42, local copies, waits for them, and re-layouts: 3.26 us -> 7.45 us
    pallas_call x6 -> x11, Pallas kernels: 20.9 us -> 23.5 us  [the longest x8 11.7 us: per_device(): parts.append(layer_part(x_rows, pieces[n]))]
    all_to_all x3, waiting for transfers between devices: 8.36 us -> 6.4 us  [exchange(): lax.all_to_all(blocks, axis, 0, 0, tiled=True, axis_index_groups=groups)]
  transfers between devices with their start and end apart: 14 -> 11, of which waited for: 6 -> 4; matrix products, arithmetic and copies ran while one was open for 0% -> 0% of each run, Pallas kernels for 19% -> 22%
where the time goes in v5:
time: 149 us; the launch traced here: 147 us
  starting transfers between devices  61.3 us (41%)
  Pallas kernels  36.3 us (24%)
  blocking collectives  30.5 us (20%)
  waiting for transfers between devices  10.2 us (7%)
  local copies, waits for them, and re-layouts  7.54 us (5%)
    all_to_all x2, blocking collectives, exchange(): lax.all_to_all(blocks, axis, 0, 0, tiled=True, axis_index_groups=groups)  30.5 us
    all_to_all x3, starting transfers between devices, exchange(): lax.all_to_all(blocks, axis, 0, 0, tiled=True, axis_index_groups=groups)  25.5 us
    ppermute x4, starting transfers between devices, per_device(): other[step] = lax.ppermute(own[step], 'user', PARTNER)  24.1 us
    pallas_call x8, Pallas kernels, per_device(): parts.append(layer_part(x_rows, pieces[n]))  11.7 us
    ppermute x3, starting transfers between devices, per_device(): own[step] = lax.ppermute(mid, 'user', shifted(SECOND, step))  9.32 us
    pallas_call x1, Pallas kernels, per_device(): call(worker_body, shape((256, WIDTH)), [SMEM] + [VMEM] * 13 + [ANY] * 8,...  8.7 us
    unnamed x42, local copies, waits for them, and re-layouts  7.45 us
    all_to_all x3, waiting for transfers between devices, exchange(): lax.all_to_all(blocks, axis, 0, 0, tiled=True, axis_index_groups=groups)  6.4 us
  transfers between devices with their start and end apart: 11, of which 4 were waited for; matrix products, arithmetic and copies ran while one was open for 0% of the time, Pallas kernels for 22%

profile of v5, /device:TPU:1, one launch (start us, length us, event | category | flops | bytes accessed | tf_op | source)
XLA Modules:
  0.0 146.8 jit_solution(9620229770397697505)
XLA Ops:
  0.7 0.1 stack.27.where
  0.7 0.6 copy-done.6
  1.4 2.4 %shard_map.131 = bf16[16,48,128]{2,1,0:T(8,128)(2,1)} custom-call(s32[6]{0:T(128)S(1)} %stack.27.where, s32[16,256]{1,0:T(8,128)S(1)} %copy-done.6, bf16[64,2048]{1,0:T(8,128)(2,1)} %w_ref.1, bf16[64,512]{1,0:T(8,128)(2,1)} %bitcast.30, bf16[256,1024]{1,0:T(8,128)(2,1)} %table_ref.3), custom_call_target="tpu_custom_call" | custom-call | tf_op jit(solution)/shard_map/pallas_call | solution.py:467
  3.8 15.7 %all-to-all-start = ((bf16[16,48,128]{2,1,0:T(8,128)(2,1)}), bf16[16,48,128]{2,1,0:T(8,128)(2,1)S(1)}, u32[]{:S(2)}, u32[]{:S(2)}) async-start(bf16[16,48,128]{2,1,0:T(8,128)(2,1)} %shard_map.131), calls=%async_computation | async-start | bytes 393216 | tf_op jit(solution)/shard_map/all_to_all | solution.py:442
  19.6 0.6 copy-done.14
  20.2 0.0 copy-done.19
  20.3 4.5 %shard_map.130 = (bf16[512,1024]{1,0:T(8,128)(2,1)S(1)}, f32[512,128]{1,0:T(8,128)S(1)}, bf16[16,128]{1,0:T(8,128)(2,1)S(1)}, bf16[512,1024]{1,0:T(8,128)(2,1)S(...) custom-call(s32[6]{0:T(128)S(1)} %stack.27.where, ...), custom_call_target="tpu_custom_call" | custom-call | tf_op jit(solution)/shard_map/pallas_call | solution.py:482
  24.7 1.0 copy-done.1
  25.7 0.8 copy-done.2
  26.5 0.6 copy-done.4
  27.2 0.6 copy-done.15
  27.8 4.3 %all-to-all-done.got = bf16[16,48,128]{2,1,0:T(8,128)(2,1)S(1)} async-done(((bf16[16,48,128]{2,1,0:T(8,128)(2,1)}), bf16[16,48,128]{2,1,0:T(8,128)(2,1)S(1)}, u32[]{:S(2)}, u32[]{:S(2)}) %all-to-all-start) | async-done | bytes 196640 | tf_op jit(solution)/shard_map/all_to_all | solution.py:442
  32.0 0.2 shard_map.132
  32.2 12.1 %all_to_all.25 = bf16[4,720,128]{2,1,0:T(8,128)(2,1)S(1)} all-to-all(bf16[4,720,128]{2,1,0:T(8,128)(2,1)S(1)} %shard_map.132), channel_id=1, replica_groups={{0,128,256,384},{32,160,288,416},{64,192,320,448},{96,224,352,480},{16,..., dimensions={0} | all-to-all | bytes 1474560 | tf_op jit(solution)/shard_map/all_to_all | solution.py:442
  44.3 4.4 %collective-permute-start.2 = (bf16[2880,128]{1,0:T(8,128)(2,1)S(1)}, bf16[2880,128]{1,0:T(8,128)(2,1)}, u32[]{:S(2)}, u32[]{:S(2)}) collective-permute-start(bf16[2880,128]{1,0:T(8,128)(2,1)S(1)} %bitcast.16), channel_id=1, source_target_pairs={{0,96},{32,0},{64,32},{96,64},{128,224},{160,128},{192,160},{224,1... | collective-permute-start | bytes 2211848 | tf_op jit(solution)/shard_map/ppermute | solution.py:522
  48.6 2.4 %collective-permute-start.1 = (bf16[2880,128]{1,0:T(8,128)(2,1)S(1)}, bf16[2880,128]{1,0:T(8,128)(2,1)}, u32[]{:S(2)}, u32[]{:S(2)}) collective-permute-start(bf16[2880,128]{1,0:T(8,128)(2,1)S(1)} %bitcast.17), channel_id=1, source_target_pairs={{0,64},{32,96},{64,0},{96,32},{128,192},{160,224},{192,128},{224,1... | collective-permute-start | bytes 2211848 | tf_op jit(solution)/shard_map/ppermute | solution.py:522
  51.1 2.5 %collective-permute-start = (bf16[2880,128]{1,0:T(8,128)(2,1)S(1)}, bf16[2880,128]{1,0:T(8,128)(2,1)}, u32[]{:S(2)}, u32[]{:S(2)}) collective-permute-start(bf16[2880,128]{1,0:T(8,128)(2,1)S(1)} %bitcast.18), channel_id=1, source_target_pairs={{0,32},{32,64},{64,96},{96,0},{128,160},{160,192},{192,224},{224,1... | collective-permute-start | bytes 2211848 | tf_op jit(solution)/shard_map/ppermute | solution.py:522
  53.6 9.0 %collective-permute-start.3 = (bf16[2880,128]{1,0:T(8,128)(2,1)S(1)}, bf16[2880,128]{1,0:T(8,128)(2,1)}, u32[]{:S(2)}, u32[]{:S(2)}) collective-permute-start(bf16[2880,128]{1,0:T(8,128)(2,1)S(1)} %bitcast.19), channel_id=1, source_target_pairs={{0,16},{16,0},{32,48},{48,32},{64,80},{80,64},{96,112},{112,96},{1... | collective-permute-start | bytes 2211848 | tf_op jit(solution)/shard_map/ppermute | solution.py:524
  62.6 2.3 %collective-permute-done.2.w.rest_11_ = bf16[2880,128]{1,0:T(8,128)(2,1)} collective-permute-done((bf16[2880,128]{1,0:T(8,128)(2,1)S(1)}, bf16[2880,128]{1,0:T(8,128)(2,1)}, u32[]{:S(2)}, u32[]{:S(2)}) %collective-permute-start.2) | collective-permute-done | bytes 737312 | tf_op jit(solution)/shard_map/ppermute | solution.py:522
  64.9 9.1 %collective-permute-start.6 = (bf16[2880,128]{1,0:T(8,128)(2,1)}, bf16[2880,128]{1,0:T(8,128)(2,1)}, u32[]{:S(2)}, u32[]{:S(2)}) collective-permute-start(bf16[2880,128]{1,0:T(8,128)(2,1)} %collective-permute-done.2.w.rest_11_), channel_id=1, source_target_pairs={{0,16},{16,0},{32,48},{48,32},{64,80},{80,64},{96,112},{112,96},{1... | collective-permute-start | bytes 2211848 | tf_op jit(solution)/shard_map/ppermute | solution.py:524
  74.0 1.9 %collective-permute-start.5 = (bf16[2880,128]{1,0:T(8,128)(2,1)}, bf16[2880,128]{1,0:T(8,128)(2,1)}, u32[]{:S(2)}, u32[]{:S(2)}) collective-permute-start(bf16[2880,128]{1,0:T(8,128)(2,1)} %collective-permute-done.1.w.rest_10_), channel_id=1, source_target_pairs={{0,16},{16,0},{32,48},{48,32},{64,80},{80,64},{96,112},{112,96},{1... | collective-permute-start | bytes 2211848 | tf_op jit(solution)/shard_map/ppermute | solution.py:524
  76.0 4.0 %collective-permute-start.4 = (bf16[2880,128]{1,0:T(8,128)(2,1)}, bf16[2880,128]{1,0:T(8,128)(2,1)}, u32[]{:S(2)}, u32[]{:S(2)}) collective-permute-start(bf16[2880,128]{1,0:T(8,128)(2,1)} %collective-permute-done.w.rest_9_), channel_id=1, source_target_pairs={{0,16},{16,0},{32,48},{48,32},{64,80},{80,64},{96,112},{112,96},{1... | collective-permute-start | bytes 2211848 | tf_op jit(solution)/shard_map/ppermute | solution.py:524
  80.0 5.8 %all-to-all-start.2 = ((bf16[32,16,1024]{2,1,0:T(8,128)(2,1)}), bf16[32,16,1024]{2,1,0:T(8,128)(2,1)S(1)}, u32[]{:S(2)}, u32[]{:S(2)}) async-start(bf16[32,16,1024]{2,1,0:T(8,128)(2,1)} %bitcast.23), calls=%async_computation.2 | async-start | bytes 2097152 | tf_op jit(solution)/shard_map/all_to_all | solution.py:442
  85.8 0.5 shard_map.133
  86.3 1.6 %shard_map.136 = (bf16[512,256]{1,0:T(8,128)(2,1)S(1)}, bf16[64,1024]{1,0:T(8,128)(2,1)S(1)}, bf16[64,512]{1,0:T(8,128)(2,1)S(1)}, f32[8,128]{1,0:T(8,128)S(1)}) custom-call(bf16[512,1024]{1,0:T(8,128)(2,1)S(1)} %get-tuple-element.62.x_ref, bf16[2880,128]{1,0:T(8,128)(2,1)} %collective-permute-done.2.w.rest_11_), custom_call_target="tpu_custom_call" | custom-call | tf_op jit(solution)/shard_map/pallas_call | solution.py:536
  87.9 1.6 %shard_map.135 = (bf16[512,256]{1,0:T(8,128)(2,1)S(1)}, bf16[64,1024]{1,0:T(8,128)(2,1)S(1)}, bf16[64,512]{1,0:T(8,128)(2,1)S(1)}, f32[8,128]{1,0:T(8,128)S(1)}) custom-call(bf16[512,1024]{1,0:T(8,128)(2,1)S(1)} %get-tuple-element.62.x_ref, bf16[2880,128]{1,0:T(8,128)(2,1)} %collective-permute-done.1.w.rest_10_), custom_call_target="tpu_custom_call" | custom-call | tf_op jit(solution)/shard_map/pallas_call | solution.py:536
  89.5 1.6 %shard_map.134 = (bf16[512,256]{1,0:T(8,128)(2,1)S(1)}, bf16[64,1024]{1,0:T(8,128)(2,1)S(1)}, bf16[64,512]{1,0:T(8,128)(2,1)S(1)}, f32[8,128]{1,0:T(8,128)S(1)}) custom-call(bf16[512,1024]{1,0:T(8,128)(2,1)S(1)} %get-tuple-element.62.x_ref, bf16[2880,128]{1,0:T(8,128)(2,1)} %collective-permute-done.w.rest_9_), custom_call_target="tpu_custom_call" | custom-call | tf_op jit(solution)/shard_map/pallas_call | solution.py:536
  91.1 1.6 %shard_map.137 = (bf16[512,256]{1,0:T(8,128)(2,1)S(1)}, bf16[64,1024]{1,0:T(8,128)(2,1)S(1)}, bf16[64,512]{1,0:T(8,128)(2,1)S(1)}, f32[8,128]{1,0:T(8,128)S(1)}) custom-call(bf16[512,1024]{1,0:T(8,128)(2,1)S(1)} %get-tuple-element.62.x_ref, bf16[2880,128]{1,0:T(8,128)(2,1)} %collective-permute-done.3.w.rest_12_), custom_call_target="tpu_custom_call" | custom-call | tf_op jit(solution)/shard_map/pallas_call | solution.py:536
  92.7 1.6 %shard_map.140 = (bf16[512,256]{1,0:T(8,128)(2,1)S(1)}, bf16[64,1024]{1,0:T(8,128)(2,1)S(1)}, bf16[64,512]{1,0:T(8,128)(2,1)S(1)}, f32[8,128]{1,0:T(8,128)S(1)}) custom-call(bf16[512,1024]{1,0:T(8,128)(2,1)S(1)} %get-tuple-element.62.x_ref, bf16[2880,128]{1,0:T(8,128)(2,1)} %collective-permute-done.6.w.rest_15_), custom_call_target="tpu_custom_call" | custom-call | tf_op jit(solution)/shard_map/pallas_call | solution.py:536
  94.4 0.6 copy-done.8
  94.9 1.6 %shard_map.139 = (bf16[512,256]{1,0:T(8,128)(2,1)S(1)}, bf16[64,1024]{1,0:T(8,128)(2,1)S(1)}, bf16[64,512]{1,0:T(8,128)(2,1)S(1)}, f32[8,128]{1,0:T(8,128)S(1)}) custom-call(bf16[512,1024]{1,0:T(8,128)(2,1)S(1)} %get-tuple-element.62.x_ref, bf16[2880,128]{1,0:T(8,128)(2,1)} %collective-permute-done.5.w.rest_14_), custom_call_target="tpu_custom_call" | custom-call | tf_op jit(solution)/shard_map/pallas_call | solution.py:536
  96.6 0.6 copy-done.10
  97.2 1.7 %shard_map.138 = (bf16[512,256]{1,0:T(8,128)(2,1)S(1)}, bf16[64,1024]{1,0:T(8,128)(2,1)S(1)}, bf16[64,512]{1,0:T(8,128)(2,1)S(1)}, f32[8,128]{1,0:T(8,128)S(1)}) custom-call(bf16[512,1024]{1,0:T(8,128)(2,1)S(1)} %get-tuple-element.62.x_ref, bf16[2880,128]{1,0:T(8,128)(2,1)} %collective-permute-done.4.w.rest_13_), custom_call_target="tpu_custom_call" | custom-call | tf_op jit(solution)/shard_map/pallas_call | solution.py:536
  98.9 0.6 copy-done.12
  99.4 2.9 %shard_map.141 = (bf16[512,1024]{1,0:T(8,128)(2,1)S(1)}, bf16[256,1024]{1,0:T(8,128)(2,1)S(1)}, bf16[256,1024]{1,0:T(8,128)(2,1)S(1)}) custom-call(s32[6]{0:T(128)S(1)} %stack.27.where, bf16[512,1024]{1,0:T(8,128)(2,1)S(1)} %copy-done, f32[512,128]{1,0:T(8,128)S(1)} %get-tuple-element.59.cols_ref, f32[1,512]{1,0:T(1,128)S(1)} %bitcast.25, ...), custom_call_target="tpu_custom_call" | custom-call | tf_op jit(solution)/shard_map/pallas_call | solution.py:539
  102.4 4.2 %shard_map.142 = (bf16[512,1024]{1,0:T(8,128)(2,1)}, bf16[16,32,512]{2,1,0:T(8,128)(2,1)S(1)}, bf16[528,512]{1,0:T(8,128)(2,1)S(1)}, f32[1,512]{1,0:T(1,128)S(1)}) custom-call(s32[6]{0:T(128)S(1)} %stack.27.where, bf16[512,1024]{1,0:T(8,128)(2,1)S(1)} %get-tuple-element.83.out_ref, bf16[256,1024]{1,0:T(8,128)(2,1)S(1)} %copy-done.3, ...), custom_call_target="tpu_custom_call" | custom-call | tf_op jit(solution)/shard_map/pallas_call | solution.py:551
  106.6 2.3 %collective-permute-start.7 = (bf16[528,512]{1,0:T(8,128)(2,1)S(1)}, bf16[528,512]{1,0:T(8,128)(2,1)S(1)}, u32[]{:S(2)}, u32[]{:S(2)}) collective-permute-start(bf16[528,512]{1,0:T(8,128)(2,1)S(1)} %get-tuple-element.95), channel_id=1, source_target_pairs={{0,16},{16,0},{32,48},{48,32},{64,80},{80,64},{96,112},{112,96},{1... | collective-permute-start | bytes 1622024 | tf_op jit(solution)/shard_map/ppermute | solution.py:563
  108.9 1.5 %collective-permute-done.7.got_ref = bf16[528,512]{1,0:T(8,128)(2,1)S(1)} collective-permute-done((bf16[528,512]{1,0:T(8,128)(2,1)S(1)}, bf16[528,512]{1,0:T(8,128)(2,1)S(1)}, u32[]{:S(2)}, u32[]{:S(2)}) %collective-permute-start.7) | collective-permute-done | bytes 540704 | tf_op jit(solution)/shard_map/ppermute | solution.py:563
  110.4 0.1 shard_map.143
  110.5 18.5 %all_to_all.26.got_ref = bf16[16,40,512]{2,1,0:T(8,128)(2,1)S(1)} all-to-all(bf16[16,40,512]{2,1,0:T(8,128)(2,1)S(1)} %shard_map.143), channel_id=1, replica_groups={{0,32,64,96,128,160,192,224,256,288,320,352,384,416,448,480},{16,48,80,..., dimensions={0} | all-to-all | bytes 1310720 | tf_op jit(solution)/shard_map/all_to_all | solution.py:442
  129.0 0.8 shard_map.145
  129.8 4.0 %all-to-all-start.4 = ((bf16[16,16,128]{2,1,0:T(8,128)(2,1)}), bf16[16,16,128]{2,1,0:T(8,128)(2,1)S(1)}, u32[]{:S(2)}, u32[]{:S(2)}) async-start(bf16[16,16,128]{2,1,0:T(8,128)(2,1)} %bitcast.13), calls=%async_computation.4 | async-start | bytes 131072 | tf_op jit(solution)/shard_map/all_to_all | solution.py:442
  133.8 0.7 copy-done.13
  134.5 0.0 copy-done.9
  134.5 8.7 %shard_map.144 = bf16[256,1024]{1,0:T(8,128)(2,1)} custom-call(s32[6]{0:T(128)S(1)} %stack.27.where, bf16[512,1024]{1,0:T(8,128)(2,1)S(1)} %bitcast.22, f32[1,1024]{1,0:T(1,128)S(1)} %bitcast.28, bf16[256,1024]{1,0:T(8,128)(2,1)S(1)} %get-tuple-element.98.o0, bf16[256,1024]{1,0:T(8,128)(2,1)S(1)} %get-tuple-element.99.o1, f32[1,512]{1,0:T(1,128)S(1)} %bitcast.26, ...), custom_call_target="tpu_custom_call" | custom-call | tf_op jit(solution)/shard_map/pallas_call | solution.py:570
  143.2 2.1 %all-to-all-done.4 = bf16[16,16,128]{2,1,0:T(8,128)(2,1)S(1)} async-done(((bf16[16,16,128]{2,1,0:T(8,128)(2,1)}), bf16[16,16,128]{2,1,0:T(8,128)(2,1)S(1)}, u32[]{:S(2)}, u32[]{:S(2)}) %all-to-all-start.4) | async-done | bytes 65568 | tf_op jit(solution)/shard_map/all_to_all | solution.py:442
  145.4 0.7 copy-done.16
  146.0 0.8 shard_map.146
  (38 shorter events, 0.1 us)
Async XLA Ops:
  0.6 0.7 copy-start.6
  3.8 15.8 %copy-start.7 = (f32[1024]{0:T(1024)S(1)}, f32[1024]{0:T(1024)}, u32[]{:S(2)}) copy-start(f32[1024]{0:T(1024)} %param.18) | copy-start | bytes 12292
  3.8 28.2 %all-to-all-start = ((bf16[16,48,128]{2,1,0:T(8,128)(2,1)}), bf16[16,48,128]{2,1,0:T(8,128)(2,1)S(1)}, u32[]{:S(2)}, u32[]{:S(2)}) async-start(bf16[16,48,128]{2,1,0:T(8,128)(2,1)} %shard_map.131), calls=%async_computation | async-start | bytes 393216 | tf_op jit(solution)/shard_map/all_to_all | solution.py:442
  19.6 0.7 copy-start.14
  19.6 0.7 copy-start.17
  19.6 0.7 copy-start.18
  19.6 0.7 copy-start.19
  20.3 6.9 %copy-start.20 = (f32[512]{0:T(512)S(1)}, f32[512]{0:T(512)}, u32[]{:S(2)}) copy-start(f32[512]{0:T(512)} %param.20) | copy-start | bytes 6148
  24.7 1.0 copy-start.1
  25.7 0.8 copy-start.2
  26.5 0.6 copy-start.4
  27.2 0.6 copy-start.15
  44.3 20.7 %collective-permute-start.2 = (bf16[2880,128]{1,0:T(8,128)(2,1)S(1)}, bf16[2880,128]{1,0:T(8,128)(2,1)}, u32[]{:S(2)}, u32[]{:S(2)}) collective-permute-start(bf16[2880,128]{1,0:T(8,128)(2,1)S(1)} %bitcast.16), channel_id=1, source_target_pairs={{0,96},{32,0},{64,32},{96,64},{128,224},{160,128},{192,160},{224,1... | collective-permute-start | bytes 2211848 | tf_op jit(solution)/shard_map/ppermute | solution.py:522
  48.6 25.4 %collective-permute-start.1 = (bf16[2880,128]{1,0:T(8,128)(2,1)S(1)}, bf16[2880,128]{1,0:T(8,128)(2,1)}, u32[]{:S(2)}, u32[]{:S(2)}) collective-permute-start(bf16[2880,128]{1,0:T(8,128)(2,1)S(1)} %bitcast.17), channel_id=1, source_target_pairs={{0,64},{32,96},{64,0},{96,32},{128,192},{160,224},{192,128},{224,1... | collective-permute-start | bytes 2211848 | tf_op jit(solution)/shard_map/ppermute | solution.py:522
  51.1 24.9 %collective-permute-start = (bf16[2880,128]{1,0:T(8,128)(2,1)S(1)}, bf16[2880,128]{1,0:T(8,128)(2,1)}, u32[]{:S(2)}, u32[]{:S(2)}) collective-permute-start(bf16[2880,128]{1,0:T(8,128)(2,1)S(1)} %bitcast.18), channel_id=1, source_target_pairs={{0,32},{32,64},{64,96},{96,0},{128,160},{160,192},{192,224},{224,1... | collective-permute-start | bytes 2211848 | tf_op jit(solution)/shard_map/ppermute | solution.py:522
  53.6 37.5 %collective-permute-start.3 = (bf16[2880,128]{1,0:T(8,128)(2,1)S(1)}, bf16[2880,128]{1,0:T(8,128)(2,1)}, u32[]{:S(2)}, u32[]{:S(2)}) collective-permute-start(bf16[2880,128]{1,0:T(8,128)(2,1)S(1)} %bitcast.19), channel_id=1, source_target_pairs={{0,16},{16,0},{32,48},{48,32},{64,80},{80,64},{96,112},{112,96},{1... | collective-permute-start | bytes 2211848 | tf_op jit(solution)/shard_map/ppermute | solution.py:524
  64.9 27.8 %collective-permute-start.6 = (bf16[2880,128]{1,0:T(8,128)(2,1)}, bf16[2880,128]{1,0:T(8,128)(2,1)}, u32[]{:S(2)}, u32[]{:S(2)}) collective-permute-start(bf16[2880,128]{1,0:T(8,128)(2,1)} %collective-permute-done.2.w.rest_11_), channel_id=1, source_target_pairs={{0,16},{16,0},{32,48},{48,32},{64,80},{80,64},{96,112},{112,96},{1... | collective-permute-start | bytes 2211848 | tf_op jit(solution)/shard_map/ppermute | solution.py:524
  74.0 20.9 %collective-permute-start.5 = (bf16[2880,128]{1,0:T(8,128)(2,1)}, bf16[2880,128]{1,0:T(8,128)(2,1)}, u32[]{:S(2)}, u32[]{:S(2)}) collective-permute-start(bf16[2880,128]{1,0:T(8,128)(2,1)} %collective-permute-done.1.w.rest_10_), channel_id=1, source_target_pairs={{0,16},{16,0},{32,48},{48,32},{64,80},{80,64},{96,112},{112,96},{1... | collective-permute-start | bytes 2211848 | tf_op jit(solution)/shard_map/ppermute | solution.py:524
  76.0 21.2 %collective-permute-start.4 = (bf16[2880,128]{1,0:T(8,128)(2,1)}, bf16[2880,128]{1,0:T(8,128)(2,1)}, u32[]{:S(2)}, u32[]{:S(2)}) collective-permute-start(bf16[2880,128]{1,0:T(8,128)(2,1)} %collective-permute-done.w.rest_9_), channel_id=1, source_target_pairs={{0,16},{16,0},{32,48},{48,32},{64,80},{80,64},{96,112},{112,96},{1... | collective-permute-start | bytes 2211848 | tf_op jit(solution)/shard_map/ppermute | solution.py:524
  80.0 30.5 %all-to-all-start.2 = ((bf16[32,16,1024]{2,1,0:T(8,128)(2,1)}), bf16[32,16,1024]{2,1,0:T(8,128)(2,1)S(1)}, u32[]{:S(2)}, u32[]{:S(2)}) async-start(bf16[32,16,1024]{2,1,0:T(8,128)(2,1)} %bitcast.23), calls=%async_computation.2 | async-start | bytes 2097152 | tf_op jit(solution)/shard_map/all_to_all | solution.py:442
  94.3 0.6 copy-start.8
  96.5 0.6 copy-start.10
  97.1 2.3 %copy-start = (bf16[512,1024]{1,0:T(8,128)(2,1)S(1)}, bf16[512,1024]{1,0:T(8,128)(2,1)}, u32[]{:S(2)}) copy-start(bf16[512,1024]{1,0:T(8,128)(2,1)} %tok_ref.3) | copy-start | bytes 3145732
  98.8 0.6 copy-start.12
  99.4 2.9 %copy-start.3 = (bf16[256,1024]{1,0:T(8,128)(2,1)S(1)}, bf16[256,1024]{1,0:T(8,128)(2,1)}, u32[]{:S(2)}) copy-start(bf16[256,1024]{1,0:T(8,128)(2,1)} %copy-done.2) | copy-start | bytes 1572868
  106.6 3.8 %collective-permute-start.7 = (bf16[528,512]{1,0:T(8,128)(2,1)S(1)}, bf16[528,512]{1,0:T(8,128)(2,1)S(1)}, u32[]{:S(2)}, u32[]{:S(2)}) collective-permute-start(bf16[528,512]{1,0:T(8,128)(2,1)S(1)} %get-tuple-element.95), channel_id=1, source_target_pairs={{0,16},{16,0},{32,48},{48,32},{64,80},{80,64},{96,112},{112,96},{1... | collective-permute-start | bytes 1622024 | tf_op jit(solution)/shard_map/ppermute | solution.py:563
  129.8 15.6 %all-to-all-start.4 = ((bf16[16,16,128]{2,1,0:T(8,128)(2,1)}), bf16[16,16,128]{2,1,0:T(8,128)(2,1)S(1)}, u32[]{:S(2)}, u32[]{:S(2)}) async-start(bf16[16,16,128]{2,1,0:T(8,128)(2,1)} %bitcast.13), calls=%async_computation.4 | async-start | bytes 131072 | tf_op jit(solution)/shard_map/all_to_all | solution.py:442
  133.8 0.7 copy-start.13
  133.8 0.7 copy-start.11
  133.8 0.7 copy-start.9
  134.5 10.8 %copy-start.5 = (bf16[256,256]{1,0:T(8,128)(2,1)S(1)}, bf16[256,256]{1,0:T(8,128)(2,1)}, u32[]{:S(2)}) copy-start(bf16[256,256]{1,0:T(8,128)(2,1)} %copy-done.4) | copy-start | bytes 393220
  145.4 0.7 copy-start.16

commit v6 on v5

--- a/solution.py
+++ b/solution.py
@@ -29,13 +29,6 @@
 SECOND = [[x * 8 + y * 2 for y in range(4)] for x in range(4)] + [
     [x * 8 + y * 2 + 1 for x in range(4)] for y in range(4)
 ]
-PIECE = 4 * 720
-
-
-def shifted(groups, step):
-    return [(g[n], g[(n + step) % 4]) for g in groups for n in range(4)]
-
-
 SAME_CORE = [[k * 2 + c for k in range(PLANE)] for c in range(2)]
 PARTNER = [(k, k ^ 1) for k in range(USERS)]
 
@@ -219,18 +212,13 @@
         out[g] = out[0]
 
 
-def fetches(pieces, w, sems):
-    return [pltpu.make_async_copy(p, w.at[n], sems.at[n]) for n, p in enumerate(pieces)]
-
-
-def kind_of(position, n):
-    return lax.rem(position + 4 - n, 4)
-
-
-def project(x, w):
-    parts = [w[i * 720 : i * 720 + W_ROWS, :] for i in range(4)]
+def project(x, w, q):
     both = jnp.concatenate(
-        [jnp.concatenate(parts[0:2], axis=0), jnp.concatenate(parts[2:4], axis=0)], axis=1
+        [
+            jnp.concatenate([w[n, :W_ROWS, :], w[n + 1, :W_ROWS, :]], axis=0)
+            for n in (4 * q, 4 * q + 2)
+        ],
+        axis=1,
     )
     return jax.nn.silu(dot(x, both)).astype(BF16)
 
@@ -250,35 +238,63 @@
             mixed_ref[lo:hi, d0:d1] = dot(weights, v[at:hi, d0:d1])
 
 
-def project_body(x_ref, w, act_ref, o_ref, g_ref, label_ref):
-    act_ref[...] = project(x_ref[...], w)
-
-    def columns(at):
-        return jnp.concatenate(
-            [w[i * 720 + at : i * 720 + at + 16, :] for i in range(4)], axis=0
-        )
-
-    for b in range(8):
-        o_ref[:, b * LANES : (b + 1) * LANES] = columns(W_ROWS + b * 16)
-    for b in range(4):
-        g_ref[:, b * LANES : (b + 1) * LANES] = columns(W_ROWS + 128 + b * 16)
-    labels = [
-        w[i * 720 + W_ROWS + 192 : (i + 1) * 720, :].astype(F32)[0:1, :] for i in range(4)
+def split_rest(w, o_ref, g_ref, label_ref):
+    for n in range(8):
+        o_ref[:, n * LANES : (n + 1) * LANES] = w[
+            :, W_ROWS + n * 16 : W_ROWS + (n + 1) * 16, :
+        ].reshape(256, LANES)
+    for n in range(4):
+        g_ref[:, n * LANES : (n + 1) * LANES] = w[
+            :, W_ROWS + 128 + n * 16 : W_ROWS + 144 + n * 16, :
+        ].reshape(256, LANES)
+    for n in range(PLANE):
+        label_ref[n : n + 1, :] = w[n, W_ROWS + 192 : W_ROWS + 208, :].astype(F32)[0:1, :]
+
+
+def layer_body(
+    x_ref,
+    w0,
+    w1_ref,
+    tok_ref,
+    cols_ref,
+    gain_ref,
+    out_ref,
+    o0,
+    o1,
+    g0,
+    g1,
+    near,
+    far,
+    kept_ref,
+    x,
+    w1,
+    tok,
+    act,
+    m0,
+    m1,
+    sems,
+):
+    copies = [
+        pltpu.make_async_copy(a, b, sems.at[n])
+        for n, (a, b) in enumerate(((x_ref, x), (w1_ref, w1), (tok_ref, tok), (w0, kept_ref)))
     ]
-    label_ref[...] = jnp.concatenate(labels + [jnp.zeros((4, LANES), F32)], axis=0)
-
-
-def finish_body(where, tok_ref, cols_ref, gain_ref, *rest):
-    acts, parts = rest[:8], rest[8:16]
-    out_ref, o0, o1, act, m0, m1 = rest[16:]
+    for copy in copies:
+        copy.start()
+    split_rest(w0, o0, g0, near)
     first = cols_ref[:, 0:1].astype(jnp.int32)
-    for half, (o, m) in enumerate(((o0, m0), (o1, m1))):
-        for n in range(4):
-            kind = kind_of(where[4 + half], n)
-            act[half, kind] = acts[4 * half + n][...]
-            o[pl.ds(pl.multiple_of(kind * 64, 64), 64), :] = parts[4 * half + n][...]
-        attend(act.at[half], first, m)
-    out_ref[...] = gated_out(tok_ref[...], act.at[0, 0], m0, o0, act.at[1, 0], m1, o1, gain_ref)
+    copies[0].wait()
+    rows = x[...]
+    for q in range(4):
+        act[0, q] = project(rows, w0, q)
+    attend(act.at[0], first, m0)
+    copies[1].wait()
+    split_rest(w1, o1, g1, far)
+    for q in range(4):
+        act[1, q] = project(rows, w1, q)
+    attend(act.at[1], first, m1)
+    copies[2].wait()
+    out_ref[...] = gated_out(tok[...], act.at[0, 0], m0, o0, act.at[1, 0], m1, o1, gain_ref)
+    copies[3].wait()
 
 
 def gated_out(rows, u0, m0, o0, u1, m1, o1, gain_ref):
@@ -296,29 +312,42 @@
     return (rows.astype(F32) + delta).astype(BF16)
 
 
-def worker_body(where, got_ref, in_gain, o0, o1, gain_ref, *rest):
-    labels, pieces = rest[:8], rest[8:16]
-    out_ref, w0, w1, a0, a1, m0, m1, sems = rest[16:]
+def worker_body(
+    where,
+    got_ref,
+    in_gain,
+    o0,
+    o1,
+    gain_ref,
+    near,
+    far,
+    w0_ref,
+    w1_ref,
+    out_ref,
+    w0,
+    w1,
+    act,
+    m0,
+    m1,
+    sems,
+):
     core, user = where[1], where[3]
-    copies = (
-        fetches(pieces[:4], w0, sems.at[0]),
-        fetches(pieces[4:], w1, sems.at[1]),
-    )
-    for copy in copies[0] + copies[1]:
+    copies = [
+        pltpu.make_async_copy(a, b, sems.at[n]) for n, (a, b) in enumerate(((w0_ref, w0), (w1_ref, w1)))
+    ]
+    for copy in copies:
         copy.start()
-    lane = lax.broadcasted_iota(jnp.int32, (32, LANES), 1)
-    sub = lax.broadcasted_iota(jnp.int32, (32, ROWS), 0)
+    lane = lax.broadcasted_iota(jnp.int32, (PLANE, LANES), 1)
+    sub = lax.broadcasted_iota(jnp.int32, (PLANE, ROWS), 0)
     slot = lax.broadcasted_iota(jnp.int32, (1, ROWS), 1)
     peer = slot // MOST
     x, y, c = peer // 8, peer // 2 % 4, peer % 2
-    outer, inner = jnp.where(c == 0, y, x), jnp.where(c == 0, x, y)
+    spot = jnp.where(c == 0, y * 4 + x, x * 4 + y)
 
     def of_peer(at):
         total = 0.0
-        for half, mine in ((0, c == core), (1, c != core)):
-            table = jnp.concatenate([r[...] for r in labels[4 * half : 4 * half + 4]], axis=0)
-            value = jnp.sum(jnp.where(lane == at, table, 0.0), axis=1, keepdims=True)
-            spot = lax.rem(where[4 + half] + 4 - outer, 4) * 8 + inner
+        for ref, mine in ((near, c == core), (far, c != core)):
+            value = jnp.sum(jnp.where(lane == at, ref[...], 0.0), axis=1, keepdims=True)
             total = total + jnp.sum(
                 jnp.where((sub == spot) & mine, value, 0.0), axis=0, keepdims=True
             )
@@ -332,31 +361,33 @@
     rows = dot(jnp.where(here, 1.0, 0.0).astype(BF16), got_ref[...]).astype(BF16)
     normed = layer_norm(rows.astype(F32), in_gain[...]).astype(BF16)
     moved = reordered(normed)
-    for position, group, w, act, mixed in (
-        (where[4], copies[0], w0, a0, m0),
-        (where[5], copies[1], w1, a1, m1),
-    ):
-        for n, copy in enumerate(group):
-            copy.wait()
-            act[kind_of(position, n)] = project(moved, w.at[n])
-        attend(act, first, mixed)
-    out_ref[...] = gated_out(rows, a0.at[0], m0, o0, a1.at[0], m1, o1, gain_ref)
-
-
-def loss_body(where, out_ref, low_ref, cols_ref, *rest):
-    groups = rest[:8]
-    grad_ref, own_ref, send_ref, own_inner, terms = rest[8:]
+    for half, (w, m) in enumerate(((w0, m0), (w1, m1))):
+        copies[half].wait()
+        for q in range(4):
+            act[half, q] = project(moved, w, q)
+        attend(act.at[half], first, m)
+    out_ref[...] = gated_out(rows, act.at[0, 0], m0, o0, act.at[1, 0], m1, o1, gain_ref)
+
+
+def loss_body(
+    where,
+    out_ref,
+    low_ref,
+    cols_ref,
+    g0_ref,
+    g1_ref,
+    grad_ref,
+    own_ref,
+    send_ref,
+    own_inner,
+    terms,
+):
     c = where[1]
 
     row = lax.broadcasted_iota(jnp.int32, (256, 256), 0)
     col = lax.broadcasted_iota(jnp.int32, (256, 256), 1)
-    halves = []
-    for half in range(2):
-        taken = lax.rem(where[4 + half] + 4 - row % 16 // 4, 4) * 64 + row % 4 * 16 + row // 16
-        swap = jnp.where(col == taken, 1.0, 0.0).astype(BF16)
-        raw = jnp.concatenate([r[...] for r in groups[4 * half : 4 * half + 4]], axis=0)
-        halves.append(dot(swap, raw))
-    g0, g1 = halves
+    swap = jnp.where(col == row % 16 * 16 + row // 16, 1.0, 0.0).astype(BF16)
+    g0, g1 = dot(swap, g0_ref[...]), dot(swap, g1_ref[...])
     size = (jnp.sum(g0 * g0, axis=1, keepdims=True) + jnp.sum(g1 * g1, axis=1, keepdims=True)) / WIDTH
     scale = lax.rsqrt(size + scale_epsilon)
     g0, g1 = (g0 * scale).astype(BF16), (g1 * scale).astype(BF16)
@@ -436,6 +467,10 @@
 
 def in_hbm(values):
     return pltpu.with_memory_space_constraint(values, pltpu.HBM)
+
+
+def copies(block, count):
+    return jnp.broadcast_to(block[None], (count, *block.shape))
 
 
 def exchange(blocks, axis, groups=None):
@@ -460,9 +495,7 @@
     core = user & 1
     x, y = user >> 3, (user >> 1) & 3
     place = jnp.where(core == 0, y * 4 + x, x * 4 + y)
-    second = jnp.where(core == 0, y, x)
-    first = jnp.where(core == 0, x, y)
-    where = jnp.stack([item, core, place, user, second, first]).astype(jnp.int32)
+    where = jnp.stack([item, core, place, user]).astype(jnp.int32)
 
     first_message = call(
         message_body,
@@ -515,38 +548,37 @@
     got, x_rows, gain = lax.optimization_barrier((got, x_rows, gain))
 
     message = call(forward_body, shape((4, W_ROWS + REST, LANES)), [VMEM, VMEM])(got, labels)
-    mid = exchange(message, "user", FIRST).reshape(PIECE, LANES)
-    mid, parcels = lax.optimization_barrier((mid, parcels))
-    own, other = {0: mid}, {}
-    for step in (1, 3, 2):
-        own[step] = lax.ppermute(mid, "user", shifted(SECOND, step))
-    for step in (0, 1, 3, 2):
-        other[step] = lax.ppermute(own[step], "user", PARTNER)
+    mid = exchange(message, "user", FIRST).reshape(4 * (W_ROWS + REST), LANES)
+    held = exchange(copies(mid, 4), "user", SECOND).reshape(PLANE, W_ROWS + REST, LANES)
+    held, parcels = lax.optimization_barrier((held, parcels))
+    held_other = lax.ppermute(held, "user", PARTNER)
     arrived = exchange(parcels.reshape(USERS, MOST, WIDTH), "user").reshape(ROWS, WIDTH)
 
-    layer_part = call(
-        project_body,
-        (shape((ROWS, 256)), shape((64, WIDTH)), shape((64, 512)), shape((8, LANES), F32)),
-        [VMEM] * 2,
-        mib=8,
-    )
-    parts = []
-    for pieces in (own, other):
-        for n in range(4):
-            parts.append(layer_part(x_rows, pieces[n]))
-    acts, o_parts, groups, tables = zip(*parts)
-    pieces = [own[n] for n in range(4)] + [other[n] for n in range(4)]
-    home_out, o_own, o_other = call(
-        finish_body,
-        (shape((ROWS, WIDTH)), shape((256, WIDTH)), shape((256, WIDTH))),
-        [SMEM] + [VMEM] * 19,
+    home_out, o_own, o_other, g_own, g_other, near, far, kept = call(
+        layer_body,
+        (
+            shape((ROWS, WIDTH)),
+            shape((256, WIDTH)),
+            shape((256, WIDTH)),
+            shape((256, 512)),
+            shape((256, 512)),
+            shape((PLANE, LANES), F32),
+            shape((PLANE, LANES), F32),
+            pltpu.HBM((PLANE, W_ROWS + REST, LANES), BF16),
+        ),
+        [HBM, VMEM, HBM, HBM, VMEM, VMEM],
         scratch=[
+            pltpu.VMEM((ROWS, WIDTH), BF16),
+            pltpu.VMEM((PLANE, W_ROWS + REST, LANES), BF16),
+            pltpu.VMEM((ROWS, WIDTH), BF16),
             pltpu.VMEM((2, 4, ROWS, 256), BF16),
             pltpu.VMEM((ROWS, 256), F32),
             pltpu.VMEM((ROWS, 256), F32),
+            pltpu.SemaphoreType.DMA((4,)),
         ],
-        mib=16,
-    )(where, tokens, cols, gain, *acts, *o_parts)
+        mib=20,
+        out_specs=(VMEM,) * 7 + (HBM,),
+    )(in_hbm(x_rows), held, in_hbm(held_other), in_hbm(tokens), cols, gain)
 
     token_grad, own_terms, sent, own_inner = call(
         loss_body,
@@ -556,12 +588,12 @@
             shape((528, ROWS)),
             shape((1, ROWS), F32),
         ),
-        [SMEM] + [VMEM] * 11,
+        [SMEM] + [VMEM] * 5,
         scratch=[pltpu.VMEM((PLANE, 2, 32, ROWS), BF16)],
         mib=16,
-    )(where, home_out, table_low, cols, *groups)
+    )(where, home_out, table_low, cols, g_own, g_other)
     partner_terms = lax.ppermute(sent, "user", PARTNER)
-    pair = call(pair_body, shape((PLANE, 40, ROWS)), [VMEM] * 3)(
+    pair = call(pair_body, pltpu.HBM((PLANE, 40, ROWS), BF16), [VMEM] * 3, out_specs=VMEM)(
         own_terms, own_inner, partner_terms
     )
     pair, arrived = lax.optimization_barrier((pair, arrived))
@@ -570,18 +602,17 @@
     layer_out = call(
         worker_body,
         shape((256, WIDTH)),
-        [SMEM] + [VMEM] * 13 + [ANY] * 8,
+        [SMEM] + [VMEM] * 7 + [HBM] * 2,
         scratch=[
-            pltpu.VMEM((4, PIECE, LANES), BF16),
-            pltpu.VMEM((4, PIECE, LANES), BF16),
-            pltpu.VMEM((4, 256, 256), BF16),
-            pltpu.VMEM((4, 256, 256), BF16),
+            pltpu.VMEM((PLANE, W_ROWS + REST, LANES), BF16),
+            pltpu.VMEM((PLANE, W_ROWS + REST, LANES), BF16),
+            pltpu.VMEM((2, 4, 256, 256), BF16),
             pltpu.VMEM((256, 256), F32),
             pltpu.VMEM((256, 256), F32),
-            pltpu.SemaphoreType.DMA((2, 4)),
+            pltpu.SemaphoreType.DMA((2,)),
         ],
         mib=24,
-    )(where, arrived, in_gain[None], o_own, o_other, gain, *tables, *pieces)
+    )(where, arrived, in_gain[None], o_own, o_other, gain, near, far, kept, in_hbm(held_other))
 
     positive_part, negative_part = call(
         plane_body, (shape((48, 256), F32), shape((256, LANES))), [VMEM]

time: 149 us -> 139 us (0.933)
  blocking collectives: 30.5 us -> 54.1 us
  starting transfers between devices: 61.3 us -> 38.6 us
  Pallas kernels: 36.3 us -> 28.1 us
  waiting for transfers between devices: 10.2 us -> 5.66 us
  local copies, waits for them, and re-layouts: 7.54 us -> 10.1 us
    ppermute x7 -> x1, starting transfers between devices: 33.4 us -> 9.3 us  [per_device(): held_other = lax.ppermute(held, 'user', PARTNER)]
    all_to_all x2 -> x3, blocking collectives: 30.5 us -> 54.1 us  [exchange(): lax.all_to_all(blocks, axis, 0, 0, tiled=True, axis_index_groups=groups)]
    pallas_call x11 -> x3, Pallas kernels: 23.5 us -> 15.3 us  [the longest x1 7.16 us: per_device(): call(layer_body, (shape((ROWS, WIDTH)), shape((256, WIDTH)), shape((256,...]
    all_to_all x3, waiting for transfers between devices: 6.4 us -> 3.48 us  [exchange(): lax.all_to_all(blocks, axis, 0, 0, tiled=True, axis_index_groups=groups)]
    unnamed x42 -> x36, local copies, waits for them, and re-layouts: 7.45 us -> 9.68 us
    ppermute x7 -> x1, waiting for transfers between devices: 2.32 us -> 0.63 us  [per_device(): held_other = lax.ppermute(held, 'user', PARTNER)]
  transfers between devices with their start and end apart: 11 -> 5, of which waited for: 4 -> 4; matrix products, arithmetic and copies ran while one was open for 0% -> 0% of each run, Pallas kernels for 22% -> 17%
where the time goes in v6:
time: 139 us; the launch traced here: 137 us
  blocking collectives  54.1 us (39%)
  starting transfers between devices  38.6 us (28%)
  Pallas kernels  28.1 us (20%)
  local copies, waits for them, and re-layouts  10.1 us (7%)
  waiting for transfers between devices  5.66 us (4%)
    all_to_all x3, blocking collectives, exchange(): lax.all_to_all(blocks, axis, 0, 0, tiled=True, axis_index_groups=groups)  54.1 us
    all_to_all x3, starting transfers between devices, exchange(): lax.all_to_all(blocks, axis, 0, 0, tiled=True, axis_index_groups=groups)  27 us
    unnamed x36, local copies, waits for them, and re-layouts  9.68 us
    ppermute x1, starting transfers between devices, per_device(): held_other = lax.ppermute(held, 'user', PARTNER)  9.3 us
    pallas_call x1, Pallas kernels, per_device(): call(layer_body, (shape((ROWS, WIDTH)), shape((256, WIDTH)), shape((256,...  7.16 us
    pallas_call x1, Pallas kernels, per_device(): call(worker_body, shape((256, WIDTH)), [SMEM] + [VMEM] * 7 + [HBM] * 2, s...  7.09 us
    pallas_call x1, Pallas kernels, per_device(): call(prepare_body, (shape((ROWS, WIDTH)), shape((ROWS, LANES), F32), shap...  4.47 us
    pallas_call x1, Pallas kernels, per_device(): call(loss_body, (shape((ROWS, WIDTH)), shape((PLANE, 32, ROWS)), shape((5...  4.21 us
  transfers between devices with their start and end apart: 5, of which 4 were waited for; matrix products, arithmetic and copies ran while one was open for 0% of the time, Pallas kernels for 17%

profile of v6, /device:TPU:1, one launch (start us, length us, event | category | flops | bytes accessed | tf_op | source)
XLA Modules:
  0.0 137.4 jit_solution(16043846799808257431)
XLA Ops:
  0.6 0.0 copy-start.17
  0.7 0.1 pad_add_fusion.where
  0.7 0.7 copy-done.9
  1.5 2.4 %shard_map.130 = bf16[16,48,128]{2,1,0:T(8,128)(2,1)} custom-call(s32[4]{0:T(128)S(1)} %pad_add_fusion.where, s32[16,256]{1,0:T(8,128)S(1)} %copy-done.9, bf16[64,2048]{1,0:T(8,128)(2,1)} %w_ref.1, bf16[64,512]{1,0:T(8,128)(2,1)} %bitcast.25, bf16[256,1024]{1,0:T(8,128)(2,1)} %table_ref.3), custom_call_target="tpu_custom_call" | custom-call | tf_op jit(solution)/shard_map/pallas_call | solution.py:500
  3.9 15.7 %all-to-all-start = ((bf16[16,48,128]{2,1,0:T(8,128)(2,1)}), bf16[16,48,128]{2,1,0:T(8,128)(2,1)S(1)}, u32[]{:S(2)}, u32[]{:S(2)}) async-start(bf16[16,48,128]{2,1,0:T(8,128)(2,1)} %shard_map.130), calls=%async_computation | async-start | bytes 393216 | tf_op jit(solution)/shard_map/all_to_all | solution.py:477
  19.6 0.0 copy-start.10
  19.6 0.7 copy-done.10
  20.4 0.7 copy-done.11
  21.0 0.7 copy-done.13
  21.7 0.7 copy-done.14
  22.4 0.7 copy-done.15
  23.0 0.7 copy-done.16
  23.7 4.5 %shard_map.131 = (bf16[512,1024]{1,0:T(8,128)(2,1)S(1)}, f32[512,128]{1,0:T(8,128)S(1)}, bf16[16,128]{1,0:T(8,128)(2,1)S(1)}, bf16[512,1024]{1,0:T(8,128)(2,1)S(...) custom-call(s32[4]{0:T(128)S(1)} %pad_add_fusion.where, ...), custom_call_target="tpu_custom_call" | custom-call | tf_op jit(solution)/shard_map/pallas_call | solution.py:515
  28.2 0.0 copy-start.1
  28.2 1.0 copy-done.1
  29.1 1.0 copy-done.2
  30.2 0.8 copy-done.3
  31.0 0.0 copy-done.17
  31.0 1.1 all-to-all-done.got
  32.1 0.2 shard_map.132
  32.3 12.1 %all_to_all.30 = bf16[4,720,128]{2,1,0:T(8,128)(2,1)S(1)} all-to-all(bf16[4,720,128]{2,1,0:T(8,128)(2,1)S(1)} %shard_map.132), channel_id=1, replica_groups={{0,128,256,384},{32,160,288,416},{64,192,320,448},{96,224,352,480},{16,..., dimensions={0} | all-to-all | bytes 1474560 | tf_op jit(solution)/shard_map/all_to_all | solution.py:477
  44.3 0.4 broadcast_in_dim.21
  44.7 24.0 %all_to_all.31 = bf16[4,2880,128]{2,1,0:T(8,128)(2,1)S(1)} all-to-all(bf16[4,2880,128]{2,1,0:T(8,128)(2,1)S(1)} %broadcast_in_dim.21), channel_id=1, replica_groups={{0,32,64,96},{128,160,192,224},{256,288,320,352},{384,416,448,480},{16,..., dimensions={0} | all-to-all | bytes 5898240 | tf_op jit(solution)/shard_map/all_to_all | solution.py:477
  68.8 9.3 %collective-permute-start = (bf16[16,720,128]{2,1,0:T(8,128)(2,1)S(1)}, bf16[16,720,128]{2,1,0:T(8,128)(2,1)}, u32[]{:S(2)}, u32[]{:S(2)}) collective-permute-start(bf16[16,720,128]{2,1,0:T(8,128)(2,1)S(1)} %bitcast.15), channel_id=1, source_target_pairs={{0,16},{16,0},{32,48},{48,32},{64,80},{80,64},{96,112},{112,96},{1... | collective-permute-start | bytes 8847368 | tf_op jit(solution)/shard_map/ppermute | solution.py:554
  78.1 4.5 %all-to-all-start.3 = ((bf16[32,16,1024]{2,1,0:T(8,128)(2,1)}), bf16[32,16,1024]{2,1,0:T(8,128)(2,1)}, u32[]{:S(2)}, u32[]{:S(2)}) async-start(bf16[32,16,1024]{2,1,0:T(8,128)(2,1)} %bitcast.17), calls=%async_computation.3 | async-start | bytes 2097152 | tf_op jit(solution)/shard_map/all_to_all | solution.py:477
  82.5 0.6 collective-permute-done.w1_ref
  83.2 7.2 %shard_map.133 = (bf16[512,1024]{1,0:T(8,128)(2,1)S(1)}, bf16[256,1024]{1,0:T(8,128)(2,1)S(1)}, bf16[256,1024]{1,0:T(8,128)(2,1)S(1)}, bf16[256,512]{1,0:T(8,128...) custom-call(bf16[512,1024]{1,0:T(8,128)(2,1)} %copy-done.1, ...), custom_call_target="tpu_custom_call" | custom-call | tf_op jit(solution)/shard_map/pallas_call | solution.py:557
  90.3 0.0 copy-start.5
  90.4 0.0 copy-start.7
  90.4 0.0 copy-done.4
  90.4 0.0 copy-start
  90.4 0.0 copy-start.12
  90.4 4.2 %shard_map.134 = (bf16[512,1024]{1,0:T(8,128)(2,1)}, bf16[16,32,512]{2,1,0:T(8,128)(2,1)S(1)}, bf16[528,512]{1,0:T(8,128)(2,1)S(1)}, f32[1,512]{1,0:T(1,128)S(1)}) custom-call(s32[4]{0:T(128)S(1)} %pad_add_fusion.where, bf16[512,1024]{1,0:T(8,128)(2,1)S(1)} %get-tuple-element.40.out_ref, bf16[256,1024]{1,0:T(8,128)(2,1)S(1)} %copy-done.4, ...), custom_call_target="tpu_custom_call" | custom-call | tf_op jit(solution)/shard_map/pallas_call | solution.py:583
  94.6 2.3 %collective-permute-start.1 = (bf16[528,512]{1,0:T(8,128)(2,1)S(1)}, bf16[528,512]{1,0:T(8,128)(2,1)S(1)}, u32[]{:S(2)}, u32[]{:S(2)}) collective-permute-start(bf16[528,512]{1,0:T(8,128)(2,1)S(1)} %get-tuple-element.46), channel_id=1, source_target_pairs={{0,16},{16,0},{32,48},{48,32},{64,80},{80,64},{96,112},{112,96},{1... | collective-permute-start | bytes 1622024 | tf_op jit(solution)/shard_map/ppermute | solution.py:595
  96.9 1.5 %collective-permute-done.1.got_ref = bf16[528,512]{1,0:T(8,128)(2,1)S(1)} collective-permute-done((bf16[528,512]{1,0:T(8,128)(2,1)S(1)}, bf16[528,512]{1,0:T(8,128)(2,1)S(1)}, u32[]{:S(2)}, u32[]{:S(2)}) %collective-permute-start.1) | collective-permute-done | bytes 540704 | tf_op jit(solution)/shard_map/ppermute | solution.py:595
  98.4 0.0 copy-done.5
  98.4 0.0 copy-done.7
  98.4 1.0 shard_map.135
  99.5 0.0 all-to-all-done.3
  99.5 18.0 %all_to_all.32.got_ref = bf16[16,40,512]{2,1,0:T(8,128)(2,1)S(1)} all-to-all(bf16[16,40,512]{2,1,0:T(8,128)(2,1)} %shard_map.135), channel_id=1, replica_groups={{0,32,64,96,128,160,192,224,256,288,320,352,384,416,448,480},{16,48,80,..., dimensions={0} | all-to-all | bytes 1310720 | tf_op jit(solution)/shard_map/all_to_all | solution.py:477
  117.4 0.8 shard_map.137
  118.2 6.8 %all-to-all-start.5 = ((bf16[16,16,128]{2,1,0:T(8,128)(2,1)}), bf16[16,16,128]{2,1,0:T(8,128)(2,1)S(1)}, u32[]{:S(2)}, u32[]{:S(2)}) async-start(bf16[16,16,128]{2,1,0:T(8,128)(2,1)} %bitcast.12), calls=%async_computation.5 | async-start | bytes 131072 | tf_op jit(solution)/shard_map/all_to_all | solution.py:477
  125.0 0.0 copy-start.6
  125.0 1.0 copy-done.6
  126.1 1.0 copy-done.8
  127.1 7.1 %shard_map.136 = bf16[256,1024]{1,0:T(8,128)(2,1)} custom-call(s32[4]{0:T(128)S(1)} %pad_add_fusion.where, bf16[512,1024]{1,0:T(8,128)(2,1)} %bitcast.11.got_ref, f32[1,1024]{1,0:T(1,128)S(1)} %bitcast.22, bf16[256,1024]{1,0:T(8,128)(2,1)S(1)} %copy-done.6, bf16[256,1024]{1,0:T(8,128)(2,1)S(1)} %copy-done.8, f32[1,512]{1,0:T(1,128)S(1)} %bitcast.20, ...), custom_call_target="tpu_custom_call" | custom-call | tf_op jit(solution)/shard_map/pallas_call | solution.py:602
  134.2 2.4 %all-to-all-done.5 = bf16[16,16,128]{2,1,0:T(8,128)(2,1)S(1)} async-done(((bf16[16,16,128]{2,1,0:T(8,128)(2,1)}), bf16[16,16,128]{2,1,0:T(8,128)(2,1)S(1)}, u32[]{:S(2)}, u32[]{:S(2)}) %all-to-all-start.5) | async-done | bytes 65568 | tf_op jit(solution)/shard_map/all_to_all | solution.py:477
  136.6 0.8 shard_map.138
  (14 shorter events, 0.0 us)
Async XLA Ops:
  0.6 30.4 %copy-start.17 = (f32[512]{0:T(512)S(1)}, f32[512]{0:T(512)}, u32[]{:S(2)}) copy-start(f32[512]{0:T(512)} %param.20) | copy-start | bytes 6148
  0.7 0.7 copy-start.9
  3.9 28.2 %all-to-all-start = ((bf16[16,48,128]{2,1,0:T(8,128)(2,1)}), bf16[16,48,128]{2,1,0:T(8,128)(2,1)S(1)}, u32[]{:S(2)}, u32[]{:S(2)}) async-start(bf16[16,48,128]{2,1,0:T(8,128)(2,1)} %shard_map.130), calls=%async_computation | async-start | bytes 393216 | tf_op jit(solution)/shard_map/all_to_all | solution.py:477
  19.6 0.7 copy-start.10
  20.4 0.7 copy-start.11
  21.0 0.7 copy-start.13
  21.7 0.7 copy-start.14
  22.4 0.7 copy-start.15
  23.0 0.7 copy-start.16
  28.2 1.0 copy-start.1
  29.1 1.0 copy-start.2
  30.2 0.8 copy-start.3
  68.8 14.4 %collective-permute-start = (bf16[16,720,128]{2,1,0:T(8,128)(2,1)S(1)}, bf16[16,720,128]{2,1,0:T(8,128)(2,1)}, u32[]{:S(2)}, u32[]{:S(2)}) collective-permute-start(bf16[16,720,128]{2,1,0:T(8,128)(2,1)S(1)} %bitcast.15), channel_id=1, source_target_pairs={{0,16},{16,0},{32,48},{48,32},{64,80},{80,64},{96,112},{112,96},{1... | collective-permute-start | bytes 8847368 | tf_op jit(solution)/shard_map/ppermute | solution.py:554
  78.1 21.4 %all-to-all-start.3 = ((bf16[32,16,1024]{2,1,0:T(8,128)(2,1)}), bf16[32,16,1024]{2,1,0:T(8,128)(2,1)}, u32[]{:S(2)}, u32[]{:S(2)}) async-start(bf16[32,16,1024]{2,1,0:T(8,128)(2,1)} %bitcast.17), calls=%async_computation.3 | async-start | bytes 2097152 | tf_op jit(solution)/shard_map/all_to_all | solution.py:477
  83.2 7.2 %copy-start.4 = (bf16[256,1024]{1,0:T(8,128)(2,1)S(1)}, bf16[256,1024]{1,0:T(8,128)(2,1)}, u32[]{:S(2)}) copy-start(bf16[256,1024]{1,0:T(8,128)(2,1)} %copy-done.3) | copy-start | bytes 1572868
  90.3 8.1 %copy-start.5 = (bf16[256,1024]{1,0:T(8,128)(2,1)}, bf16[256,1024]{1,0:T(8,128)(2,1)S(1)}, u32[]{:S(2)}) copy-start(bf16[256,1024]{1,0:T(8,128)(2,1)S(1)} %get-tuple-element.49.o0) | copy-start | bytes 1572868
  90.4 8.1 %copy-start.7 = (bf16[256,1024]{1,0:T(8,128)(2,1)}, bf16[256,1024]{1,0:T(8,128)(2,1)S(1)}, u32[]{:S(2)}) copy-start(bf16[256,1024]{1,0:T(8,128)(2,1)S(1)} %get-tuple-element.50.o1) | copy-start | bytes 1572868
  90.4 34.6 %copy-start = (bf16[16,720,128]{2,1,0:T(8,128)(2,1)S(1)}, bf16[16,720,128]{2,1,0:T(8,128)(2,1)}, u32[]{:S(2)}) copy-start(bf16[16,720,128]{2,1,0:T(8,128)(2,1)} %get-tuple-element.53.w0_ref) | copy-start | bytes 8847364
  90.4 34.6 %copy-start.12 = (f32[1024]{0:T(1024)S(1)}, f32[1024]{0:T(1024)}, u32[]{:S(2)}) copy-start(f32[1024]{0:T(1024)} %param.18) | copy-start | bytes 12292
  94.6 3.8 %collective-permute-start.1 = (bf16[528,512]{1,0:T(8,128)(2,1)S(1)}, bf16[528,512]{1,0:T(8,128)(2,1)S(1)}, u32[]{:S(2)}, u32[]{:S(2)}) collective-permute-start(bf16[528,512]{1,0:T(8,128)(2,1)S(1)} %get-tuple-element.46), channel_id=1, source_target_pairs={{0,16},{16,0},{32,48},{48,32},{64,80},{80,64},{96,112},{112,96},{1... | collective-permute-start | bytes 1622024 | tf_op jit(solution)/shard_map/ppermute | solution.py:595
  118.2 18.4 %all-to-all-start.5 = ((bf16[16,16,128]{2,1,0:T(8,128)(2,1)}), bf16[16,16,128]{2,1,0:T(8,128)(2,1)S(1)}, u32[]{:S(2)}, u32[]{:S(2)}) async-start(bf16[16,16,128]{2,1,0:T(8,128)(2,1)} %bitcast.12), calls=%async_computation.5 | async-start | bytes 131072 | tf_op jit(solution)/shard_map/all_to_all | solution.py:477
  125.0 1.0 copy-start.6
  126.1 1.0 copy-start.8

commit v7 on v6

--- a/solution.py
+++ b/solution.py
@@ -72,7 +72,7 @@
 
 
 def message_body(
-    where, neg_ref, w_ref, o_ref, table_ref, out_ref, w_part, o_part, rows, turned, quads, sems
+    where, neg_ref, w_ref, o_ref, table_ref, out_ref, neg, w_part, o_part, rows, turned, quads, sems
 ):
     item, core, place = where[0], where[1], where[2]
     chunk = lax.div(place, 2)
@@ -85,16 +85,17 @@
             o_ref.at[:, pl.ds((core * 2 + place // 8) * LANES, LANES)], o_part, sems.at[1]
         ),
         pltpu.make_async_copy(table_ref.at[:, pl.ds(core * 512, 512)], rows, sems.at[2]),
+        pltpu.make_async_copy(neg_ref, neg, sems.at[3]),
     )
     for copy in copies:
         copy.start()
+    for copy in copies:
+        copy.wait()
     lane = lax.broadcasted_iota(jnp.int32, (ITEMS, 256), 1)
     ids = jnp.sum(
-        jnp.where(lane == item * 16 + place, neg_ref[...].astype(F32), 0.0), axis=1, keepdims=True
+        jnp.where(lane == item * 16 + place, neg[...].astype(F32), 0.0), axis=1, keepdims=True
     ).astype(jnp.int32)
     pick = jnp.where(lane == ids - item * 256, 1.0, 0.0).astype(BF16)
-    for copy in copies:
-        copy.wait()
     turned[...] = jnp.transpose(o_part[...].astype(F32))
     part = turned[pl.ds((place % 8) * 16, 16), :]
     part = jnp.concatenate([part[0:8, :], part[8:16, :]], axis=1).astype(BF16)
@@ -108,41 +109,29 @@
     out_ref[:, 40:48, :] = quads[...].astype(BF16)
 
 
-def prepare_body(
-    where,
-    tok_ref,
-    len_ref,
-    dest_ref,
-    off_ref,
-    pos_ref,
-    in_gain,
-    table_ref,
-    neg_ref,
-    x_ref,
-    cols_ref,
-    label_ref,
-    parcel_ref,
-    low_ref,
-    hat_ref,
-    scale_ref,
-    hits_ref,
-    tok,
-    tab,
-    hat,
-    turned,
-    sems,
-):
-    item, user = where[0], where[3]
-    copies = (
-        pltpu.make_async_copy(tok_ref, tok, sems.at[0]),
-        pltpu.make_async_copy(table_ref, tab, sems.at[1]),
-    )
+def prepare_body(where, *refs):
+    sources, results = refs[:9], refs[9:18]
+    scratch, (xs, parcels, lows, hat, turned, in_sems, out_sems) = refs[18:27], refs[27:]
+    x_ref, cols_ref, label_ref, parcel_ref, low_ref, hat_ref, scale_ref, ids_ref, gain_ref = results
+    tok, len_ref, dest_ref, off_ref, pos_ref, in_gain, tab, neg_ref, out_gain = scratch
+    item, core, user = where[0], where[1], where[3]
+    copies = [
+        pltpu.make_async_copy(a, b, in_sems.at[n]) for n, (a, b) in enumerate(zip(sources, scratch))
+    ]
     for copy in copies:
         copy.start()
     for copy in copies:
         copy.wait()
+    late = [
+        pltpu.make_async_copy(a, b, out_sems.at[n])
+        for n, (a, b) in enumerate(((xs, x_ref), (parcels, parcel_ref), (lows, low_ref)))
+    ]
+    gain = out_gain[...]
+    turned_gain = jnp.concatenate([gain[:, 256:512], gain[:, 0:256]], axis=1)
+    gain_ref[...] = jnp.where(core == 0, gain, turned_gain)
     normed = layer_norm(tok[...].astype(F32), in_gain[...]).astype(BF16)
-    x_ref[...] = reordered(normed)
+    xs[...] = reordered(normed)
+    late[0].start()
 
     lens, dest, off = (r[...].astype(F32) for r in (len_ref, dest_ref, off_ref))
     sub = lax.broadcasted_iota(jnp.int32, (32, 32), 0)
@@ -176,21 +165,24 @@
     within = (slot[:, 0:1] % MOST).astype(F32)
     source = jnp.where(within < count, begin + within, -1.0)
     send = lax.broadcasted_iota(jnp.int32, (ROWS, ROWS), 1).astype(F32) == source
-    parcel_ref[...] = dot(jnp.where(send, 1.0, 0.0).astype(BF16), tok[...]).astype(BF16)
+    parcels[...] = dot(jnp.where(send, 1.0, 0.0).astype(BF16), tok[...]).astype(BF16)
+    late[1].start()
 
     table = tab[...].astype(F32)
     scale = lax.rsqrt(jnp.mean(table * table, axis=1, keepdims=True) + scale_epsilon)
     hat[...] = table * scale
-    low_ref[...] = hat[...].astype(BF16)
+    lows[...] = hat[...].astype(BF16)
+    late[2].start()
     turned[...] = jnp.transpose(hat[:, pl.ds((user // 4) * LANES, LANES)])
     hat_ref[...] = turned[pl.ds((user % 4) * 32, 32), :]
     scale_ref[...] = jnp.transpose(jnp.broadcast_to(scale, (256, LANES)))[0:1, :]
 
-    ids = jnp.broadcast_to(neg_ref[...].astype(F32)[:, None, :], (ITEMS, 16, 256)).reshape(256, 256)
-    spot = lax.broadcasted_iota(jnp.int32, (256, 256), 0) % 16 + item * 16
-    lanes = lax.broadcasted_iota(jnp.int32, (256, 256), 1)
-    ids = jnp.sum(jnp.where(lanes == spot, ids, 0.0), axis=1, keepdims=True)
-    hits_ref[...] = jnp.where(lanes.astype(F32) == ids - (item * 256).astype(F32), 1.0, 0.0).astype(BF16)
+    sub = lax.broadcasted_iota(jnp.int32, (ITEMS, 256), 0)
+    group = jnp.sum(jnp.where(sub == item, neg_ref[...].astype(F32), 0.0), axis=0, keepdims=True)
+    owner = lax.broadcasted_iota(jnp.int32, (1, 256), 1) // 16
+    ids_ref[...] = group - (owner * 256).astype(F32)
+    for copy in late:
+        copy.wait()
 
 
 def forward_body(got, label, out):
@@ -259,13 +251,15 @@
     cols_ref,
     gain_ref,
     out_ref,
-    o0,
-    o1,
+    o0_ref,
+    o1_ref,
     g0,
     g1,
     near,
     far,
     kept_ref,
+    o0,
+    o1,
     x,
     w1,
     tok,
@@ -274,13 +268,12 @@
     m1,
     sems,
 ):
-    copies = [
-        pltpu.make_async_copy(a, b, sems.at[n])
-        for n, (a, b) in enumerate(((x_ref, x), (w1_ref, w1), (tok_ref, tok), (w0, kept_ref)))
-    ]
-    for copy in copies:
+    pairs = ((x_ref, x), (w1_ref, w1), (tok_ref, tok), (w0, kept_ref), (o0, o0_ref), (o1, o1_ref))
+    copies = [pltpu.make_async_copy(a, b, sems.at[n]) for n, (a, b) in enumerate(pairs)]
+    for copy in copies[:3]:
         copy.start()
     split_rest(w0, o0, g0, near)
+    copies[4].start()
     first = cols_ref[:, 0:1].astype(jnp.int32)
     copies[0].wait()
     rows = x[...]
@@ -288,13 +281,16 @@
         act[0, q] = project(rows, w0, q)
     attend(act.at[0], first, m0)
     copies[1].wait()
+    copies[3].start()
     split_rest(w1, o1, g1, far)
+    copies[5].start()
     for q in range(4):
         act[1, q] = project(rows, w1, q)
     attend(act.at[1], first, m1)
     copies[2].wait()
     out_ref[...] = gated_out(tok[...], act.at[0, 0], m0, o0, act.at[1, 0], m1, o1, gain_ref)
-    copies[3].wait()
+    for copy in copies[3:]:
+        copy.wait()
 
 
 def gated_out(rows, u0, m0, o0, u1, m1, o1, gain_ref):
@@ -316,8 +312,8 @@
     where,
     got_ref,
     in_gain,
-    o0,
-    o1,
+    o0_ref,
+    o1_ref,
     gain_ref,
     near,
     far,
@@ -326,15 +322,16 @@
     out_ref,
     w0,
     w1,
+    o0,
+    o1,
     act,
     m0,
     m1,
     sems,
 ):
     core, user = where[1], where[3]
-    copies = [
-        pltpu.make_async_copy(a, b, sems.at[n]) for n, (a, b) in enumerate(((w0_ref, w0), (w1_ref, w1)))
-    ]
+    pairs = ((w0_ref, w0), (w1_ref, w1), (o0_ref, o0), (o1_ref, o1))
+    copies = [pltpu.make_async_copy(a, b, sems.at[n]) for n, (a, b) in enumerate(pairs)]
     for copy in copies:
         copy.start()
     lane = lax.broadcasted_iota(jnp.int32, (PLANE, LANES), 1)
@@ -366,6 +363,8 @@
         for q in range(4):
             act[half, q] = project(moved, w, q)
         attend(act.at[half], first, m)
+    copies[2].wait()
+    copies[3].wait()
     out_ref[...] = gated_out(rows, act.at[0, 0], m0, o0, act.at[1, 0], m1, o1, gain_ref)
 
 
@@ -440,7 +439,7 @@
         out_ref[k, 32:40, :] = tail[0:8, :]
 
 
-def plane_body(got_ref, pos_ref, neg_ref):
+def plane_body(got_ref, ids_ref, pos_ref, neg_ref):
     acc = got_ref[0].astype(F32)
     for k in range(1, PLANE):
         acc = acc + got_ref[k].astype(F32)
@@ -448,12 +447,18 @@
     top = inner.astype(BF16).astype(F32)
     full = jnp.concatenate([acc[0:32, :], split_rows(top, inner - top)], axis=0)
     pos_ref[...] = full[:, 0:256]
-    tail = jnp.concatenate([full[:, 256:512], jnp.zeros((80, 256), F32)], axis=0)
+    tail = jnp.concatenate(
+        [full[0:34, 256:512], ids_ref[...], jnp.zeros((93, 256), F32)], axis=0
+    )
     neg_ref[...] = jnp.transpose(tail).astype(BF16)
 
 
-def item_body(pos_ref, hits_ref, got_ref, hat_ref, scale_ref, out_ref):
-    total = pos_ref[...] + dot(got_ref[...], hits_ref[...], ((0,), (0,)))[0:48, :]
+def item_body(pos_ref, got_ref, hat_ref, scale_ref, out_ref):
+    got = got_ref[...]
+    ids = got.astype(F32)[:, 34:35]
+    hits = lax.broadcasted_iota(jnp.int32, (256, 256), 1).astype(F32) == ids
+    hits = jnp.where(hits, 1.0, 0.0).astype(BF16)
+    total = pos_ref[...] + dot(got, hits, ((0,), (0,)))[0:48, :]
     inner = (total[32:33, :] + total[33:34, :]) / WIDTH
     out_ref[...] = (total[0:32, :] - hat_ref[...] * inner) * scale_ref[...]
 
@@ -500,51 +505,70 @@
     first_message = call(
         message_body,
         shape((ITEMS, 48, LANES)),
-        [SMEM, VMEM, HBM, HBM, HBM],
+        [SMEM, HBM, HBM, HBM, HBM],
         scratch=[
+            pltpu.VMEM((ITEMS, 256), jnp.int32),
             pltpu.VMEM((32, LANES), BF16),
             pltpu.VMEM((64, LANES), BF16),
             pltpu.VMEM((256, 512), BF16),
             pltpu.VMEM((LANES, 64), F32),
             pltpu.VMEM((ITEMS, 8, LANES), F32),
-            pltpu.SemaphoreType.DMA((3,)),
+            pltpu.SemaphoreType.DMA((4,)),
         ],
-    )(where, negatives, in_hbm(w_uvqk), in_hbm(w_out.T), in_hbm(table))
+    )(where, in_hbm(negatives), in_hbm(w_uvqk), in_hbm(w_out.T), in_hbm(table))
     got = exchange(first_message, "item")
 
-    x_rows, cols, labels, parcels, table_low, hat_part, table_scale, hits = call(
+    x_rows, cols, labels, parcels, table_low, hat_part, table_scale, group_ids, gain = call(
         prepare_body,
         (
-            shape((ROWS, WIDTH)),
+            pltpu.HBM((ROWS, WIDTH), BF16),
             shape((ROWS, LANES), F32),
             shape((16, LANES)),
-            shape((ROWS, WIDTH)),
-            shape((256, WIDTH)),
+            pltpu.HBM((ROWS, WIDTH), BF16),
+            pltpu.HBM((256, WIDTH), BF16),
             shape((32, 256), F32),
             shape((1, 256), F32),
-            shape((256, 256)),
+            shape((1, 256), F32),
+            shape((1, 512), F32),
         ),
-        [SMEM, HBM] + [VMEM] * 5 + [HBM, VMEM],
+        [SMEM] + [HBM] * 9,
         scratch=[
+            pltpu.VMEM((ROWS, WIDTH), BF16),
+            pltpu.VMEM((1, 32), jnp.int32),
+            pltpu.VMEM((1, 32), jnp.int32),
+            pltpu.VMEM((1, 32), jnp.int32),
+            pltpu.VMEM((1, ROWS), jnp.int32),
+            pltpu.VMEM((1, WIDTH), F32),
+            pltpu.VMEM((256, WIDTH), BF16),
+            pltpu.VMEM((ITEMS, 256), jnp.int32),
+            pltpu.VMEM((1, 512), F32),
+            pltpu.VMEM((ROWS, WIDTH), BF16),
             pltpu.VMEM((ROWS, WIDTH), BF16),
             pltpu.VMEM((256, WIDTH), BF16),
             pltpu.VMEM((256, WIDTH), F32),
             pltpu.VMEM((LANES, 256), F32),
-            pltpu.SemaphoreType.DMA((2,)),
+            pltpu.SemaphoreType.DMA((9,)),
+            pltpu.SemaphoreType.DMA((3,)),
         ],
-        mib=24,
+        mib=28,
+        out_specs=(HBM, VMEM, VMEM, HBM, HBM, VMEM, VMEM, VMEM, VMEM),
     )(
         where,
-        in_hbm(tokens),
-        lengths,
-        destination,
-        worker_offset,
-        positives[None],
-        in_gain[None],
-        in_hbm(table),
-        negatives,
-    )
-    gain = jnp.where(core == 0, out_gain, jnp.roll(out_gain, 256))[None]
+        *(
+            in_hbm(v)
+            for v in (
+                tokens,
+                lengths,
+                destination,
+                worker_offset,
+                positives[None],
+                in_gain[None],
+                table,
+                negatives,
+                out_gain[None],
+            )
+        ),
+    )
     got, x_rows, gain = lax.optimization_barrier((got, x_rows, gain))
 
     message = call(forward_body, shape((4, W_ROWS + REST, LANES)), [VMEM, VMEM])(got, labels)
@@ -558,8 +582,8 @@
         layer_body,
         (
             shape((ROWS, WIDTH)),
-            shape((256, WIDTH)),
-            shape((256, WIDTH)),
+            pltpu.HBM((256, WIDTH), BF16),
+            pltpu.HBM((256, WIDTH), BF16),
             shape((256, 512)),
             shape((256, 512)),
             shape((PLANE, LANES), F32),
@@ -568,16 +592,18 @@
         ),
         [HBM, VMEM, HBM, HBM, VMEM, VMEM],
         scratch=[
+            pltpu.VMEM((256, WIDTH), BF16),
+            pltpu.VMEM((256, WIDTH), BF16),
             pltpu.VMEM((ROWS, WIDTH), BF16),
             pltpu.VMEM((PLANE, W_ROWS + REST, LANES), BF16),
             pltpu.VMEM((ROWS, WIDTH), BF16),
             pltpu.VMEM((2, 4, ROWS, 256), BF16),
             pltpu.VMEM((ROWS, 256), F32),
             pltpu.VMEM((ROWS, 256), F32),
-            pltpu.SemaphoreType.DMA((4,)),
+            pltpu.SemaphoreType.DMA((6,)),
         ],
         mib=20,
-        out_specs=(VMEM,) * 7 + (HBM,),
+        out_specs=(VMEM, HBM, HBM, VMEM, VMEM, VMEM, VMEM, HBM),
     )(in_hbm(x_rows), held, in_hbm(held_other), in_hbm(tokens), cols, gain)
 
     token_grad, own_terms, sent, own_inner = call(
@@ -602,24 +628,26 @@
     layer_out = call(
         worker_body,
         shape((256, WIDTH)),
-        [SMEM] + [VMEM] * 7 + [HBM] * 2,
+        [SMEM, VMEM, VMEM, HBM, HBM, VMEM, VMEM, VMEM, HBM, HBM],
         scratch=[
             pltpu.VMEM((PLANE, W_ROWS + REST, LANES), BF16),
             pltpu.VMEM((PLANE, W_ROWS + REST, LANES), BF16),
+            pltpu.VMEM((256, WIDTH), BF16),
+            pltpu.VMEM((256, WIDTH), BF16),
             pltpu.VMEM((2, 4, 256, 256), BF16),
             pltpu.VMEM((256, 256), F32),
             pltpu.VMEM((256, 256), F32),
-            pltpu.SemaphoreType.DMA((2,)),
+            pltpu.SemaphoreType.DMA((4,)),
         ],
         mib=24,
     )(where, arrived, in_gain[None], o_own, o_other, gain, near, far, kept, in_hbm(held_other))
 
     positive_part, negative_part = call(
-        plane_body, (shape((48, 256), F32), shape((256, LANES))), [VMEM]
-    )(plane)
+        plane_body, (shape((48, 256), F32), shape((256, LANES))), [VMEM] * 2
+    )(plane, group_ids)
     owned = exchange(negative_part.reshape(ITEMS, 16, LANES), "item").reshape(256, LANES)
-    item_grad = call(item_body, shape((32, 256), F32), [VMEM] * 5)(
-        positive_part, hits, owned, hat_part, table_scale
+    item_grad = call(item_body, shape((32, 256), F32), [VMEM] * 4)(
+        positive_part, owned, hat_part, table_scale
     ).T
     return (layer_out, token_grad, item_grad)
 

time: 139 us -> 139 us (level)
  waiting for transfers between devices: 5.66 us -> 9.29 us
  local copies, waits for them, and re-layouts: 10.1 us -> 8.02 us
  starting transfers between devices: 38.6 us -> 36.6 us
    all_to_all x3, waiting for transfers between devices: 3.48 us -> 7.11 us  [exchange(): lax.all_to_all(blocks, axis, 0, 0, tiled=True, axis_index_groups=groups)]
    all_to_all x3, starting transfers between devices: 27 us -> 24.9 us  [exchange(): lax.all_to_all(blocks, axis, 0, 0, tiled=True, axis_index_groups=groups)]
    unnamed x36 -> x32, local copies, waits for them, and re-layouts: 9.68 us -> 7.64 us
  transfers between devices with their start and end apart: 5 -> 5, of which waited for: 4 -> 4; matrix products, arithmetic and copies ran while one was open for 0% -> 0% of each run, Pallas kernels for 17% -> 18%
where the time goes in v7:
time: 139 us; the launch traced here: 138 us
  blocking collectives  54.1 us (39%)
  starting transfers between devices  36.6 us (26%)
  Pallas kernels  28.7 us (21%)
  waiting for transfers between devices  9.29 us (7%)
  local copies, waits for them, and re-layouts  8.02 us (6%)
    all_to_all x3, blocking collectives, exchange(): lax.all_to_all(blocks, axis, 0, 0, tiled=True, axis_index_groups=groups)  54.1 us
    all_to_all x3, starting transfers between devices, exchange(): lax.all_to_all(blocks, axis, 0, 0, tiled=True, axis_index_groups=groups)  24.9 us
    ppermute x1, starting transfers between devices, per_device(): held_other = lax.ppermute(held, 'user', PARTNER)  9.3 us
    unnamed x32, local copies, waits for them, and re-layouts  7.64 us
    pallas_call x1, Pallas kernels, per_device(): call(worker_body, shape((256, WIDTH)), [SMEM, VMEM, VMEM, HBM, HBM, VMEM,...  7.31 us
    all_to_all x3, waiting for transfers between devices, exchange(): lax.all_to_all(blocks, axis, 0, 0, tiled=True, axis_index_groups=groups)  7.11 us
    pallas_call x1, Pallas kernels, per_device(): call(layer_body, (shape((ROWS, WIDTH)), pltpu.HBM((256, WIDTH), BF16), pl...  6.51 us
    pallas_call x1, Pallas kernels, per_device(): call(prepare_body, (pltpu.HBM((ROWS, WIDTH), BF16), shape((ROWS, LANES),...  5.99 us
  transfers between devices with their start and end apart: 5, of which 4 were waited for; matrix products, arithmetic and copies ran while one was open for 0% of the time, Pallas kernels for 18%

profile of v7, /device:TPU:1, one launch (start us, length us, event | category | flops | bytes accessed | tf_op | source)
XLA Modules:
  0.0 137.5 jit_solution(2508310170177170476)
XLA Ops:
  0.6 0.1 pad_add_fusion.where
  0.7 2.5 %shard_map.130 = bf16[16,48,128]{2,1,0:T(8,128)(2,1)} custom-call(s32[4]{0:T(128)S(1)} %pad_add_fusion.where, s32[16,256]{1,0:T(8,128)} %refs_7_.1, bf16[64,2048]{1,0:T(8,128)(2,1)} %w_ref.1, bf16[64,512]{1,0:T(8,128)(2,1)} %bitcast.23, bf16[256,1024]{1,0:T(8,128)(2,1)} %refs_6_.1), custom_call_target="tpu_custom_call" | custom-call | tf_op jit(solution)/shard_map/pallas_call | solution.py:505
  3.2 15.7 %all-to-all-start = ((bf16[16,48,128]{2,1,0:T(8,128)(2,1)}), bf16[16,48,128]{2,1,0:T(8,128)(2,1)S(1)}, u32[]{:S(2)}, u32[]{:S(2)}) async-start(bf16[16,48,128]{2,1,0:T(8,128)(2,1)} %shard_map.130), calls=%async_computation | async-start | bytes 393216 | tf_op jit(solution)/shard_map/all_to_all | solution.py:482
  19.0 6.0 %shard_map.131 = (bf16[512,1024]{1,0:T(8,128)(2,1)}, f32[512,128]{1,0:T(8,128)S(1)}, bf16[16,128]{1,0:T(8,128)(2,1)S(1)}, bf16[512,1024]{1,0:T(8,128)(2,1)}, bf1...) custom-call(s32[4]{0:T(128)S(1)} %pad_add_fusion.where, ...), custom_call_target="tpu_custom_call" | custom-call | tf_op jit(solution)/shard_map/pallas_call | solution.py:521
  25.0 0.0 copy-start.7
  25.0 0.6 copy-done.7
  25.6 0.0 copy-start.14
  25.6 0.6 copy-done.14
  26.1 0.0 copy-start.12
  26.2 5.3 %all-to-all-done.got = bf16[16,48,128]{2,1,0:T(8,128)(2,1)S(1)} async-done(((bf16[16,48,128]{2,1,0:T(8,128)(2,1)}), bf16[16,48,128]{2,1,0:T(8,128)(2,1)S(1)}, u32[]{:S(2)}, u32[]{:S(2)}) %all-to-all-start) | async-done | bytes 196640 | tf_op jit(solution)/shard_map/all_to_all | solution.py:482
  31.5 0.2 shard_map.132
  31.6 12.1 %all_to_all.30 = bf16[4,720,128]{2,1,0:T(8,128)(2,1)S(1)} all-to-all(bf16[4,720,128]{2,1,0:T(8,128)(2,1)S(1)} %shard_map.132), channel_id=1, replica_groups={{0,128,256,384},{32,160,288,416},{64,192,320,448},{96,224,352,480},{16,..., dimensions={0} | all-to-all | bytes 1474560 | tf_op jit(solution)/shard_map/all_to_all | solution.py:482
  43.7 0.4 broadcast_in_dim.21
  44.1 24.0 %all_to_all.31 = bf16[4,2880,128]{2,1,0:T(8,128)(2,1)S(1)} all-to-all(bf16[4,2880,128]{2,1,0:T(8,128)(2,1)S(1)} %broadcast_in_dim.21), channel_id=1, replica_groups={{0,32,64,96},{128,160,192,224},{256,288,320,352},{384,416,448,480},{16,..., dimensions={0} | all-to-all | bytes 5898240 | tf_op jit(solution)/shard_map/all_to_all | solution.py:482
  68.1 9.3 %collective-permute-start = (bf16[16,720,128]{2,1,0:T(8,128)(2,1)S(1)}, bf16[16,720,128]{2,1,0:T(8,128)(2,1)}, u32[]{:S(2)}, u32[]{:S(2)}) collective-permute-start(bf16[16,720,128]{2,1,0:T(8,128)(2,1)S(1)} %bitcast.15), channel_id=1, source_target_pairs={{0,16},{16,0},{32,48},{48,32},{64,80},{80,64},{96,112},{112,96},{1... | collective-permute-start | bytes 8847368 | tf_op jit(solution)/shard_map/ppermute | solution.py:578
  77.4 4.5 %all-to-all-start.3 = ((bf16[32,16,1024]{2,1,0:T(8,128)(2,1)}), bf16[32,16,1024]{2,1,0:T(8,128)(2,1)}, u32[]{:S(2)}, u32[]{:S(2)}) async-start(bf16[32,16,1024]{2,1,0:T(8,128)(2,1)} %bitcast.22), calls=%async_computation.3 | async-start | bytes 2097152 | tf_op jit(solution)/shard_map/all_to_all | solution.py:482
  81.9 0.6 collective-permute-done.w1_ref
  82.5 0.0 copy-done.12
  82.5 0.0 copy-start.3
  82.5 6.5 %shard_map.133 = (bf16[512,1024]{1,0:T(8,128)(2,1)S(1)}, bf16[256,1024]{1,0:T(8,128)(2,1)}, bf16[256,1024]{1,0:T(8,128)(2,1)}, bf16[256,512]{1,0:T(8,128)(2,1)S(...) custom-call(bf16[512,1024]{1,0:T(8,128)(2,1)} %get-tuple-element.35., ...), custom_call_target="tpu_custom_call" | custom-call | tf_op jit(solution)/shard_map/pallas_call | solution.py:581
  89.0 0.0 copy-start.10
  89.0 0.6 copy-done.10
  89.6 0.0 copy-done.3
  89.6 0.0 copy-start
  89.6 0.0 copy-start.9
  89.6 4.2 %shard_map.134 = (bf16[512,1024]{1,0:T(8,128)(2,1)}, bf16[16,32,512]{2,1,0:T(8,128)(2,1)S(1)}, bf16[528,512]{1,0:T(8,128)(2,1)S(1)}, f32[1,512]{1,0:T(1,128)S(1)}) custom-call(s32[4]{0:T(128)S(1)} %pad_add_fusion.where, bf16[512,1024]{1,0:T(8,128)(2,1)S(1)} %get-tuple-element.42.out_ref, bf16[256,1024]{1,0:T(8,128)(2,1)S(1)} %copy-done.3, ...), custom_call_target="tpu_custom_call" | custom-call | tf_op jit(solution)/shard_map/pallas_call | solution.py:609
  93.8 2.4 %collective-permute-start.1 = (bf16[528,512]{1,0:T(8,128)(2,1)S(1)}, bf16[528,512]{1,0:T(8,128)(2,1)S(1)}, u32[]{:S(2)}, u32[]{:S(2)}) collective-permute-start(bf16[528,512]{1,0:T(8,128)(2,1)S(1)} %get-tuple-element.48), channel_id=1, source_target_pairs={{0,16},{16,0},{32,48},{48,32},{64,80},{80,64},{96,112},{112,96},{1... | collective-permute-start | bytes 1622024 | tf_op jit(solution)/shard_map/ppermute | solution.py:621
  96.2 1.5 %collective-permute-done.1.got_ref = bf16[528,512]{1,0:T(8,128)(2,1)S(1)} collective-permute-done((bf16[528,512]{1,0:T(8,128)(2,1)S(1)}, bf16[528,512]{1,0:T(8,128)(2,1)S(1)}, u32[]{:S(2)}, u32[]{:S(2)}) %collective-permute-start.1) | collective-permute-done | bytes 540704 | tf_op jit(solution)/shard_map/ppermute | solution.py:621
  97.8 1.0 shard_map.135
  98.8 0.0 all-to-all-done.3
  98.8 18.0 %all_to_all.32.got_ref = bf16[16,40,512]{2,1,0:T(8,128)(2,1)S(1)} all-to-all(bf16[16,40,512]{2,1,0:T(8,128)(2,1)} %shard_map.135), channel_id=1, replica_groups={{0,32,64,96,128,160,192,224,256,288,320,352,384,416,448,480},{16,48,80,..., dimensions={0} | all-to-all | bytes 1310720 | tf_op jit(solution)/shard_map/all_to_all | solution.py:482
  116.8 0.2 shard_map.137
  116.9 0.6 copy-done.5
  117.5 0.6 copy-done.4
  118.2 4.7 %all-to-all-start.5 = ((bf16[16,16,128]{2,1,0:T(8,128)(2,1)}), bf16[16,16,128]{2,1,0:T(8,128)(2,1)S(1)}, u32[]{:S(2)}, u32[]{:S(2)}) async-start(bf16[16,16,128]{2,1,0:T(8,128)(2,1)} %bitcast.18), calls=%async_computation.5 | async-start | bytes 131072 | tf_op jit(solution)/shard_map/all_to_all | solution.py:482
  122.9 0.0 copy-done
  122.9 0.0 copy-done.9
  122.9 0.0 copy-done.1
  122.9 0.0 copy-start.2
  122.9 1.0 copy-done.2
  123.9 0.7 copy-done.11
  124.6 0.7 copy-done.13
  125.3 7.3 %shard_map.136 = bf16[256,1024]{1,0:T(8,128)(2,1)} custom-call(s32[4]{0:T(128)S(1)} %pad_add_fusion.where, bf16[512,1024]{1,0:T(8,128)(2,1)} %bitcast.11.got_ref, f32[1,1024]{1,0:T(1,128)S(1)} %bitcast.20, bf16[256,1024]{1,0:T(8,128)(2,1)S(1)} %copy-done.1, bf16[256,1024]{1,0:T(8,128)(2,1)S(1)} %copy-done.2, f32[1,512]{1,0:T(1,128)S(1)} %copy-done.13, ...), custom_call_target="tpu_custom_call" | custom-call | tf_op jit(solution)/shard_map/pallas_call | solution.py:628
  132.6 1.8 %all-to-all-done.5 = bf16[16,16,128]{2,1,0:T(8,128)(2,1)S(1)} async-done(((bf16[16,16,128]{2,1,0:T(8,128)(2,1)}), bf16[16,16,128]{2,1,0:T(8,128)(2,1)S(1)}, u32[]{:S(2)}, u32[]{:S(2)}) %all-to-all-start.5) | async-done | bytes 65568 | tf_op jit(solution)/shard_map/all_to_all | solution.py:482
  134.4 0.8 copy-done.6
  135.2 0.8 copy-done.8
  136.0 0.7 copy-done.15
  136.6 0.9 shard_map.138
  (8 shorter events, 0.0 us)
Async XLA Ops:
  3.2 28.2 %all-to-all-start = ((bf16[16,48,128]{2,1,0:T(8,128)(2,1)}), bf16[16,48,128]{2,1,0:T(8,128)(2,1)S(1)}, u32[]{:S(2)}, u32[]{:S(2)}) async-start(bf16[16,48,128]{2,1,0:T(8,128)(2,1)} %shard_map.130), calls=%async_computation | async-start | bytes 393216 | tf_op jit(solution)/shard_map/all_to_all | solution.py:482
  25.0 0.6 copy-start.7
  25.6 0.6 copy-start.14
  26.1 56.4 %copy-start.12 = (f32[1,512]{1,0:T(1,128)}, f32[1,512]{1,0:T(1,128)S(1)}, u32[]{:S(2)}) copy-start(f32[1,512]{1,0:T(1,128)S(1)} %get-tuple-element.41.gain_ref) | copy-start | bytes 6148
  68.1 14.4 %collective-permute-start = (bf16[16,720,128]{2,1,0:T(8,128)(2,1)S(1)}, bf16[16,720,128]{2,1,0:T(8,128)(2,1)}, u32[]{:S(2)}, u32[]{:S(2)}) collective-permute-start(bf16[16,720,128]{2,1,0:T(8,128)(2,1)S(1)} %bitcast.15), channel_id=1, source_target_pairs={{0,16},{16,0},{32,48},{48,32},{64,80},{80,64},{96,112},{112,96},{1... | collective-permute-start | bytes 8847368 | tf_op jit(solution)/shard_map/ppermute | solution.py:578
  77.4 21.4 %all-to-all-start.3 = ((bf16[32,16,1024]{2,1,0:T(8,128)(2,1)}), bf16[32,16,1024]{2,1,0:T(8,128)(2,1)}, u32[]{:S(2)}, u32[]{:S(2)}) async-start(bf16[32,16,1024]{2,1,0:T(8,128)(2,1)} %bitcast.22), calls=%async_computation.3 | async-start | bytes 2097152 | tf_op jit(solution)/shard_map/all_to_all | solution.py:482
  82.5 7.1 %copy-start.3 = (bf16[256,1024]{1,0:T(8,128)(2,1)S(1)}, bf16[256,1024]{1,0:T(8,128)(2,1)}, u32[]{:S(2)}) copy-start(bf16[256,1024]{1,0:T(8,128)(2,1)} %get-tuple-element.43.low_ref) | copy-start | bytes 1572868
  89.0 0.6 copy-start.10
  89.6 33.2 %copy-start = (bf16[16,720,128]{2,1,0:T(8,128)(2,1)S(1)}, bf16[16,720,128]{2,1,0:T(8,128)(2,1)}, u32[]{:S(2)}) copy-start(bf16[16,720,128]{2,1,0:T(8,128)(2,1)} %get-tuple-element.55.w0_ref) | copy-start | bytes 8847364
  89.6 33.2 %copy-start.9 = (f32[1024]{0:T(1024)S(1)}, f32[1024]{0:T(1024)}, u32[]{:S(2)}) copy-start(f32[1024]{0:T(1024)} %param.18) | copy-start | bytes 12292
  93.8 29.0 %copy-start.1 = (bf16[256,1024]{1,0:T(8,128)(2,1)S(1)}, bf16[256,1024]{1,0:T(8,128)(2,1)}, u32[]{:S(2)}) copy-start(bf16[256,1024]{1,0:T(8,128)(2,1)} %get-tuple-element.51.o0_ref) | copy-start | bytes 1572868
  93.8 4.0 %collective-permute-start.1 = (bf16[528,512]{1,0:T(8,128)(2,1)S(1)}, bf16[528,512]{1,0:T(8,128)(2,1)S(1)}, u32[]{:S(2)}, u32[]{:S(2)}) collective-permute-start(bf16[528,512]{1,0:T(8,128)(2,1)S(1)} %get-tuple-element.48), channel_id=1, source_target_pairs={{0,16},{16,0},{32,48},{48,32},{64,80},{80,64},{96,112},{112,96},{1... | collective-permute-start | bytes 1622024 | tf_op jit(solution)/shard_map/ppermute | solution.py:621
  116.9 0.6 copy-start.5
  117.5 0.6 copy-start.4
  118.2 16.3 %all-to-all-start.5 = ((bf16[16,16,128]{2,1,0:T(8,128)(2,1)}), bf16[16,16,128]{2,1,0:T(8,128)(2,1)S(1)}, u32[]{:S(2)}, u32[]{:S(2)}) async-start(bf16[16,16,128]{2,1,0:T(8,128)(2,1)} %bitcast.18), calls=%async_computation.5 | async-start | bytes 131072 | tf_op jit(solution)/shard_map/all_to_all | solution.py:482
  122.9 1.0 copy-start.2
  123.9 0.7 copy-start.11
  124.6 0.7 copy-start.13
  134.4 0.8 copy-start.6
  135.2 0.8 copy-start.8
  136.0 0.7 copy-start.15

commit v8 on v7

--- a/solution.py
+++ b/solution.py
@@ -380,8 +380,11 @@
     send_ref,
     own_inner,
     terms,
+    grad,
+    sem,
 ):
     c = where[1]
+    out_copy = pltpu.make_async_copy(grad, grad_ref, sem)
 
     row = lax.broadcasted_iota(jnp.int32, (256, 256), 0)
     col = lax.broadcasted_iota(jnp.int32, (256, 256), 1)
@@ -411,7 +414,8 @@
     )
     grad_hat = dot(grads, rows) * factor
     inner = jnp.mean(grad_hat * hat, axis=1, keepdims=True)
-    grad_ref[...] = ((grad_hat - hat * inner) * out_scale).astype(BF16)
+    grad[...] = ((grad_hat - hat * inner) * out_scale).astype(BF16)
+    out_copy.start()
     sums = dot(low, grads, ((0,), (0,))) * factor
     terms[...] = sums.astype(BF16).reshape(PLANE, 2, 32, ROWS)
     for k in range(PLANE):
@@ -421,6 +425,7 @@
     own_inner[...] = products
     top = products.astype(BF16).astype(F32)
     send_ref[512:528, :] = split_rows(top, products - top).astype(BF16)
+    out_copy.wait()
 
 
 def split_rows(top, rest):
@@ -428,21 +433,34 @@
     return jnp.where(at == 0, top, jnp.where(at == 1, rest, 0.0))
 
 
-def pair_body(own_ref, inner_ref, got_ref, out_ref):
+def quarter(source, target, sems, n):
+    at = pl.ds(n * 4, 4)
+    return pltpu.make_async_copy(source.at[at], target.at[at], sems.at[n])
+
+
+def pair_body(own_ref, inner_ref, got_ref, out_ref, out, sems):
     other = got_ref[512:528, :].astype(F32)
     inner = inner_ref[...] + other[0:1, :] + other[1:2, :]
     top = inner.astype(BF16).astype(F32)
     tail = split_rows(top, inner - top).astype(BF16)
     for k in range(PLANE):
         mine = own_ref[k].astype(F32) + got_ref[k * 32 : (k + 1) * 32, :].astype(F32)
-        out_ref[k, 0:32, :] = mine.astype(BF16)
-        out_ref[k, 32:40, :] = tail[0:8, :]
-
-
-def plane_body(got_ref, ids_ref, pos_ref, neg_ref):
-    acc = got_ref[0].astype(F32)
-    for k in range(1, PLANE):
-        acc = acc + got_ref[k].astype(F32)
+        out[k, 0:32, :] = mine.astype(BF16)
+        out[k, 32:40, :] = tail[0:8, :]
+        if k % 4 == 3:
+            quarter(out, out_ref, sems, k // 4).start()
+    for n in range(4):
+        quarter(out, out_ref, sems, n).wait()
+
+
+def plane_body(got_ref, ids_ref, pos_ref, neg_ref, got, sems):
+    for n in range(4):
+        quarter(got_ref, got, sems, n).start()
+    acc = 0.0
+    for k in range(PLANE):
+        if k % 4 == 0:
+            quarter(got_ref, got, sems, k // 4).wait()
+        acc = acc + got[k].astype(F32)
     inner = acc[32:33, :] + acc[33:34, :]
     top = inner.astype(BF16).astype(F32)
     full = jnp.concatenate([acc[0:32, :], split_rows(top, inner - top)], axis=0)
@@ -609,17 +627,23 @@
     token_grad, own_terms, sent, own_inner = call(
         loss_body,
         (
-            shape((ROWS, WIDTH)),
+            pltpu.HBM((ROWS, WIDTH), BF16),
             shape((PLANE, 32, ROWS)),
             shape((528, ROWS)),
             shape((1, ROWS), F32),
         ),
         [SMEM] + [VMEM] * 5,
-        scratch=[pltpu.VMEM((PLANE, 2, 32, ROWS), BF16)],
+        scratch=[
+            pltpu.VMEM((PLANE, 2, 32, ROWS), BF16),
+            pltpu.VMEM((ROWS, WIDTH), BF16),
+            pltpu.SemaphoreType.DMA,
+        ],
         mib=16,
+        out_specs=(HBM, VMEM, VMEM, VMEM),
     )(where, home_out, table_low, cols, g_own, g_other)
     partner_terms = lax.ppermute(sent, "user", PARTNER)
-    pair = call(pair_body, pltpu.HBM((PLANE, 40, ROWS), BF16), [VMEM] * 3, out_specs=VMEM)(
+    blocks = [pltpu.VMEM((PLANE, 40, ROWS), BF16), pltpu.SemaphoreType.DMA((4,))]
+    pair = call(pair_body, pltpu.HBM((PLANE, 40, ROWS), BF16), [VMEM] * 3, out_specs=HBM, scratch=blocks)(
         own_terms, own_inner, partner_terms
     )
     pair, arrived = lax.optimization_barrier((pair, arrived))
@@ -643,8 +667,8 @@
     )(where, arrived, in_gain[None], o_own, o_other, gain, near, far, kept, in_hbm(held_other))
 
     positive_part, negative_part = call(
-        plane_body, (shape((48, 256), F32), shape((256, LANES))), [VMEM] * 2
-    )(plane, group_ids)
+        plane_body, (shape((48, 256), F32), shape((256, LANES))), [HBM, VMEM], scratch=blocks
+    )(in_hbm(plane), group_ids)
     owned = exchange(negative_part.reshape(ITEMS, 16, LANES), "item").reshape(256, LANES)
     item_grad = call(item_body, shape((32, 256), F32), [VMEM] * 4)(
         positive_part, owned, hat_part, table_scale

time: 139 us -> 140 us (level)
  no operation moved by 1% of the time
where the time goes in v8:
time: 140 us; the launch traced here: 139 us
  blocking collectives  54.2 us (39%)
  starting transfers between devices  36.6 us (26%)
  Pallas kernels  29.8 us (21%)
  waiting for transfers between devices  9.29 us (7%)
  local copies, waits for them, and re-layouts  8.02 us (6%)
    all_to_all x3, blocking collectives, exchange(): lax.all_to_all(blocks, axis, 0, 0, tiled=True, axis_index_groups=groups)  54.2 us
    all_to_all x3, starting transfers between devices, exchange(): lax.all_to_all(blocks, axis, 0, 0, tiled=True, axis_index_groups=groups)  24.9 us
    ppermute x1, starting transfers between devices, per_device(): held_other = lax.ppermute(held, 'user', PARTNER)  9.3 us
    unnamed x32, local copies, waits for them, and re-layouts  7.64 us
    pallas_call x1, Pallas kernels, per_device(): call(worker_body, shape((256, WIDTH)), [SMEM, VMEM, VMEM, HBM, HBM, VMEM,...  7.31 us
    all_to_all x3, waiting for transfers between devices, exchange(): lax.all_to_all(blocks, axis, 0, 0, tiled=True, axis_index_groups=groups)  7.11 us
    pallas_call x1, Pallas kernels, per_device(): call(layer_body, (shape((ROWS, WIDTH)), pltpu.HBM((256, WIDTH), BF16), pl...  6.51 us
    pallas_call x1, Pallas kernels, per_device(): call(prepare_body, (pltpu.HBM((ROWS, WIDTH), BF16), shape((ROWS, LANES),...  5.99 us
  transfers between devices with their start and end apart: 5, of which 4 were waited for; matrix products, arithmetic and copies ran while one was open for 0% of the time, Pallas kernels for 18%

profile of v8, /device:TPU:1, one launch (start us, length us, event | category | flops | bytes accessed | tf_op | source)
XLA Modules:
  0.0 138.8 jit_solution(4430250992850330831)
XLA Ops:
  0.6 0.1 pad_add_fusion.where
  0.7 2.5 %shard_map.130 = bf16[16,48,128]{2,1,0:T(8,128)(2,1)} custom-call(s32[4]{0:T(128)S(1)} %pad_add_fusion.where, s32[16,256]{1,0:T(8,128)} %refs_7_.1, bf16[64,2048]{1,0:T(8,128)(2,1)} %w_ref.1, bf16[64,512]{1,0:T(8,128)(2,1)} %bitcast.23, bf16[256,1024]{1,0:T(8,128)(2,1)} %refs_6_.1), custom_call_target="tpu_custom_call" | custom-call | tf_op jit(solution)/shard_map/pallas_call | solution.py:523
  3.2 15.7 %all-to-all-start = ((bf16[16,48,128]{2,1,0:T(8,128)(2,1)}), bf16[16,48,128]{2,1,0:T(8,128)(2,1)S(1)}, u32[]{:S(2)}, u32[]{:S(2)}) async-start(bf16[16,48,128]{2,1,0:T(8,128)(2,1)} %shard_map.130), calls=%async_computation | async-start | bytes 393216 | tf_op jit(solution)/shard_map/all_to_all | solution.py:500
  19.0 6.0 %shard_map.131 = (bf16[512,1024]{1,0:T(8,128)(2,1)}, f32[512,128]{1,0:T(8,128)S(1)}, bf16[16,128]{1,0:T(8,128)(2,1)S(1)}, bf16[512,1024]{1,0:T(8,128)(2,1)}, bf1...) custom-call(s32[4]{0:T(128)S(1)} %pad_add_fusion.where, ...), custom_call_target="tpu_custom_call" | custom-call | tf_op jit(solution)/shard_map/pallas_call | solution.py:539
  25.0 0.0 copy-start.7
  25.0 0.6 copy-done.7
  25.6 0.0 copy-start.14
  25.6 0.6 copy-done.14
  26.1 0.0 copy-start.12
  26.2 5.3 %all-to-all-done.got = bf16[16,48,128]{2,1,0:T(8,128)(2,1)S(1)} async-done(((bf16[16,48,128]{2,1,0:T(8,128)(2,1)}), bf16[16,48,128]{2,1,0:T(8,128)(2,1)S(1)}, u32[]{:S(2)}, u32[]{:S(2)}) %all-to-all-start) | async-done | bytes 196640 | tf_op jit(solution)/shard_map/all_to_all | solution.py:500
  31.5 0.2 shard_map.132
  31.6 12.1 %all_to_all.30 = bf16[4,720,128]{2,1,0:T(8,128)(2,1)S(1)} all-to-all(bf16[4,720,128]{2,1,0:T(8,128)(2,1)S(1)} %shard_map.132), channel_id=1, replica_groups={{0,128,256,384},{32,160,288,416},{64,192,320,448},{96,224,352,480},{16,..., dimensions={0} | all-to-all | bytes 1474560 | tf_op jit(solution)/shard_map/all_to_all | solution.py:500
  43.7 0.4 broadcast_in_dim.21
  44.1 24.0 %all_to_all.31 = bf16[4,2880,128]{2,1,0:T(8,128)(2,1)S(1)} all-to-all(bf16[4,2880,128]{2,1,0:T(8,128)(2,1)S(1)} %broadcast_in_dim.21), channel_id=1, replica_groups={{0,32,64,96},{128,160,192,224},{256,288,320,352},{384,416,448,480},{16,..., dimensions={0} | all-to-all | bytes 5898240 | tf_op jit(solution)/shard_map/all_to_all | solution.py:500
  68.1 9.3 %collective-permute-start = (bf16[16,720,128]{2,1,0:T(8,128)(2,1)S(1)}, bf16[16,720,128]{2,1,0:T(8,128)(2,1)}, u32[]{:S(2)}, u32[]{:S(2)}) collective-permute-start(bf16[16,720,128]{2,1,0:T(8,128)(2,1)S(1)} %bitcast.15), channel_id=1, source_target_pairs={{0,16},{16,0},{32,48},{48,32},{64,80},{80,64},{96,112},{112,96},{1... | collective-permute-start | bytes 8847368 | tf_op jit(solution)/shard_map/ppermute | solution.py:596
  77.4 4.5 %all-to-all-start.3 = ((bf16[32,16,1024]{2,1,0:T(8,128)(2,1)}), bf16[32,16,1024]{2,1,0:T(8,128)(2,1)}, u32[]{:S(2)}, u32[]{:S(2)}) async-start(bf16[32,16,1024]{2,1,0:T(8,128)(2,1)} %bitcast.22), calls=%async_computation.3 | async-start | bytes 2097152 | tf_op jit(solution)/shard_map/all_to_all | solution.py:500
  81.9 0.6 collective-permute-done.w1_ref
  82.5 0.0 copy-done.12
  82.5 0.0 copy-start.3
  82.5 6.5 %shard_map.133 = (bf16[512,1024]{1,0:T(8,128)(2,1)S(1)}, bf16[256,1024]{1,0:T(8,128)(2,1)}, bf16[256,1024]{1,0:T(8,128)(2,1)}, bf16[256,512]{1,0:T(8,128)(2,1)S(...) custom-call(bf16[512,1024]{1,0:T(8,128)(2,1)} %get-tuple-element.35., ...), custom_call_target="tpu_custom_call" | custom-call | tf_op jit(solution)/shard_map/pallas_call | solution.py:599
  89.0 0.0 copy-start.10
  89.0 0.6 copy-done.10
  89.6 0.0 copy-done.3
  89.6 4.2 %shard_map.134 = (bf16[512,1024]{1,0:T(8,128)(2,1)}, bf16[16,32,512]{2,1,0:T(8,128)(2,1)S(1)}, bf16[528,512]{1,0:T(8,128)(2,1)S(1)}, f32[1,512]{1,0:T(1,128)S(1)}) custom-call(s32[4]{0:T(128)S(1)} %pad_add_fusion.where, bf16[512,1024]{1,0:T(8,128)(2,1)S(1)} %get-tuple-element.42.out_ref, bf16[256,1024]{1,0:T(8,128)(2,1)S(1)} %copy-done.3, ...), custom_call_target="tpu_custom_call" | custom-call | tf_op jit(solution)/shard_map/pallas_call | solution.py:627
  93.8 0.0 copy-start.1
  93.9 2.4 %collective-permute-start.1 = (bf16[528,512]{1,0:T(8,128)(2,1)S(1)}, bf16[528,512]{1,0:T(8,128)(2,1)S(1)}, u32[]{:S(2)}, u32[]{:S(2)}) collective-permute-start(bf16[528,512]{1,0:T(8,128)(2,1)S(1)} %get-tuple-element.48), channel_id=1, source_target_pairs={{0,16},{16,0},{32,48},{48,32},{64,80},{80,64},{96,112},{112,96},{1... | collective-permute-start | bytes 1622024 | tf_op jit(solution)/shard_map/ppermute | solution.py:644
  96.3 1.5 %collective-permute-done.1.got_ref = bf16[528,512]{1,0:T(8,128)(2,1)S(1)} collective-permute-done((bf16[528,512]{1,0:T(8,128)(2,1)S(1)}, bf16[528,512]{1,0:T(8,128)(2,1)S(1)}, u32[]{:S(2)}, u32[]{:S(2)}) %collective-permute-start.1) | collective-permute-done | bytes 540704 | tf_op jit(solution)/shard_map/ppermute | solution.py:644
  97.8 1.0 shard_map.135
  98.8 0.0 all-to-all-done.3
  98.8 18.1 %all_to_all.32.got_ref = bf16[16,40,512]{2,1,0:T(8,128)(2,1)} all-to-all(bf16[16,40,512]{2,1,0:T(8,128)(2,1)} %shard_map.135), channel_id=1, replica_groups={{0,32,64,96,128,160,192,224,256,288,320,352,384,416,448,480},{16,48,80,..., dimensions={0} | all-to-all | bytes 1310720 | tf_op jit(solution)/shard_map/all_to_all | solution.py:500
  116.9 1.3 shard_map.137
  118.2 0.0 copy-start.5
  118.2 0.6 copy-done.5
  118.8 0.6 copy-done.4
  119.4 4.7 %all-to-all-start.5 = ((bf16[16,16,128]{2,1,0:T(8,128)(2,1)}), bf16[16,16,128]{2,1,0:T(8,128)(2,1)S(1)}, u32[]{:S(2)}, u32[]{:S(2)}) async-start(bf16[16,16,128]{2,1,0:T(8,128)(2,1)} %bitcast.18), calls=%async_computation.5 | async-start | bytes 131072 | tf_op jit(solution)/shard_map/all_to_all | solution.py:500
  124.1 0.0 copy-done
  124.1 0.0 copy-done.9
  124.2 0.0 copy-done.1
  124.2 0.0 copy-start.2
  124.2 1.0 copy-done.2
  125.2 0.7 copy-done.11
  125.9 0.7 copy-done.13
  126.6 7.3 %shard_map.136 = bf16[256,1024]{1,0:T(8,128)(2,1)} custom-call(s32[4]{0:T(128)S(1)} %pad_add_fusion.where, bf16[512,1024]{1,0:T(8,128)(2,1)} %bitcast.11.got_ref, f32[1,1024]{1,0:T(1,128)S(1)} %bitcast.20, bf16[256,1024]{1,0:T(8,128)(2,1)S(1)} %copy-done.1, bf16[256,1024]{1,0:T(8,128)(2,1)S(1)} %copy-done.2, f32[1,512]{1,0:T(1,128)S(1)} %copy-done.13, ...), custom_call_target="tpu_custom_call" | custom-call | tf_op jit(solution)/shard_map/pallas_call | solution.py:652
  133.9 1.8 %all-to-all-done.5 = bf16[16,16,128]{2,1,0:T(8,128)(2,1)S(1)} async-done(((bf16[16,16,128]{2,1,0:T(8,128)(2,1)}), bf16[16,16,128]{2,1,0:T(8,128)(2,1)S(1)}, u32[]{:S(2)}, u32[]{:S(2)}) %all-to-all-start.5) | async-done | bytes 65568 | tf_op jit(solution)/shard_map/all_to_all | solution.py:500
  135.7 0.8 copy-done.6
  136.5 0.8 copy-done.8
  137.3 0.7 copy-done.15
  137.9 0.9 shard_map.138
  (8 shorter events, 0.0 us)
Async XLA Ops:
  3.2 28.2 %all-to-all-start = ((bf16[16,48,128]{2,1,0:T(8,128)(2,1)}), bf16[16,48,128]{2,1,0:T(8,128)(2,1)S(1)}, u32[]{:S(2)}, u32[]{:S(2)}) async-start(bf16[16,48,128]{2,1,0:T(8,128)(2,1)} %shard_map.130), calls=%async_computation | async-start | bytes 393216 | tf_op jit(solution)/shard_map/all_to_all | solution.py:500
  25.0 0.6 copy-start.7
  25.6 0.6 copy-start.14
  26.1 56.4 %copy-start.12 = (f32[1,512]{1,0:T(1,128)}, f32[1,512]{1,0:T(1,128)S(1)}, u32[]{:S(2)}) copy-start(f32[1,512]{1,0:T(1,128)S(1)} %get-tuple-element.41.gain_ref) | copy-start | bytes 6148
  68.1 14.4 %collective-permute-start = (bf16[16,720,128]{2,1,0:T(8,128)(2,1)S(1)}, bf16[16,720,128]{2,1,0:T(8,128)(2,1)}, u32[]{:S(2)}, u32[]{:S(2)}) collective-permute-start(bf16[16,720,128]{2,1,0:T(8,128)(2,1)S(1)} %bitcast.15), channel_id=1, source_target_pairs={{0,16},{16,0},{32,48},{48,32},{64,80},{80,64},{96,112},{112,96},{1... | collective-permute-start | bytes 8847368 | tf_op jit(solution)/shard_map/ppermute | solution.py:596
  77.4 21.4 %all-to-all-start.3 = ((bf16[32,16,1024]{2,1,0:T(8,128)(2,1)}), bf16[32,16,1024]{2,1,0:T(8,128)(2,1)}, u32[]{:S(2)}, u32[]{:S(2)}) async-start(bf16[32,16,1024]{2,1,0:T(8,128)(2,1)} %bitcast.22), calls=%async_computation.3 | async-start | bytes 2097152 | tf_op jit(solution)/shard_map/all_to_all | solution.py:500
  82.5 7.1 %copy-start.3 = (bf16[256,1024]{1,0:T(8,128)(2,1)S(1)}, bf16[256,1024]{1,0:T(8,128)(2,1)}, u32[]{:S(2)}) copy-start(bf16[256,1024]{1,0:T(8,128)(2,1)} %get-tuple-element.43.low_ref) | copy-start | bytes 1572868
  89.0 0.6 copy-start.10
  89.6 34.5 %copy-start = (bf16[16,720,128]{2,1,0:T(8,128)(2,1)S(1)}, bf16[16,720,128]{2,1,0:T(8,128)(2,1)}, u32[]{:S(2)}) copy-start(bf16[16,720,128]{2,1,0:T(8,128)(2,1)} %get-tuple-element.55.w0_ref) | copy-start | bytes 8847364
  89.6 34.5 %copy-start.9 = (f32[1024]{0:T(1024)S(1)}, f32[1024]{0:T(1024)}, u32[]{:S(2)}) copy-start(f32[1024]{0:T(1024)} %param.18) | copy-start | bytes 12292
  93.8 30.3 %copy-start.1 = (bf16[256,1024]{1,0:T(8,128)(2,1)S(1)}, bf16[256,1024]{1,0:T(8,128)(2,1)}, u32[]{:S(2)}) copy-start(bf16[256,1024]{1,0:T(8,128)(2,1)} %get-tuple-element.51.o0_ref) | copy-start | bytes 1572868
  93.9 4.0 %collective-permute-start.1 = (bf16[528,512]{1,0:T(8,128)(2,1)S(1)}, bf16[528,512]{1,0:T(8,128)(2,1)S(1)}, u32[]{:S(2)}, u32[]{:S(2)}) collective-permute-start(bf16[528,512]{1,0:T(8,128)(2,1)S(1)} %get-tuple-element.48), channel_id=1, source_target_pairs={{0,16},{16,0},{32,48},{48,32},{64,80},{80,64},{96,112},{112,96},{1... | collective-permute-start | bytes 1622024 | tf_op jit(solution)/shard_map/ppermute | solution.py:644
  118.2 0.6 copy-start.5
  118.8 0.6 copy-start.4
  119.4 16.3 %all-to-all-start.5 = ((bf16[16,16,128]{2,1,0:T(8,128)(2,1)}), bf16[16,16,128]{2,1,0:T(8,128)(2,1)S(1)}, u32[]{:S(2)}, u32[]{:S(2)}) async-start(bf16[16,16,128]{2,1,0:T(8,128)(2,1)} %bitcast.18), calls=%async_computation.5 | async-start | bytes 131072 | tf_op jit(solution)/shard_map/all_to_all | solution.py:500
  124.2 1.0 copy-start.2
  125.2 0.7 copy-start.11
  125.9 0.7 copy-start.13
  135.7 0.8 copy-start.6
  136.5 0.8 copy-start.8
  137.3 0.7 copy-start.15
